TPU v7x, 32 devices: a whole 2x2x4 slice. The times are simulated.
32 devices in a mesh: batch: 4 (over y, x), segment: 8 (over z, core).
Axes of the slice: x: 2, y: 2, z: 4, core: 2. Of those that a mesh axis runs over, the one named last changes fastest.
Arguments:
- tokens: bfloat16 [16, 1024, 1024], P('batch', 'segment'), may hold values from -6 to 6
- doc_ids: int32 [16, 1024], P('batch'), may hold values from 0 to 3, as said below
- knn_index: int32 [16, 1024, 8, 32], P('batch', 'segment'), may hold values from 0 to 255, as said below
- mem_keys: bfloat16 [256, 1024], P('segment'), may hold values from -6 to 6
- mem_values: bfloat16 [256, 1024], P('segment'), may hold values from -6 to 6
- qkv_weight: bfloat16 [8, 256, 3072], P('segment', None, 'batch'), may hold values from -0.1875 to 0.1875
- out_weight: bfloat16 [8, 256, 1024], P('segment', None, 'batch'), may hold values from -0.75 to 0.75
- in_weight: bfloat16 [8, 256, 4096], P('segment', None, 'batch'), may hold values from -0.1875 to 0.1875
- down_weight: bfloat16 [8, 1024, 1024], P('segment', None, 'batch'), may hold values from -0.09375 to 0.09375
- norm_gain: bfloat16 [8, 2, 256], P('segment', None, 'batch'), may hold values from 0.5 to 1.5
- norm_bias: bfloat16 [8, 2, 256], P('segment', None, 'batch'), may hold values from -2 to 2
- rel_table: float32 [2, 32, 8], replicated, may hold values from -4 to 4
- mem_gate: float32 [8], replicated, may hold values from -2 to 2
- cotangent: bfloat16 [16, 1024, 1024], P('batch', 'segment'), may hold values from -6 to 6
Outputs:
- mixed: bfloat16 [16, 1024, 1024], P('batch', 'segment')
- input_grad: bfloat16 [16, 1024, 1024], P('batch', 'segment')
- qkv_grad: float32 [8, 256, 3072], P('segment', None, 'batch')
- out_grad: float32 [8, 256, 1024], P('segment', None, 'batch')
- in_grad: float32 [8, 256, 4096], P('segment', None, 'batch')
- down_grad: float32 [8, 1024, 1024], P('segment', None, 'batch')
- gain_grad: float32 [8, 2, 256], P('segment', None, 'batch')
- bias_grad: float32 [8, 2, 256], P('segment', None, 'batch')
- table_grad: float32 [2, 32, 8], replicated
- gate_grad: float32 [8], replicated
Inputs may be any that keep to these rules, and one draw needn't show every extreme that they name: `doc_ids`: along a sequence the document numbers never fall; among the 4 sequences of each index of batch one, drawn from the seed, is a single document. `knn_index`: the 32 slots of one token and head are distinct.
All inputs are finite; a program needn't handle non-finite values.
Results may differ from a plain program's by a relative error of at most 0.019.
Values may be sent and summed in bfloat16 or wider, within the bound.
No kernel may reach another device: no remote copies, remote signals or barrier semaphores. Data moves between devices by JAX's collectives and lax.ppermute only.
A program may use at most 512 MiB of HBM per device.

v0:
```python
import math

import jax
import jax.numpy as jnp
import numpy as np
from jax import lax
from jax.sharding import PartitionSpec as P

WIN = 512
LAYERS = 2
MICRO = 4
MEM_DEV = 32


norm_eps = 1e-05
big_negative = -1e30
bucket_edges = np.ceil(16.0 * 8.0 ** (np.arange(1, 16) / 16.0)).astype(np.int32)
highest = lax.Precision.HIGHEST


def from_partner(shard, axis, bit):
    return lax.ppermute(shard, axis, [(i, i ^ 1 << bit) for i in range(lax.axis_size(axis))])


def shortened(shard):

    def short(part):
        return part.astype(jnp.bfloat16) if part.dtype == jnp.float32 else part

    return jax.tree.map(short, shard)


def shifted(block, axis, distance):
    devices = range(lax.axis_size(axis))
    route = [(i - distance, i) for i in devices if i - distance in devices]
    return lax.ppermute(block, axis, route)


def bucket_of(distance):
    edges = jnp.asarray(bucket_edges)
    beyond = jnp.sum((distance[..., None] >= edges).astype(jnp.int32), axis=-1)
    return jnp.where(distance < 16, distance, 16 + beyond)


def smooth_act(values):
    return jax.nn.gelu(values, approximate=True)


def normalize(values):
    center = values - jnp.mean(values, axis=-1, keepdims=True)
    factor = lax.rsqrt(jnp.mean(center * center, axis=-1, keepdims=True) + norm_eps)
    return (center * factor, factor)


def norm_back(upstream, normal, factor, gain_row):
    gain_part = jnp.sum(upstream * normal, axis=0)
    shift_part = jnp.sum(upstream, axis=0)
    scaled = upstream * gain_row
    inner_part = (
        scaled
        - jnp.mean(scaled, axis=-1, keepdims=True)
        - normal * jnp.mean(scaled * normal, axis=-1, keepdims=True)
    )
    return (factor * inner_part, gain_part, shift_part)


def local_probs(queries, keys_span, position_bias, allowed, score_scale):
    scores = (
        jnp.einsum("sqhd,skhd->shqk", queries, keys_span, preferred_element_type=jnp.float32)
        * score_scale
    )
    scores = jnp.where(allowed[:, None], scores + position_bias[None], big_negative)
    raised = jnp.exp(scores - jnp.max(scores, axis=-1, keepdims=True))
    return raised / jnp.sum(raised, axis=-1, keepdims=True)


def pick_scores(queries, slot_rows, memory):
    head_count, head_dim = (queries.shape[1], queries.shape[2])
    turn_count = memory.shape[0] // MEM_DEV

    def pick_step(turn_no, running):
        section = lax.dynamic_slice_in_dim(memory, turn_no * MEM_DEV, MEM_DEV, 0).reshape(
            MEM_DEV, head_count, head_dim
        )
        scores = jnp.einsum("rhd,chd->rhc", queries, section, preferred_element_type=jnp.float32)
        slot_ids = turn_no * MEM_DEV + jnp.arange(MEM_DEV, dtype=jnp.int32)
        matched = slot_rows[..., None] == slot_ids
        return running + jnp.sum(jnp.where(matched, scores[:, :, None, :], 0.0), axis=-1)

    return lax.fori_loop(0, turn_count, pick_step, jnp.zeros(slot_rows.shape, jnp.float32))


def place_rows(chosen, slot_rows, memory):
    row_total, head_count = (chosen.shape[0], chosen.shape[1])
    head_dim = memory.shape[1] // head_count
    turn_count = memory.shape[0] // MEM_DEV

    def place_step(turn_no, running):
        section = lax.dynamic_slice_in_dim(memory, turn_no * MEM_DEV, MEM_DEV, 0).reshape(
            MEM_DEV, head_count, head_dim
        )
        slot_ids = turn_no * MEM_DEV + jnp.arange(MEM_DEV, dtype=jnp.int32)
        matched = slot_rows[..., None] == slot_ids
        spread = jnp.sum(jnp.where(matched, chosen[..., None], jnp.zeros((), jnp.bfloat16)), axis=2)
        return running + jnp.einsum(
            "rhc,chd->rhd", spread, section, preferred_element_type=jnp.float32
        )

    return lax.fori_loop(
        0, turn_count, place_step, jnp.zeros((row_total, head_count, head_dim), jnp.float32)
    )


def gather_rows(parts, segment_index):
    bit_count = lax.axis_size("segment").bit_length() - 1
    along = (0, 0, 0, 0, 1, 1)
    qkv_part, out_part, in_part, down_part, gain_part, bias_part = parts
    for bit_no in range(1, bit_count):
        others = from_partner(
            (qkv_part, out_part, in_part, down_part, gain_part, bias_part), "segment", bit_no
        )
        upper_flag = segment_index // (1 << bit_no) % 2 == 1
        joined = []
        for own_part, other_part, axis_no in zip(
            (qkv_part, out_part, in_part, down_part, gain_part, bias_part), others, along
        ):
            leading = jnp.where(upper_flag, other_part, own_part)
            trailing = jnp.where(upper_flag, own_part, other_part)
            joined.append(jnp.concatenate([leading, trailing], axis=axis_no))
        qkv_part, out_part, in_part, down_part, gain_part, bias_part = joined
    return (qkv_part, out_part, in_part, down_part, gain_part, bias_part)


def gather_cols(parts):
    qkv_part, out_part, in_part, down_part, gain_part, bias_part = parts
    return (
        lax.all_gather(qkv_part, "batch", axis=1, tiled=True),
        lax.all_gather(out_part, "batch", axis=1, tiled=True),
        lax.all_gather(in_part, "batch", axis=1, tiled=True),
        lax.all_gather(down_part, "batch", axis=1, tiled=True),
        lax.all_gather(gain_part, "batch", axis=2, tiled=True),
        lax.all_gather(bias_part, "batch", axis=2, tiled=True),
    )


def scatter_rows(parts, segment_index):
    bit_count = lax.axis_size("segment").bit_length() - 1
    along = (0, 0, 0, 0, 1, 1)
    current = list(parts)
    for bit_no in range(bit_count - 1, 0, -1):
        upper_flag = segment_index // (1 << bit_no) % 2 == 1
        sends, keeps = ([], [])
        for member, axis_no in zip(current, along):
            half_size = member.shape[axis_no] // 2
            lower_half = lax.slice_in_dim(member, 0, half_size, axis=axis_no)
            upper_half = lax.slice_in_dim(member, half_size, 2 * half_size, axis=axis_no)
            sends.append(jnp.where(upper_flag, lower_half, upper_half))
            keeps.append(jnp.where(upper_flag, upper_half, lower_half))
        others = from_partner(
            (
                shortened(sends[0]),
                shortened(sends[1]),
                shortened(sends[2]),
                shortened(sends[3]),
                shortened(sends[4]),
                shortened(sends[5]),
            ),
            "segment",
            bit_no,
        )
        current = [kept + other_part for kept, other_part in zip(keeps, others)]
    return tuple(current)


def scatter_cols(parts):
    qkv_part, out_part, in_part, down_part, gain_part, bias_part = parts
    return (
        lax.psum_scatter(
            qkv_part.astype(jnp.bfloat16), "batch", scatter_dimension=1, tiled=True
        ).astype(jnp.float32),
        lax.psum_scatter(
            out_part.astype(jnp.bfloat16), "batch", scatter_dimension=1, tiled=True
        ).astype(jnp.float32),
        lax.psum_scatter(
            in_part.astype(jnp.bfloat16), "batch", scatter_dimension=1, tiled=True
        ).astype(jnp.float32),
        lax.psum_scatter(
            down_part.astype(jnp.bfloat16), "batch", scatter_dimension=1, tiled=True
        ).astype(jnp.float32),
        lax.psum_scatter(
            gain_part.astype(jnp.bfloat16), "batch", scatter_dimension=2, tiled=True
        ).astype(jnp.float32),
        lax.psum_scatter(
            bias_part.astype(jnp.bfloat16), "batch", scatter_dimension=2, tiled=True
        ).astype(jnp.float32),
    )


def edge_up(values):
    return shifted(values, "segment", 1)


def edge_down(values):
    return shifted(values, "segment", -1)


def pass_up(values):
    return shifted(values.astype(jnp.bfloat16), "segment", 1).astype(values.dtype)


def pass_down(values):
    return shifted(values.astype(jnp.bfloat16), "segment", -1).astype(values.dtype)


def on_device(
    tokens,
    doc_ids,
    knn_index,
    mem_keys,
    mem_values,
    qkv_weight,
    out_weight,
    in_weight,
    down_weight,
    norm_gain,
    norm_bias,
    rel_table,
    mem_gate,
    cotangent,
):
    seq_count, block_len, model_width = tokens.shape
    micro_seqs = seq_count // MICRO
    stretch_len = LAYERS * block_len
    row_count = micro_seqs * stretch_len
    head_count = rel_table.shape[2]
    head_dim = model_width // head_count
    bucket_count = rel_table.shape[1]
    topk_count = knn_index.shape[3]
    gain_cols = norm_gain.shape[2]
    reach_blocks = WIN // stretch_len
    span_len = (reach_blocks + 1) * stretch_len
    score_scale = 1.0 / math.sqrt(head_dim)
    segment_index = lax.axis_index("segment")
    layer_index = segment_index % LAYERS
    stretch_index = segment_index // LAYERS
    is_upper = layer_index == 1
    stretch_total = lax.axis_size("segment") // LAYERS
    batch_total = lax.axis_size("batch")
    upper_tokens = edge_down(tokens)
    stretch_tokens = jnp.concatenate([tokens, upper_tokens], axis=1).astype(jnp.float32)
    lower_cotangent = edge_up(cotangent)
    stretch_cotangent = jnp.concatenate([lower_cotangent, cotangent], axis=1).astype(jnp.float32)
    lower_slots = shifted(knn_index, "segment", 1)
    stretch_slots = jnp.concatenate([lower_slots, knn_index], axis=1)
    doc_padded = jnp.concatenate(
        [jnp.full((seq_count, reach_blocks * stretch_len), -1, jnp.int32), doc_ids], axis=1
    )
    doc_keys = lax.dynamic_slice_in_dim(doc_padded, stretch_index * stretch_len, span_len, 1)
    doc_query = lax.dynamic_slice_in_dim(
        doc_padded, (stretch_index + reach_blocks) * stretch_len, stretch_len, 1
    )
    distance = (
        jnp.arange(stretch_len, dtype=jnp.int32)[:, None]
        + reach_blocks * stretch_len
        - jnp.arange(span_len, dtype=jnp.int32)[None, :]
    )
    allowed_all = ((distance >= 0) & (distance < WIN))[None] & (
        doc_query[:, :, None] == doc_keys[:, None, :]
    )
    bucket_ids = bucket_of(jnp.clip(distance, 0, WIN - 1))
    table_onehot = (bucket_ids[..., None] == jnp.arange(bucket_count, dtype=jnp.int32)).astype(
        jnp.float32
    )
    table_now = lax.dynamic_index_in_dim(rel_table, layer_index, 0, keepdims=False)
    position_bias = jnp.einsum("qkb,bh->hqk", table_onehot, table_now, precision=highest)
    gate_sig = jax.nn.sigmoid(mem_gate)
    gate_live = jnp.where(is_upper, gate_sig, 0.0)
    gate_wide = jnp.repeat(gate_live, head_dim)
    shards = (
        qkv_weight[0],
        out_weight[0],
        in_weight[0],
        down_weight[0],
        norm_gain[0].reshape(2, 1, 1, gain_cols),
        norm_bias[0].reshape(2, 1, 1, gain_cols),
    )
    gathered = gather_cols(gather_rows(shards, segment_index))
    qkv_full, out_full, in_full, down_full = (gathered[0], gathered[1], gathered[2], gathered[3])
    gains = gathered[4].reshape(2, model_width).astype(jnp.float32)
    shifts = gathered[5].reshape(2, model_width).astype(jnp.float32)
    whole_keys, whole_values = (
        lax.all_gather(mem_keys, "segment", axis=0, tiled=True),
        lax.all_gather(mem_values, "segment", axis=0, tiled=True),
    )

    def with_memory(flat_query, slot_rows):
        picked = pick_scores(flat_query, slot_rows, whole_keys) * score_scale
        raised = jnp.exp(picked - jnp.max(picked, axis=-1, keepdims=True))
        prob_rows = raised / jnp.sum(raised, axis=-1, keepdims=True)
        mixed_rows = place_rows(prob_rows.astype(jnp.bfloat16), slot_rows, whole_values)
        return (mixed_rows.reshape(row_count, model_width), prob_rows)

    def without_memory(flat_query, slot_rows):
        return (
            jnp.zeros((row_count, model_width), jnp.float32),
            jnp.zeros((row_count, head_count, topk_count), jnp.float32),
        )

    def memory_back(flat_grad, prob_rows, slot_rows):
        chosen_grad = pick_scores(flat_grad, slot_rows, whole_values)
        chosen_score = (
            prob_rows * (chosen_grad - jnp.sum(prob_rows * chosen_grad, axis=-1, keepdims=True))
        ).astype(jnp.bfloat16)
        return place_rows(chosen_score, slot_rows, whole_keys).reshape(row_count, model_width)

    def memory_skip(flat_grad, prob_rows, slot_rows):
        return jnp.zeros((row_count, model_width), jnp.float32)

    received = jnp.zeros((row_count, model_width), jnp.float32)
    stored_list = []
    top_outputs = []
    for tick_no in range(MICRO + 1):
        micro_no = jnp.clip(tick_no - layer_index, 0, MICRO - 1)
        first_seq = micro_no * micro_seqs
        own_tokens = lax.dynamic_slice_in_dim(stretch_tokens, first_seq, micro_seqs, 0).reshape(
            row_count, model_width
        )
        hidden = jnp.where(is_upper, received, own_tokens)
        allowed = lax.dynamic_slice_in_dim(allowed_all, first_seq, micro_seqs, 0)
        slot_rows = lax.dynamic_slice_in_dim(stretch_slots, first_seq, micro_seqs, 0).reshape(
            row_count, head_count, topk_count
        )
        forward_normal_one, forward_factor_one = normalize(hidden)
        forward_normed = (forward_normal_one * gains[0] + shifts[0]).astype(jnp.bfloat16)
        projected = jnp.dot(forward_normed, qkv_full, preferred_element_type=jnp.float32).astype(
            jnp.bfloat16
        )
        forward_queries = projected[:, :model_width].reshape(
            micro_seqs, stretch_len, head_count, head_dim
        )
        own_keys = projected[:, model_width : 2 * model_width].reshape(
            micro_seqs, stretch_len, model_width
        )
        own_values = projected[:, 2 * model_width :].reshape(micro_seqs, stretch_len, model_width)
        key_parts = []
        value_parts = []
        for forward_distance_back in range(reach_blocks, 0, -1):
            forward_got_keys, forward_got_values = shifted(
                (own_keys, own_values), "segment", LAYERS * forward_distance_back
            )
            key_parts.append(forward_got_keys)
            value_parts.append(forward_got_values)
        forward_keys_span = jnp.concatenate(key_parts + [own_keys], axis=1).reshape(
            micro_seqs, span_len, head_count, head_dim
        )
        forward_values_span = jnp.concatenate(value_parts + [own_values], axis=1).reshape(
            micro_seqs, span_len, head_count, head_dim
        )
        forward_probs_local = local_probs(
            forward_queries, forward_keys_span, position_bias, allowed, score_scale
        )
        forward_local_out = jnp.einsum(
            "shqk,skhd->sqhd",
            forward_probs_local.astype(jnp.bfloat16),
            forward_values_span,
            preferred_element_type=jnp.float32,
        ).reshape(row_count, model_width)
        forward_flat_query = forward_queries.reshape(row_count, head_count, head_dim)
        forward_memory_out, forward_memory_probs = lax.cond(
            is_upper, with_memory, without_memory, forward_flat_query, slot_rows
        )
        combined = gate_wide * forward_memory_out + (1.0 - gate_wide) * forward_local_out
        forward_attended = combined.astype(jnp.bfloat16)
        after = hidden + jnp.dot(forward_attended, out_full, preferred_element_type=jnp.float32)
        forward_normal_two, forward_factor_two = normalize(after)
        forward_normed_two = (forward_normal_two * gains[1] + shifts[1]).astype(jnp.bfloat16)
        forward_pre_act = jnp.dot(forward_normed_two, in_full, preferred_element_type=jnp.float32)
        forward_activity = smooth_act(forward_pre_act).astype(jnp.bfloat16)
        result = after + jnp.dot(forward_activity, down_full, preferred_element_type=jnp.float32)
        forward_stored = (
            forward_normal_one,
            forward_factor_one,
            forward_normed,
            forward_queries,
            forward_keys_span,
            forward_values_span,
            forward_local_out,
            forward_memory_out,
            forward_memory_probs,
            forward_attended,
            forward_normal_two,
            forward_factor_two,
            forward_normed_two,
            forward_pre_act,
        )
        result, stored = (result, forward_stored)
        stored_list.append((stored, allowed, slot_rows))
        if tick_no >= 1:
            top_outputs.append(result)
        if tick_no < MICRO:
            received = pass_up(result)
    coming = jnp.zeros((row_count, model_width), jnp.float32)
    totals = None
    table_total = jnp.zeros((bucket_count, head_count), jnp.float32)
    gate_total = jnp.zeros((head_count,), jnp.float32)
    bottom_grads = []
    for turn_no in range(MICRO + 1):
        slot_no = MICRO - turn_no
        stored, allowed, slot_rows = stored_list[slot_no]
        if slot_no >= 1:
            top_grad = stretch_cotangent[(slot_no - 1) * micro_seqs : slot_no * micro_seqs].reshape(
                row_count, model_width
            )
        else:
            top_grad = jnp.zeros((row_count, model_width), jnp.float32)
        upstream = jnp.where(is_upper, top_grad, coming)
        (
            normal_one,
            factor_one,
            normed,
            queries,
            keys_span,
            values_span,
            local_out,
            memory_out,
            memory_probs,
            attended,
            normal_two,
            factor_two,
            normed_two,
            pre_act,
        ) = stored
        activity, act_pull = jax.vjp(smooth_act, pre_act)
        activity = activity.astype(jnp.bfloat16)
        upstream_low = upstream.astype(jnp.bfloat16)
        down_part = jnp.einsum(
            "rf,rd->fd", activity, upstream_low, preferred_element_type=jnp.float32
        )
        activity_grad = jnp.einsum(
            "rd,fd->rf", upstream_low, down_full, preferred_element_type=jnp.float32
        )
        before_grad = act_pull(activity_grad)[0].astype(jnp.bfloat16)
        in_part = jnp.einsum(
            "rd,rf->df", normed_two, before_grad, preferred_element_type=jnp.float32
        )
        normed_two_grad = jnp.einsum(
            "rf,df->rd", before_grad, in_full, preferred_element_type=jnp.float32
        )
        after_term, gain_two, shift_two = norm_back(
            normed_two_grad, normal_two, factor_two, gains[1]
        )
        after_grad = upstream + after_term
        after_low = after_grad.astype(jnp.bfloat16)
        out_part = jnp.einsum("re,rd->ed", attended, after_low, preferred_element_type=jnp.float32)
        attended_grad = jnp.einsum(
            "rd,ed->re", after_low, out_full, preferred_element_type=jnp.float32
        ).astype(jnp.bfloat16)
        attended_wide = attended_grad.astype(jnp.float32)
        memory_grad = (gate_wide * attended_wide).astype(jnp.bfloat16)
        local_grad = ((1.0 - gate_wide) * attended_wide).astype(jnp.bfloat16)
        gate_sums = jnp.sum(
            (attended_wide * (memory_out - local_out)).reshape(row_count, head_count, head_dim),
            axis=(0, 2),
        )
        gate_part = gate_sums * gate_live * (1.0 - gate_live)
        probs_local = local_probs(queries, keys_span, position_bias, allowed, score_scale)
        probs_low = probs_local.astype(jnp.bfloat16)
        local_four = local_grad.reshape(micro_seqs, stretch_len, head_count, head_dim)
        prob_grad = jnp.einsum(
            "sqhd,skhd->shqk", local_four, values_span, preferred_element_type=jnp.float32
        )
        score_grad = (
            probs_local * (prob_grad - jnp.sum(probs_local * prob_grad, axis=-1, keepdims=True))
        ).astype(jnp.bfloat16)
        query_grad = (
            jnp.einsum("shqk,skhd->sqhd", score_grad, keys_span, preferred_element_type=jnp.float32)
            * score_scale
        ).reshape(row_count, model_width)
        key_grad = (
            jnp.einsum("shqk,sqhd->skhd", score_grad, queries, preferred_element_type=jnp.float32)
            * score_scale
        ).reshape(micro_seqs, span_len, model_width)
        value_grad = jnp.einsum(
            "shqk,sqhd->skhd", probs_low, local_four, preferred_element_type=jnp.float32
        ).reshape(micro_seqs, span_len, model_width)
        table_part = jnp.einsum(
            "qkb,hqk->bh",
            table_onehot,
            jnp.sum(score_grad, axis=0, dtype=jnp.float32),
            precision=highest,
        )
        own_key_grad = key_grad[:, reach_blocks * stretch_len :]
        own_value_grad = value_grad[:, reach_blocks * stretch_len :]
        for distance_back in range(1, reach_blocks + 1):
            first_row = (reach_blocks - distance_back) * stretch_len
            got_keys, got_values = (
                shifted(
                    key_grad[:, first_row : first_row + stretch_len].astype(jnp.bfloat16),
                    "segment",
                    -LAYERS * distance_back,
                ).astype(jnp.float32),
                shifted(
                    value_grad[:, first_row : first_row + stretch_len].astype(jnp.bfloat16),
                    "segment",
                    -LAYERS * distance_back,
                ).astype(jnp.float32),
            )
            own_key_grad = own_key_grad + got_keys
            own_value_grad = own_value_grad + got_values
        backward_flat_grad = memory_grad.reshape(row_count, head_count, head_dim)
        memory_query = lax.cond(
            is_upper, memory_back, memory_skip, backward_flat_grad, memory_probs, slot_rows
        )
        query_grad = query_grad + memory_query * score_scale
        projected_grad = jnp.concatenate(
            [
                query_grad.astype(jnp.bfloat16),
                own_key_grad.reshape(row_count, model_width).astype(jnp.bfloat16),
                own_value_grad.reshape(row_count, model_width).astype(jnp.bfloat16),
            ],
            axis=1,
        )
        qkv_part = jnp.einsum(
            "rd,re->de", normed, projected_grad, preferred_element_type=jnp.float32
        )
        normed_grad = jnp.einsum(
            "re,de->rd", projected_grad, qkv_full, preferred_element_type=jnp.float32
        )
        input_term, gain_one, shift_one = norm_back(normed_grad, normal_one, factor_one, gains[0])
        input_part = after_grad + input_term
        grads = (
            qkv_part,
            out_part,
            in_part,
            down_part,
            jnp.stack([gain_one, gain_two]),
            jnp.stack([shift_one, shift_two]),
        )
        input_part, grads, table_part, gate_part = (input_part, grads, table_part, gate_part)
        totals = grads if totals is None else jax.tree.map(jnp.add, totals, grads)
        table_total = table_total + table_part
        gate_total = gate_total + gate_part
        if turn_no >= 1:
            bottom_grads.append(input_part)
        if turn_no < MICRO:
            coming = pass_down(input_part)
    top_stack = jnp.stack(top_outputs).astype(jnp.bfloat16)
    moved_down = edge_down(top_stack[:, :block_len])
    mixed_out = jnp.where(is_upper, top_stack[:, block_len:], moved_down)
    bottom_stack = jnp.stack(bottom_grads[::-1]).astype(jnp.bfloat16)
    moved_up = edge_up(bottom_stack[:, block_len:])
    input_out = jnp.where(is_upper, moved_up, bottom_stack[:, :block_len])
    shaped = (
        totals[0],
        totals[1],
        totals[2],
        totals[3],
        totals[4].reshape(2, stretch_total, batch_total, gain_cols),
        totals[5].reshape(2, stretch_total, batch_total, gain_cols),
    )
    reduced = scatter_cols(scatter_rows(shaped, segment_index))
    layer_pick = jnp.arange(LAYERS, dtype=jnp.int32)[:, None, None] == layer_index
    table_stack = jnp.where(layer_pick, table_total[None], 0.0)
    table_sum, gate_sum = lax.psum((table_stack, gate_total), ("batch", "segment"))
    return (
        mixed_out,
        input_out,
        reduced[0][None],
        reduced[1][None],
        reduced[2][None],
        reduced[3][None],
        reduced[4].reshape(1, 2, gain_cols),
        reduced[5].reshape(1, 2, gain_cols),
        table_sum,
        gate_sum,
    )


def solution(mesh):
    placed = (
        P("batch", "segment", None),
        P("batch", None),
        P("batch", "segment", None, None),
        P("segment", None),
        P("segment", None),
        P("segment", None, "batch"),
        P("segment", None, "batch"),
        P("segment", None, "batch"),
        P("segment", None, "batch"),
        P("segment", None, "batch"),
        P("segment", None, "batch"),
        P(),
        P(),
        P("batch", "segment", None),
    )
    return jax.shard_map(
        on_device,
        mesh=mesh,
        in_specs=placed,
        out_specs=(
            P("batch", "segment", None),
            P("batch", "segment", None),
            P("segment", None, "batch"),
            P("segment", None, "batch"),
            P("segment", None, "batch"),
            P("segment", None, "batch"),
            P("segment", None, "batch"),
            P("segment", None, "batch"),
            P(),
            P(),
        ),
        check_vma=False,
    )
```

profile of v0, /device:TPU:1, one launch (start us, length us, event | category | flops | bytes accessed | tf_op | source)
XLA Modules:
  0.0 2678.9 jit_solution(9384507625469070875)
XLA Ops:
  21.8 34.1 %collective-permute-done.7 = bf16[512,768]{1,0:T(8,128)(2,1)S(1)} collective-permute-done((bf16[512,768]{1,0:T(8,128)(2,1)S(1)}, bf16[512,768]{1,0:T(8,128)(2,1)S(1)}, u32[]{:S(2)}, u32[]{:S(2)}) %collective-permute-start.7) | collective-permute-done | bytes 786464 | tf_op jit(solution)/shard_map/ppermute | solution.py:22
  94.6 45.2 %collective-permute-done.15 = bf16[512,1024]{1,0:T(8,128)(2,1)S(1)} collective-permute-done((bf16[512,1024]{1,0:T(8,128)(2,1)S(1)}, bf16[512,1024]{1,0:T(8,128)(2,1)S(1)}, u32[]{:S(2)}, u32[]{:S(2)}) %collective-permute-start.15) | collective-permute-done | bytes 1048608 | tf_op jit(solution)/shard_map/ppermute | solution.py:22
  158.4 45.3 %collective-permute-done.17 = bf16[2048,256]{1,0:T(8,128)(2,1)S(1)} collective-permute-done((bf16[2048,256]{1,0:T(8,128)(2,1)S(1)}, bf16[2048,256]{1,0:T(8,128)(2,1)S(1)}, u32[]{:S(2)}, u32[]{:S(2)}) %collective-permute-start.17) | collective-permute-done | bytes 1048608 | tf_op jit(solution)/shard_map/ppermute | solution.py:22
  219.3 35.8 %copy.488 = pred[256,768,32]{1,2,0:T(32,128)(4,1)} copy(pred[256,768,32]{0,2,1:T(32,128)(4,1)S(1)} %iota_compare_fusion) | data formatting | bytes 12582912 | tf_op jit(solution)/shard_map/eq | solution.py:271
  347.5 53.0 %conditional.10 = (f32[256,8,32]{0,2,1:T(8,128)}, f32[256,1024]{1,0:T(8,128)}) conditional(s32[]{:T(128)} %convert_element_type.651, () %tuple.438, (s32[1,256,8,32]{1,3,2,0:T(8,128)}, bf16[256,1024]{1,0:T(8,128)(2,1)S(1)}, bf16[256,8,128]{2,1,0:T(8,128)(2,1)S(1)}, bf16[256,1024]{1,0:T(8,128)(2,1)S(1)}) %tuple.1018), branch_computations={%region_2.3_spmd, %region_3.12_spmd} | conditional | flops 46928008 | bytes 9044986 | solution.py:369
  480.9 37.5 %conditional.11 = (f32[256,8,32]{0,2,1:T(8,128)S(1)}, f32[256,1024]{1,0:T(8,128)}) conditional(s32[]{:T(128)} %convert_element_type.651, () %tuple.440, (s32[1,256,8,32]{1,3,2,0:T(8,128)S(1)}, bf16[256,1024]{1,0:T(8,128)(2,1)S(1)}, bf16[256,8,128]{2,1,0:T(8,128)(2,1)S(1)}, bf16[256,1024]{1,0:T(8,128)(2,1)S(1)}) %tuple.1019), branch_computations={%region_19.20_spmd, %region_20.29_spmd} | conditional | flops 46928008 | bytes 9044986 | solution.py:369
  596.6 62.9 %conditional.12 = (f32[256,8,32]{0,2,1:T(8,128)}, f32[256,1024]{1,0:T(8,128)}) conditional(s32[]{:T(128)} %convert_element_type.651, () %tuple.442, (s32[1,256,8,32]{1,3,2,0:T(8,128)S(1)}, bf16[256,1024]{1,0:T(8,128)(2,1)S(1)}, bf16[256,8,128]{2,1,0:T(8,128)(2,1)S(1)}, bf16[256,1024]{1,0:T(8,128)(2,1)}) %tuple.1020), branch_computations={%region_35.36_spmd, %region_36.45_spmd} | conditional | flops 46928008 | bytes 11142166 | solution.py:369
  599.3 29.0 %while.284 = (s32[]{:T(128)}, f32[256,8,32]{0,2,1:T(8,128)S(1)}, s32[1,256,8,32]{1,3,2,0:T(8,128)S(1)}, bf16[256,1024]{1,0:T(8,128)(2,1)S(1)}, bf16[256,8,128]{2...) while((s32[]{:T(128)}, f32[256,8,32]{0,2,1:T(8,128)S(1)}, ...), condition=%wide.region_39.39_spmd.clone, body=%wide.region_37.38_spmd.clone.sunk | while | flops 23134244 | bytes 2425253 | solution.py:90
  629.2 28.8 %while.285 = (s32[]{:T(128)}, f32[256,8,128]{0,2,1:T(8,128)S(1)}, bf16[256,1024]{1,0:T(8,128)(2,1)}, s32[1,256,8,32]{1,3,2,0:T(8,128)S(1)}, bf16[256,8,32]{0,2,1...) while((s32[]{:T(128)}, f32[256,8,128]{0,2,1:T(8,128)S(1)}, ...), condition=%wide.region_44.44_spmd.clone, body=%wide.region_42.43_spmd.clone.sunk | while | flops 23527464 | bytes 2818469 | solution.py:109
  734.1 60.5 %conditional.13 = (f32[256,8,32]{0,2,1:T(8,128)}, f32[256,1024]{1,0:T(8,128)}) conditional(s32[]{:T(128)} %convert_element_type.651, () %tuple.444, (s32[1,256,8,32]{1,3,2,0:T(8,128)S(1)}, bf16[256,1024]{1,0:T(8,128)(2,1)}, bf16[256,8,128]{2,1,0:T(8,128)(2,1)S(1)}, bf16[256,1024]{1,0:T(8,128)(2,1)}) %tuple.1021), branch_computations={%region_51.52_spmd, %region_52.61_spmd} | conditional | flops 46928008 | bytes 11142166 | solution.py:369
  764.3 28.8 %while.287 = (s32[]{:T(128)}, f32[256,8,128]{0,2,1:T(8,128)S(1)}, bf16[256,1024]{1,0:T(8,128)(2,1)}, s32[1,256,8,32]{1,3,2,0:T(8,128)S(1)}, bf16[256,8,32]{0,2,1...) while((s32[]{:T(128)}, f32[256,8,128]{0,2,1:T(8,128)S(1)}, ...), condition=%wide.region_60.60_spmd.clone, body=%wide.region_58.59_spmd.clone.sunk | while | flops 23527464 | bytes 2818469 | solution.py:109
  895.0 60.7 %conditional.14 = (f32[256,8,32]{0,2,1:T(8,128)}, f32[256,1024]{1,0:T(8,128)}) conditional(s32[]{:T(128)} %convert_element_type.651, () %tuple.446, (s32[1,256,8,32]{1,3,2,0:T(8,128)S(1)}, bf16[256,1024]{1,0:T(8,128)(2,1)}, bf16[256,8,128]{2,1,0:T(8,128)(2,1)S(1)}, bf16[256,1024]{1,0:T(8,128)(2,1)}) %tuple.1017), branch_computations={%region_67.68_spmd, %region_68.77_spmd} | conditional | flops 46928008 | bytes 11142166 | solution.py:369
  1073.7 91.5 %conditional.15 = (f32[256,1024]{0,1:T(8,128)}) conditional(s32[]{:T(128)} %convert_element_type.651, () %tuple.448, (bf16[256,1024]{1,0:T(8,128)(2,1)}, s32[1,256,8,32]{1,3,2,0:T(8,128)S(1)}, bf16[256,1024]{1,0:T(8,128)(2,1)S(1)}, f32[256,8,32]{0,2,1:T(8,128)}, bf16[256,1024]{1,0:T(8,128)(2,1)S(1)}) %tuple.1012), branch_computations={%region_84.85_spmd, %region_85.93_spmd} | conditional | flops 46925932 | bytes 7996402 | solution.py:511
  1077.8 48.1 %while.290 = (s32[]{:T(128)}, f32[256,8,32]{0,2,1:T(8,128)}, s32[1,256,8,32]{1,3,2,0:T(8,128)S(1)}, bf16[256,1024]{1,0:T(8,128)(2,1)S(1)}, bf16[256,8,128]{2,0,1...) while((s32[]{:T(128)}, f32[256,8,32]{0,2,1:T(8,128)}, ...), condition=%wide.region_88.88_spmd.clone, body=%wide.region_86.87_spmd.clone.sunk | while | flops 23134244 | bytes 2425253 | solution.py:90
  1127.8 37.3 %while.291 = (s32[]{:T(128)}, f32[256,8,128]{0,2,1:T(8,128)}, bf16[256,1024]{1,0:T(8,128)(2,1)S(1)}, s32[1,256,8,32]{1,3,2,0:T(8,128)S(1)}, bf16[256,8,32]{0,2,1...) while((s32[]{:T(128)}, f32[256,8,128]{0,2,1:T(8,128)}, ...), condition=%wide.region_92.92_spmd.clone, body=%wide.region_90.91_spmd.clone.sunk | while | flops 23527464 | bytes 2818469 | solution.py:109
  1253.2 91.6 %conditional.16 = (f32[256,1024]{0,1:T(8,128)}) conditional(s32[]{:T(128)} %convert_element_type.651, () %tuple.450, (bf16[256,1024]{1,0:T(8,128)(2,1)}, s32[1,256,8,32]{1,3,2,0:T(8,128)S(1)}, bf16[256,1024]{1,0:T(8,128)(2,1)S(1)}, f32[256,8,32]{0,2,1:T(8,128)}, bf16[256,1024]{1,0:T(8,128)(2,1)S(1)}) %tuple.1013), branch_computations={%region_98.99_spmd, %region_99.107_spmd} | conditional | flops 46925932 | bytes 7996402 | solution.py:511
  1257.8 47.9 %while.292 = (s32[]{:T(128)}, f32[256,8,32]{0,2,1:T(8,128)}, s32[1,256,8,32]{1,3,2,0:T(8,128)S(1)}, bf16[256,1024]{1,0:T(8,128)(2,1)S(1)}, bf16[256,8,128]{2,0,1...) while((s32[]{:T(128)}, f32[256,8,32]{0,2,1:T(8,128)}, ...), condition=%wide.region_102.102_spmd.clone, body=%wide.region_100.101_spmd.clone.sunk | while | flops 23134244 | bytes 2425253 | solution.py:90
  1307.7 37.0 %while.293 = (s32[]{:T(128)}, f32[256,8,128]{0,2,1:T(8,128)}, bf16[256,1024]{1,0:T(8,128)(2,1)S(1)}, s32[1,256,8,32]{1,3,2,0:T(8,128)S(1)}, bf16[256,8,32]{0,2,1...) while((s32[]{:T(128)}, f32[256,8,128]{0,2,1:T(8,128)}, ...), condition=%wide.region_106.106_spmd.clone, body=%wide.region_104.105_spmd.clone.sunk | while | flops 23527464 | bytes 2818469 | solution.py:109
  1442.5 91.7 %conditional.17 = (f32[256,1024]{0,1:T(8,128)}) conditional(s32[]{:T(128)} %convert_element_type.651, () %tuple.452, (bf16[256,1024]{1,0:T(8,128)(2,1)}, s32[1,256,8,32]{1,3,2,0:T(8,128)S(1)}, bf16[256,1024]{1,0:T(8,128)(2,1)S(1)}, f32[256,8,32]{0,2,1:T(8,128)}, bf16[256,1024]{1,0:T(8,128)(2,1)S(1)}) %tuple.1014), branch_computations={%region_112.113_spmd, %region_113.121_spmd} | conditional | flops 46925932 | bytes 7996402 | solution.py:511
  1447.1 47.7 %while.294 = (s32[]{:T(128)}, f32[256,8,32]{0,2,1:T(8,128)}, s32[1,256,8,32]{1,3,2,0:T(8,128)S(1)}, bf16[256,1024]{1,0:T(8,128)(2,1)S(1)}, bf16[256,8,128]{2,0,1...) while((s32[]{:T(128)}, f32[256,8,32]{0,2,1:T(8,128)}, ...), condition=%wide.region_116.116_spmd.clone, body=%wide.region_114.115_spmd.clone.sunk | while | flops 23134244 | bytes 2425253 | solution.py:90
  1496.7 37.5 %while.295 = (s32[]{:T(128)}, f32[256,8,128]{0,2,1:T(8,128)}, bf16[256,1024]{1,0:T(8,128)(2,1)S(1)}, s32[1,256,8,32]{1,3,2,0:T(8,128)S(1)}, bf16[256,8,32]{0,2,1...) while((s32[]{:T(128)}, f32[256,8,128]{0,2,1:T(8,128)}, ...), condition=%wide.region_120.120_spmd.clone, body=%wide.region_118.119_spmd.clone.sunk | while | flops 23527464 | bytes 2818469 | solution.py:109
  1632.1 91.7 %conditional.18 = (f32[256,1024]{0,1:T(8,128)}) conditional(s32[]{:T(128)} %convert_element_type.651, () %tuple.454, (bf16[256,1024]{1,0:T(8,128)(2,1)}, s32[1,256,8,32]{1,3,2,0:T(8,128)S(1)}, bf16[256,1024]{1,0:T(8,128)(2,1)S(1)}, f32[256,8,32]{0,2,1:T(8,128)}, bf16[256,1024]{1,0:T(8,128)(2,1)S(1)}) %tuple.1023), branch_computations={%region_126.127_spmd, %region_127.135_spmd} | conditional | flops 46925932 | bytes 7996402 | solution.py:511
  1636.7 47.7 %while.296 = (s32[]{:T(128)}, f32[256,8,32]{0,2,1:T(8,128)}, s32[1,256,8,32]{1,3,2,0:T(8,128)S(1)}, bf16[256,1024]{1,0:T(8,128)(2,1)S(1)}, bf16[256,8,128]{2,0,1...) while((s32[]{:T(128)}, f32[256,8,32]{0,2,1:T(8,128)}, ...), condition=%wide.region_130.130_spmd.clone, body=%wide.region_128.129_spmd.clone.sunk | while | flops 23134244 | bytes 2425253 | solution.py:90
  1686.3 37.5 %while.297 = (s32[]{:T(128)}, f32[256,8,128]{0,2,1:T(8,128)}, bf16[256,1024]{1,0:T(8,128)(2,1)S(1)}, s32[1,256,8,32]{1,3,2,0:T(8,128)S(1)}, bf16[256,8,32]{0,2,1...) while((s32[]{:T(128)}, f32[256,8,128]{0,2,1:T(8,128)}, ...), condition=%wide.region_134.134_spmd.clone, body=%wide.region_132.133_spmd.clone.sunk | while | flops 23527464 | bytes 2818469 | solution.py:109
  1833.6 28.9 %add_add_fusion.1 = f32[1024,4096]{1,0:T(8,128)} fusion(f32[1024,4096]{1,0:T(8,128)} %fusion.436, f32[1024,4096]{1,0:T(8,128)} %fusion.438, f32[1024,4096]{1,0:T(8,128)} %fusion.442, f32[1024,4096]{1,0:T(8,128)} %fusion.440, bf16[256,4096]{1,0:T(8,128)(2,1)} %copy-done.121, f32[256,1024]{1,0:T(8,128)S(1)} %copy-done.58, f32[1024]{0:T(1024)S(1)} %add.1664, ...), kind=kOutput, calls=%fused_computation.247 | convolution fusion | flops 2165571584 | bytes 87042048 | tf_op jit(solution)/shard_map/rd,rf->df/dot_general | solution.py:443
  1870.9 69.5 %conditional.19 = (f32[256,1024]{0,1:T(8,128)}) conditional(s32[]{:T(128)} %convert_element_type.651, () %tuple.456, (bf16[256,1024]{1,0:T(8,128)(2,1)S(1)}, s32[1,256,8,32]{1,3,2,0:T(8,128)}, bf16[256,1024]{1,0:T(8,128)(2,1)S(1)}, f32[256,8,32]{0,2,1:T(8,128)}, bf16[256,1024]{1,0:T(8,128)(2,1)S(1)}) %tuple.1022), branch_computations={%region_140.141_spmd, %region_141.149_spmd} | conditional | flops 46925932 | bytes 7996402 | solution.py:511
  1902.7 37.5 %while.299 = (s32[]{:T(128)}, f32[256,8,128]{0,2,1:T(8,128)}, bf16[256,1024]{1,0:T(8,128)(2,1)S(1)}, s32[1,256,8,32]{1,3,2,0:T(8,128)}, bf16[256,8,32]{0,2,1:T(8...) while((s32[]{:T(128)}, f32[256,8,128]{0,2,1:T(8,128)}, ...), condition=%wide.region_148.148_spmd.clone, body=%wide.region_146.147_spmd.clone.sunk | while | flops 23527464 | bytes 2818469 | solution.py:109
  1981.6 30.6 %add_add_fusion = f32[4096,1024]{1,0:T(8,128)} fusion(f32[4096,1024]{1,0:T(8,128)} %fusion.444, f32[4096,1024]{1,0:T(8,128)} %fusion.445, f32[4096,1024]{1,0:T(8,128)} %fusion.382, f32[4096,1024]{1,0:T(8,128)} %fusion.446, bf16[256,1024]{1,0:T(8,128)(2,1)S(1)} %copy-done.120, pred[]{:T(512)S(6)} %eq.964, f32[256,4096]{1,0:T(8,128)} %fusion.435), kind=kOutput, calls=%fused_computation.246 | convolution fusion | flops 2174484480 | bytes 88604672 | tf_op jit(solution)/shard_map/rf,rd->fd/dot_general | solution.py:436
  2012.2 71.3 %collective-permute-done.67 = bf16[512,1024]{1,0:T(8,128)(2,1)} collective-permute-done((bf16[512,1024]{1,0:T(8,128)(2,1)}, bf16[512,1024]{1,0:T(8,128)(2,1)}, u32[]{:S(2)}, u32[]{:S(2)}) %collective-permute-start.67) | collective-permute-done | bytes 1048608 | tf_op jit(solution)/shard_map/ppermute | solution.py:22
  2106.8 223.8 %collective-permute-done.65 = bf16[512,3072]{1,0:T(8,128)(2,1)} collective-permute-done((bf16[512,3072]{1,0:T(8,128)(2,1)}, bf16[512,3072]{1,0:T(8,128)(2,1)}, u32[]{:S(2)}, u32[]{:S(2)}) %collective-permute-start.65) | collective-permute-done | bytes 3145760 | tf_op jit(solution)/shard_map/ppermute | solution.py:22
  2353.8 94.3 %collective-permute-done.66 = bf16[256,3072]{1,0:T(8,128)(2,1)S(1)} collective-permute-done((bf16[256,3072]{1,0:T(8,128)(2,1)S(1)}, bf16[256,3072]{1,0:T(8,128)(2,1)S(1)}, u32[]{:S(2)}, u32[]{:S(2)}) %collective-permute-start.66) | collective-permute-done | bytes 1572896 | tf_op jit(solution)/shard_map/ppermute | solution.py:22
  2566.4 48.9 %all-reduce.3 = (f32[2,32,8]{1,2,0:T(8,128)}, f32[8]{0:T(128)}) all-reduce(f32[2,32,8]{1,2,0:T(8,128)S(1)} %broadcast_select_fusion.16, f32[8]{0:T(128)S(1)} %multiply_multiply_fusion.10), channel_id=1, replica_groups=mesh['batch'=4,'segment'=8] {'batch','segment'}, use_global_device_ids=true, to_apply=%region_177.178 | all-reduce | flops 520 | bytes 4160 | tf_op jit(solution)/shard_map/psum | solution.py:564
  (1864 shorter events, 2192.2 us)
Async XLA Ops:
  7.2 311.5 %all-gather.5.cloned.1.call-start = ((), (), s32[]{:S(2)}) async-start(), calls=%async_computation.4 | async-start | bytes 7864320 | tf_op jit(solution)/shard_map/all_gather | solution.py:137
  57.6 374.9 %all-gather.7.cloned.1.call-start = ((), (), s32[]{:S(2)}) async-start(), calls=%async_computation.5 | async-start | bytes 2621440 | tf_op jit(solution)/shard_map/all_gather | solution.py:138
  78.0 357.6 %all-gather.9.cloned.1.call-start = ((), (), s32[]{:S(2)}) async-start(), calls=%async_computation.6 | async-start | bytes 10485760 | tf_op jit(solution)/shard_map/all_gather | solution.py:139
  141.8 301.7 %all-gather.11.cloned.1.call-start = ((), (), s32[]{:S(2)}) async-start(), calls=%async_computation.7 | async-start | bytes 10485760 | tf_op jit(solution)/shard_map/all_gather | solution.py:140
  205.8 2458.3 %reduce-scatter.9.cloned.1.call-start = ((), (), s32[]{:S(2)}) async-start(), calls=%async_computation.9 | async-start | bytes 655360 | tf_op jit(solution)/shard_map/reduce_scatter | solution.py:181
  205.8 108.7 %collective-permute-start = (bf16[4,128,1024]{2,1,0:T(8,128)(2,1)}, bf16[4,128,1024]{2,1,0:T(8,128)(2,1)}, u32[]{:S(2)}, u32[]{:S(2)}) collective-permute-start(bf16[4,128,1024]{2,1,0:T(8,128)(2,1)} %param.75), channel_id=1, source_target_pairs={{1,0},{2,1},{3,2},{4,3},{5,4},{6,5},{7,6},{9,8},{10,9},{11,10},{12... | collective-permute-start | bytes 3145736 | tf_op jit(solution)/shard_map/ppermute | solution.py:36
  210.5 128.6 %collective-permute-start.1 = (s32[4,128,8,32]{1,3,2,0:T(8,128)}, s32[4,128,8,32]{1,3,2,0:T(8,128)}, u32[]{:S(2)}, u32[]{:S(2)}) collective-permute-start(s32[4,128,8,32]{1,3,2,0:T(8,128)} %param.77), channel_id=1, source_target_pairs={{0,1},{1,2},{2,3},{3,4},{4,5},{5,6},{6,7},{8,9},{9,10},{10,11},{11... | collective-permute-start | bytes 1572872 | tf_op jit(solution)/shard_map/ppermute | solution.py:36
  1246.8 113.6 %collective-permute-start.48 = (bf16[1,256,1024]{1,2,0:T(8,128)(2,1)}, bf16[1,256,1024]{1,2,0:T(8,128)(2,1)}, u32[]{:S(2)}, u32[]{:S(2)}) collective-permute-start(bf16[1,256,1024]{1,2,0:T(8,128)(2,1)} %get-tuple-element.3349), channel_id=1, source_target_pairs={{4,0},{5,1},{6,2},{7,3},{12,8},{13,9},{14,10},{15,11},{20,16},{21,... | collective-permute-start | bytes 1572872 | tf_op jit(solution)/shard_map/ppermute | solution.py:36
  1248.1 112.4 %collective-permute-start.47 = (bf16[1,256,1024]{1,2,0:T(8,128)(2,1)}, bf16[1,256,1024]{1,2,0:T(8,128)(2,1)}, u32[]{:S(2)}, u32[]{:S(2)}) collective-permute-start(bf16[1,256,1024]{1,2,0:T(8,128)(2,1)} %get-tuple-element.3348), channel_id=1, source_target_pairs={{2,0},{3,1},{4,2},{5,3},{6,4},{7,5},{10,8},{11,9},{12,10},{13,11},... | collective-permute-start | bytes 1572872 | tf_op jit(solution)/shard_map/ppermute | solution.py:36
  1250.6 111.5 %collective-permute-start.46 = (bf16[1,256,1024]{1,2,0:T(8,128)(2,1)}, bf16[1,256,1024]{1,2,0:T(8,128)(2,1)}, u32[]{:S(2)}, u32[]{:S(2)}) collective-permute-start(bf16[1,256,1024]{1,2,0:T(8,128)(2,1)} %get-tuple-element.3341), channel_id=1, source_target_pairs={{4,0},{5,1},{6,2},{7,3},{12,8},{13,9},{14,10},{15,11},{20,16},{21,... | collective-permute-start | bytes 1572872 | tf_op jit(solution)/shard_map/ppermute | solution.py:36
  1251.9 110.3 %collective-permute-start.45 = (bf16[1,256,1024]{1,2,0:T(8,128)(2,1)}, bf16[1,256,1024]{1,2,0:T(8,128)(2,1)}, u32[]{:S(2)}, u32[]{:S(2)}) collective-permute-start(bf16[1,256,1024]{1,2,0:T(8,128)(2,1)} %get-tuple-element.3340), channel_id=1, source_target_pairs={{2,0},{3,1},{4,2},{5,3},{6,4},{7,5},{10,8},{11,9},{12,10},{13,11},... | collective-permute-start | bytes 1572872 | tf_op jit(solution)/shard_map/ppermute | solution.py:36
  1436.1 113.9 %collective-permute-start.53 = (bf16[1,256,1024]{1,2,0:T(8,128)(2,1)}, bf16[1,256,1024]{1,2,0:T(8,128)(2,1)}, u32[]{:S(2)}, u32[]{:S(2)}) collective-permute-start(bf16[1,256,1024]{1,2,0:T(8,128)(2,1)} %get-tuple-element.3339), channel_id=1, source_target_pairs={{4,0},{5,1},{6,2},{7,3},{12,8},{13,9},{14,10},{15,11},{20,16},{21,... | collective-permute-start | bytes 1572872 | tf_op jit(solution)/shard_map/ppermute | solution.py:36
  1437.4 112.6 %collective-permute-start.52 = (bf16[1,256,1024]{1,2,0:T(8,128)(2,1)}, bf16[1,256,1024]{1,2,0:T(8,128)(2,1)}, u32[]{:S(2)}, u32[]{:S(2)}) collective-permute-start(bf16[1,256,1024]{1,2,0:T(8,128)(2,1)} %get-tuple-element.3338), channel_id=1, source_target_pairs={{2,0},{3,1},{4,2},{5,3},{6,4},{7,5},{10,8},{11,9},{12,10},{13,11},... | collective-permute-start | bytes 1572872 | tf_op jit(solution)/shard_map/ppermute | solution.py:36
  1439.9 111.8 %collective-permute-start.51 = (bf16[1,256,1024]{1,2,0:T(8,128)(2,1)}, bf16[1,256,1024]{1,2,0:T(8,128)(2,1)}, u32[]{:S(2)}, u32[]{:S(2)}) collective-permute-start(bf16[1,256,1024]{1,2,0:T(8,128)(2,1)} %get-tuple-element.3331), channel_id=1, source_target_pairs={{4,0},{5,1},{6,2},{7,3},{12,8},{13,9},{14,10},{15,11},{20,16},{21,... | collective-permute-start | bytes 1572872 | tf_op jit(solution)/shard_map/ppermute | solution.py:36
  1441.2 110.5 %collective-permute-start.50 = (bf16[1,256,1024]{1,2,0:T(8,128)(2,1)}, bf16[1,256,1024]{1,2,0:T(8,128)(2,1)}, u32[]{:S(2)}, u32[]{:S(2)}) collective-permute-start(bf16[1,256,1024]{1,2,0:T(8,128)(2,1)} %get-tuple-element.3330), channel_id=1, source_target_pairs={{2,0},{3,1},{4,2},{5,3},{6,4},{7,5},{10,8},{11,9},{12,10},{13,11},... | collective-permute-start | bytes 1572872 | tf_op jit(solution)/shard_map/ppermute | solution.py:36
  1625.8 113.8 %collective-permute-start.58 = (bf16[1,256,1024]{1,2,0:T(8,128)(2,1)}, bf16[1,256,1024]{1,2,0:T(8,128)(2,1)}, u32[]{:S(2)}, u32[]{:S(2)}) collective-permute-start(bf16[1,256,1024]{1,2,0:T(8,128)(2,1)} %get-tuple-element.3329), channel_id=1, source_target_pairs={{4,0},{5,1},{6,2},{7,3},{12,8},{13,9},{14,10},{15,11},{20,16},{21,... | collective-permute-start | bytes 1572872 | tf_op jit(solution)/shard_map/ppermute | solution.py:36
  1627.0 112.5 %collective-permute-start.57 = (bf16[1,256,1024]{1,2,0:T(8,128)(2,1)}, bf16[1,256,1024]{1,2,0:T(8,128)(2,1)}, u32[]{:S(2)}, u32[]{:S(2)}) collective-permute-start(bf16[1,256,1024]{1,2,0:T(8,128)(2,1)} %get-tuple-element.3328), channel_id=1, source_target_pairs={{2,0},{3,1},{4,2},{5,3},{6,4},{7,5},{10,8},{11,9},{12,10},{13,11},... | collective-permute-start | bytes 1572872 | tf_op jit(solution)/shard_map/ppermute | solution.py:36
  1629.5 111.7 %collective-permute-start.56 = (bf16[1,256,1024]{1,2,0:T(8,128)(2,1)}, bf16[1,256,1024]{1,2,0:T(8,128)(2,1)}, u32[]{:S(2)}, u32[]{:S(2)}) collective-permute-start(bf16[1,256,1024]{1,2,0:T(8,128)(2,1)} %get-tuple-element.3321), channel_id=1, source_target_pairs={{4,0},{5,1},{6,2},{7,3},{12,8},{13,9},{14,10},{15,11},{20,16},{21,... | collective-permute-start | bytes 1572872 | tf_op jit(solution)/shard_map/ppermute | solution.py:36
  1630.8 110.4 %collective-permute-start.55 = (bf16[1,256,1024]{1,2,0:T(8,128)(2,1)}, bf16[1,256,1024]{1,2,0:T(8,128)(2,1)}, u32[]{:S(2)}, u32[]{:S(2)}) collective-permute-start(bf16[1,256,1024]{1,2,0:T(8,128)(2,1)} %get-tuple-element.3320), channel_id=1, source_target_pairs={{2,0},{3,1},{4,2},{5,3},{6,4},{7,5},{10,8},{11,9},{12,10},{13,11},... | collective-permute-start | bytes 1572872 | tf_op jit(solution)/shard_map/ppermute | solution.py:36
  1796.7 148.4 %collective-permute-start.63 = (bf16[1,256,1024]{1,2,0:T(8,128)(2,1)}, bf16[1,256,1024]{1,2,0:T(8,128)(2,1)}, u32[]{:S(2)}, u32[]{:S(2)}) collective-permute-start(bf16[1,256,1024]{1,2,0:T(8,128)(2,1)} %get-tuple-element.3319), channel_id=1, source_target_pairs={{4,0},{5,1},{6,2},{7,3},{12,8},{13,9},{14,10},{15,11},{20,16},{21,... | collective-permute-start | bytes 1572872 | tf_op jit(solution)/shard_map/ppermute | solution.py:36
  1798.0 147.2 %collective-permute-start.62 = (bf16[1,256,1024]{1,2,0:T(8,128)(2,1)}, bf16[1,256,1024]{1,2,0:T(8,128)(2,1)}, u32[]{:S(2)}, u32[]{:S(2)}) collective-permute-start(bf16[1,256,1024]{1,2,0:T(8,128)(2,1)} %get-tuple-element.3318), channel_id=1, source_target_pairs={{2,0},{3,1},{4,2},{5,3},{6,4},{7,5},{10,8},{11,9},{12,10},{13,11},... | collective-permute-start | bytes 1572872 | tf_op jit(solution)/shard_map/ppermute | solution.py:36
  1807.9 139.1 %collective-permute-start.61 = (bf16[1,256,1024]{1,2,0:T(8,128)(2,1)}, bf16[1,256,1024]{1,2,0:T(8,128)(2,1)}, u32[]{:S(2)}, u32[]{:S(2)}) collective-permute-start(bf16[1,256,1024]{1,2,0:T(8,128)(2,1)} %get-tuple-element.3311), channel_id=1, source_target_pairs={{4,0},{5,1},{6,2},{7,3},{12,8},{13,9},{14,10},{15,11},{20,16},{21,... | collective-permute-start | bytes 1572872 | tf_op jit(solution)/shard_map/ppermute | solution.py:36
  1809.4 137.5 %collective-permute-start.60 = (bf16[1,256,1024]{1,2,0:T(8,128)(2,1)}, bf16[1,256,1024]{1,2,0:T(8,128)(2,1)}, u32[]{:S(2)}, u32[]{:S(2)}) collective-permute-start(bf16[1,256,1024]{1,2,0:T(8,128)(2,1)} %get-tuple-element.3310), channel_id=1, source_target_pairs={{2,0},{3,1},{4,2},{5,3},{6,4},{7,5},{10,8},{11,9},{12,10},{13,11},... | collective-permute-start | bytes 1572872 | tf_op jit(solution)/shard_map/ppermute | solution.py:36
  1817.6 265.9 %collective-permute-start.67 = (bf16[512,1024]{1,0:T(8,128)(2,1)}, bf16[512,1024]{1,0:T(8,128)(2,1)}, u32[]{:S(2)}, u32[]{:S(2)}) collective-permute-start(bf16[512,1024]{1,0:T(8,128)(2,1)} %select_convert_fusion.6), channel_id=1, source_target_pairs={{0,4},{1,5},{2,6},{3,7},{4,0},{5,1},{6,2},{7,3},{8,12},{9,13},{10,... | collective-permute-start | bytes 3145736 | tf_op jit(solution)/shard_map/ppermute | solution.py:22
  1945.2 393.6 %collective-permute-start.69 = (bf16[512,4096]{1,0:T(8,128)(2,1)}, bf16[512,4096]{1,0:T(8,128)(2,1)}, u32[]{:S(2)}, u32[]{:S(2)}) collective-permute-start(bf16[512,4096]{1,0:T(8,128)(2,1)} %select_convert_fusion.1), channel_id=1, source_target_pairs={{0,4},{1,5},{2,6},{3,7},{4,0},{5,1},{6,2},{7,3},{8,12},{9,13},{10,... | collective-permute-start | bytes 12582920 | tf_op jit(solution)/shard_map/ppermute | solution.py:22
  1979.3 351.4 %collective-permute-start.65 = (bf16[512,3072]{1,0:T(8,128)(2,1)}, bf16[512,3072]{1,0:T(8,128)(2,1)}, u32[]{:S(2)}, u32[]{:S(2)}) collective-permute-start(bf16[512,3072]{1,0:T(8,128)(2,1)} %select_convert_fusion.2), channel_id=1, source_target_pairs={{0,4},{1,5},{2,6},{3,7},{4,0},{5,1},{6,2},{7,3},{8,12},{9,13},{10,... | collective-permute-start | bytes 9437192 | tf_op jit(solution)/shard_map/ppermute | solution.py:22
  2095.3 439.5 %collective-permute-start.71 = (bf16[2048,1024]{1,0:T(8,128)(2,1)}, bf16[2048,1024]{1,0:T(8,128)(2,1)}, u32[]{:S(2)}, u32[]{:S(2)}) collective-permute-start(bf16[2048,1024]{1,0:T(8,128)(2,1)} %select_convert_fusion), channel_id=1, source_target_pairs={{0,4},{1,5},{2,6},{3,7},{4,0},{5,1},{6,2},{7,3},{8,12},{9,13},{10,... | collective-permute-start | bytes 12582920 | tf_op jit(solution)/shard_map/ppermute | solution.py:22
  2106.8 558.9 %reduce-scatter.7.cloned.1.call-start = ((), (), s32[]{:S(2)}) async-start(), calls=%async_computation.8 | async-start | bytes 1966080 | tf_op jit(solution)/shard_map/reduce_scatter | solution.py:178
  2338.7 109.3 %collective-permute-start.66 = (bf16[256,3072]{1,0:T(8,128)(2,1)S(1)}, bf16[256,3072]{1,0:T(8,128)(2,1)S(1)}, u32[]{:S(2)}, u32[]{:S(2)}) collective-permute-start(bf16[256,3072]{1,0:T(8,128)(2,1)S(1)} %select_convert_fusion.5), channel_id=1, source_target_pairs={{0,2},{1,3},{2,0},{3,1},{4,6},{5,7},{6,4},{7,5},{8,10},{9,11},{10,... | collective-permute-start | bytes 4718600 | tf_op jit(solution)/shard_map/ppermute | solution.py:22
  2352.3 163.8 %collective-permute-start.70 = (bf16[256,4096]{1,0:T(8,128)(2,1)}, bf16[256,4096]{1,0:T(8,128)(2,1)}, u32[]{:S(2)}, u32[]{:S(2)}) collective-permute-start(bf16[256,4096]{1,0:T(8,128)(2,1)} %select_convert_fusion.4), channel_id=1, source_target_pairs={{0,2},{1,3},{2,0},{3,1},{4,6},{5,7},{6,4},{7,5},{8,10},{9,11},{10,... | collective-permute-start | bytes 6291464 | tf_op jit(solution)/shard_map/ppermute | solution.py:22
  2450.0 217.6 %reduce-scatter.11.cloned.1.call-start = ((), (), s32[]{:S(2)}) async-start(), calls=%async_computation.10 | async-start | bytes 2621440 | tf_op jit(solution)/shard_map/reduce_scatter | solution.py:184
  2522.8 147.0 %reduce-scatter.13.cloned.1.call-start = ((), (), s32[]{:S(2)}) async-start(), calls=%async_computation.11 | async-start | bytes 2621440 | tf_op jit(solution)/shard_map/reduce_scatter | solution.py:187
  (374 other events, 7059.0 us)
Sparse Core Ops, SparseCore 0:
  57.7 71.8 all-gather.4
  131.5 35.1 all-gather.6
  168.5 87.6 all-gather.8
  257.9 87.6 all-gather.10
  2106.9 21.3 reduce-scatter.8
  2450.1 27.6 reduce-scatter.6
  2522.8 32.6 reduce-scatter.10
  2628.7 35.8 reduce-scatter.12
where the time goes:
time: 2700 us; the launch traced here: 2680 us
  matrix products  841 us (31%)
  other arithmetic  661 us (24%)
  waiting for transfers between devices  635 us (24%)
  local copies, waits for them, and re-layouts  259 us (10%)
  starting transfers between devices  155 us (6%)
  blocking collectives  101 us (4%)
    ppermute x24, waiting for transfers between devices, from_partner(): lax.ppermute(shard, axis, [(i, i ^ 1 << bit) for i in range(lax.axis_size...  581 us
    reduce_sum x80, other arithmetic, pick_step(): jnp.sum(jnp.where(matched, scores[:, :, None, :], 0.0), axis=-1)  213 us
    reduce_sum x80, other arithmetic, place_step(): jnp.sum(jnp.where(matched, chosen[..., None], jnp.zeros((), jnp.bfloat16)...  171 us
    dot_general x80, matrix products, place_step(): jnp.einsum('rhc,chd->rhd', spread, section, preferred_element_type=jnp.fl...  137 us
    ppermute x53, starting transfers between devices, shifted(): return lax.ppermute(block, axis, route)  106 us
    dot_general x80, matrix products, pick_step(): jnp.einsum('rhd,chd->rhc', queries, section, preferred_element_type=jnp.f...  76.5 us
    dot_general x5, matrix products, on_device(): jnp.einsum('rf,rd->fd', activity, upstream_low, preferred_element_type=jn...  74.9 us
    unnamed x663, local copies, waits for them, and re-layouts  72.4 us
  transfers between devices with their start and end apart: 85, of which 26 were waited for; matrix products, arithmetic and copies ran while one was open for 49% of the time, Pallas kernels for 0%

commit v1 on v0

v1 whole, which is shorter than its diff:
```python
import functools
import math

import jax
import jax.numpy as jnp
import numpy as np
from jax import lax
from jax.experimental import pallas as pl
from jax.experimental.pallas import tpu as pltpu
from jax.sharding import PartitionSpec as P

WIN = 512
LAYERS = 2
CORES = 2
QB = 256

norm_eps = 1e-05
big_negative = -1e30
bucket_edges = np.ceil(16.0 * 8.0 ** (np.arange(1, 16) / 16.0)).astype(np.int32)
highest = lax.Precision.HIGHEST
f32 = jnp.float32
bf16 = jnp.bfloat16
VMEM_LIMIT = 48 * 1024 * 1024


def permuted(block, axis, route):
    count = lax.axis_size(axis)
    return lax.ppermute(block, axis, [(i, route(i)) for i in range(count)])


def core_swap(block):
    return permuted(block, "segment", lambda i: i ^ 1)


def pick(index, parts):
    return lax.select_n(index, *parts)


def ring_gather(block, stretch):
    count = lax.axis_size("segment")
    total = count // CORES
    parts = [block]
    for _ in range(total - 1):
        parts.append(permuted(parts[-1], "segment", lambda i: (i + CORES) % count))
    return jnp.concatenate([pick((stretch - k) % total, parts) for k in range(total)], axis=1)


def plane_gather(block, batch):
    rows = block.shape[0]
    half = rows // 2
    across = permuted(block, "batch", lambda i: i ^ 1)
    along = permuted(block, "batch", lambda i: i ^ 2)
    far_low = permuted(along[:half], "batch", lambda i: i ^ 1)
    far_high = permuted(across[half:], "batch", lambda i: i ^ 2)
    whole = jnp.zeros((4 * rows,) + block.shape[1:], block.dtype)
    whole = lax.dynamic_update_slice(whole, block, (batch * rows, 0))
    whole = lax.dynamic_update_slice(whole, across, ((batch ^ 1) * rows, 0))
    whole = lax.dynamic_update_slice(whole, along, ((batch ^ 2) * rows, 0))
    whole = lax.dynamic_update_slice(whole, far_low, ((batch ^ 3) * rows, 0))
    return lax.dynamic_update_slice(whole, far_high, ((batch ^ 3) * rows + half, 0))


def plane_scatter(whole, batch):
    rows = whole.shape[0] // 4
    half = rows // 2

    def part(which, first, size):
        return lax.dynamic_slice_in_dim(whole, (batch ^ which) * rows + first, size, 0)

    def total(*terms):
        return functools.reduce(jnp.add, [t.astype(f32) for t in terms])

    got_low = permuted(part(3, 0, half), "batch", lambda i: i ^ 1)
    got_high = permuted(part(3, half, half), "batch", lambda i: i ^ 2)
    to_along = jnp.concatenate(
        [total(part(2, 0, half), got_low).astype(bf16), part(2, half, half)], axis=0
    )
    to_across = jnp.concatenate(
        [part(1, 0, half), total(part(1, half, half), got_high).astype(bf16)], axis=0
    )
    from_along = permuted(to_along, "batch", lambda i: i ^ 2)
    from_across = permuted(to_across, "batch", lambda i: i ^ 1)
    return total(part(0, 0, rows), from_along, from_across)


def ring_scatter(block, stretch):
    count = lax.axis_size("segment")
    total = count // CORES
    width = block.shape[1] // total
    columns = [block[:, k * width : (k + 1) * width] for k in range(total)]

    def own(offset):
        return pick((stretch - offset) % total, columns)

    travelling = own(1).astype(bf16)
    for step in range(1, total):
        got = permuted(travelling, "segment", lambda i: (i + CORES) % count)
        summed = got.astype(f32) + own(1 + step).astype(f32)
        travelling = summed.astype(bf16)
    return summed


def qkv_half(matrix, core):
    rows, cols = matrix.shape
    split = matrix.reshape(rows, cols // 256, 2, 128)
    return split[:, :, core].reshape(rows, cols // 2).T


def out_half(matrix, core):
    rows, cols = matrix.shape
    return matrix.reshape(rows // 256, 2, 128, cols)[:, core].reshape(rows // 2, cols).T


def in_half(matrix, core, parts):
    rows, cols = matrix.shape
    return matrix.reshape(rows, parts, 2, cols // parts // 2)[:, :, core].reshape(rows, cols // 2).T


def down_half(matrix, core, parts):
    rows, cols = matrix.shape
    return matrix.reshape(parts, 2, rows // parts // 2, cols)[:, core].reshape(rows // 2, cols).T


def qkv_whole(halves):
    cols, rows = halves[0].shape
    stacked = jnp.stack([h.T.reshape(rows, cols // 128, 128) for h in halves], axis=2)
    return stacked.reshape(rows, 2 * cols)


def out_whole(halves):
    cols, rows = halves[0].shape
    stacked = jnp.stack([h.T.reshape(rows // 128, 128, cols) for h in halves], axis=1)
    return stacked.reshape(2 * rows, cols)


def in_whole(halves, parts):
    cols, rows = halves[0].shape
    stacked = jnp.stack([h.T.reshape(rows, parts, cols // parts) for h in halves], axis=2)
    return stacked.reshape(rows, 2 * cols)


def down_whole(halves, parts):
    cols, rows = halves[0].shape
    stacked = jnp.stack([h.T.reshape(parts, rows // parts, cols) for h in halves], axis=1)
    return stacked.reshape(2 * rows, cols)


def halves_of(parts):
    return (
        qkv_half,
        out_half,
        functools.partial(in_half, parts=parts),
        functools.partial(down_half, parts=parts),
    )


def wholes_of(parts):
    return (
        qkv_whole,
        out_whole,
        functools.partial(in_whole, parts=parts),
        functools.partial(down_whole, parts=parts),
    )


def gather_by_chip(shards, core, stretch, batch):
    low_core = core == 0
    layers = ([], [])
    for shard, half in zip(shards, halves_of(1)):
        first, second = half(shard, 0), half(shard, 1)
        mine = jnp.where(low_core, first, second)
        got = core_swap(jnp.where(low_core, second, first))
        for layer, block in ((0, jnp.where(low_core, mine, got)), (1, jnp.where(low_core, got, mine))):
            layers[layer].append(plane_gather(ring_gather(block, stretch), batch))
    return layers


def gather_plain(shards, core):
    layers = ([], [])
    for shard, half in zip(shards, halves_of(4)):
        rows = lax.all_gather(shard, "batch", axis=1, tiled=True)
        slots = lax.all_gather(rows, "segment", axis=0, tiled=False)
        for layer in range(LAYERS):
            matrix = slots[layer::LAYERS].reshape(-1, rows.shape[1])
            layers[layer].append(
                jnp.where(core == 0, half(matrix, 0), half(matrix, 1))
            )
    return layers


def scatter_by_chip(grads, stretch, batch):
    return ring_scatter(plane_scatter(grads, batch), stretch)


def finish_by_chip(parts, core):
    low_core = core == 0
    done = []
    for lower, upper, whole in zip(parts[0], parts[1], wholes_of(1)):
        kept = jnp.where(low_core, lower, upper)
        got = core_swap(jnp.where(low_core, upper, lower).astype(bf16)).astype(f32)
        done.append(whole((jnp.where(low_core, kept, got), jnp.where(low_core, got, kept)))[None])
    return done


def scatter_plain(parts, core):
    done = []
    slots = lax.axis_size("segment")
    for lower, upper, whole in zip(parts[0], parts[1], wholes_of(4)):
        layers = []
        for half in (lower, upper):
            empty = jnp.zeros_like(half)
            matrix = whole((jnp.where(core == 0, half, empty), jnp.where(core == 0, empty, half)))
            layers.append(matrix.reshape(slots // LAYERS, -1, matrix.shape[1]))
        stacked = jnp.stack(layers, axis=1).reshape(slots, -1, layers[0].shape[2])
        rows = lax.psum_scatter(stacked, "segment", scatter_dimension=0, tiled=True)
        columns = lax.psum_scatter(rows, "batch", scatter_dimension=2, tiled=True)
        done.append(columns.astype(f32))
    return done


def spans(row_count, halo):
    for first in range(0, row_count, QB):
        start = max(0, first + halo - WIN)
        yield first, start, first + halo + QB - start


def mask_kernel(index_ref, mask_ref):
    rows, slots = mask_ref.shape[1], mask_ref.shape[2]
    chunk = 64
    width = 256
    for low in range(0, slots, width):
        slot_ids = lax.broadcasted_iota(jnp.int32, (chunk, width), 1) + low

        def step(turn, carry):
            first = pl.multiple_of(turn * chunk, chunk)
            index = index_ref[0, pl.ds(first, chunk), :]
            bias = jnp.full((chunk, width), big_negative, f32)
            for t in range(index.shape[1]):
                bias = jnp.where(index[:, t : t + 1] == slot_ids, 0.0, bias)
            mask_ref[0, pl.ds(first, chunk), low : low + width] = bias.astype(bf16)
            return carry

        lax.fori_loop(0, rows // chunk, step, 0)


def slot_mask(index, slots):
    heads, rows, chosen = index.shape
    return pl.pallas_call(
        mask_kernel,
        out_shape=jax.ShapeDtypeStruct((heads, rows, slots), bf16),
        grid=(heads,),
        in_specs=[pl.BlockSpec((1, rows, chosen), lambda h: (h, 0, 0))],
        out_specs=pl.BlockSpec((1, rows, slots), lambda h: (h, 0, 0)),
        compiler_params=pltpu.CompilerParams(vmem_limit_bytes=VMEM_LIMIT),
        cost_estimate=pl.CostEstimate(
            flops=2 * heads * rows * slots * chosen, transcendentals=0, bytes_accessed=4 * heads * rows * slots
        ),
        name="slot_mask",
    )(index)


def nt_dot(left, right):
    return lax.dot_general(left, right, (((1,), (1,)), ((), ())), preferred_element_type=f32)


def tn_dot(left, right):
    return lax.dot_general(left, right, (((0,), (0,)), ((), ())), preferred_element_type=f32)


def nn_dot(left, right):
    return lax.dot_general(left, right, (((1,), (0,)), ((), ())), preferred_element_type=f32)


def forward_kernel(halo, with_memory, scale, *refs):
    refs = list(refs)
    bias_ref, docs_col, docs_row, q_ref, k_ref, v_ref = refs[:6]
    del refs[:6]
    if halo:
        k_halo, v_halo = refs[:2]
        del refs[:2]
    if with_memory:
        mem_k, mem_v, mask_ref, gate_ref = refs[:4]
        del refs[:4]
        o_ref, probs_ref, slots_ref, differ_ref = refs[:4]
        del refs[:4]
    else:
        o_ref, probs_ref = refs[:2]
        del refs[:2]
    if halo:
        keys, values = refs
        keys[:halo] = k_halo[...]
        keys[halo:] = k_ref[...]
        values[:halo] = v_halo[...]
        values[halo:] = v_ref[...]
    else:
        keys, values = k_ref, v_ref
    width = WIN + QB
    lanes = bias_ref.shape[2]
    tile = pltpu.roll(
        jnp.broadcast_to(bias_ref[0], (QB, lanes)), 0, axis=1, stride=1, stride_axis=0
    )[:, :width]
    if with_memory:
        opened = gate_ref[pl.program_id(0)]
    for first, start, count in spans(q_ref.shape[0], halo):
        rows = slice(first, first + QB)
        query = q_ref[rows]
        scores = nt_dot(query, keys[start : start + count]) * scale + tile[:, width - count :]
        same = docs_col[rows] == docs_row[:, start : start + count]
        scores = jnp.where(same, scores, big_negative)
        raised = jnp.exp(scores - jnp.max(scores, axis=-1, keepdims=True))
        probs = (raised * (1.0 / jnp.sum(raised, axis=-1, keepdims=True))).astype(bf16)
        probs_ref[0, rows, width - count :] = probs
        local = nn_dot(probs, values[start : start + count])
        if with_memory:
            picked = nt_dot(query, mem_k[...]) * scale + mask_ref[0, rows].astype(f32)
            raised = jnp.exp(picked - jnp.max(picked, axis=-1, keepdims=True))
            slot_probs = (raised * (1.0 / jnp.sum(raised, axis=-1, keepdims=True))).astype(bf16)
            slots_ref[0, rows] = slot_probs
            differ = nn_dot(slot_probs, mem_v[...]) - local
            differ_ref[rows] = differ.astype(bf16)
            local = local + opened * differ
        o_ref[rows] = local.astype(bf16)


def backward_kernel(halo, with_memory, scale, *refs):
    refs = list(refs)
    q_ref, k_ref, v_ref, do_ref, probs_ref = refs[:5]
    del refs[:5]
    if halo:
        k_halo, v_halo = refs[:2]
        del refs[:2]
    if with_memory:
        mem_k, mem_v, slots_ref, differ_ref, gate_ref = refs[:5]
        del refs[:5]
    d_ref, table_ref = refs[:2]
    del refs[:2]
    if with_memory:
        gate_grad = refs.pop(0)
    if halo:
        halo_grad = refs.pop(0)
    dk, dv, table = refs[:3]
    del refs[:3]
    if halo:
        keys, values = refs
        keys[:halo] = k_halo[...]
        keys[halo:] = k_ref[...]
        values[:halo] = v_halo[...]
        values[halo:] = v_ref[...]
    else:
        keys, values = k_ref, v_ref
    head = pl.program_id(0)
    heads = pl.num_programs(0)
    row_count, head_dim = q_ref.shape
    width = WIN + QB
    lanes = table.shape[1]
    dk[...] = jnp.zeros_like(dk)
    dv[...] = jnp.zeros_like(dv)
    table[...] = jnp.zeros_like(table)
    if with_memory:
        opened = gate_ref[head]
        gate_sum = jnp.zeros((1, head_dim), f32)
    here = pl.multiple_of(head * head_dim, head_dim)
    for first, start, count in spans(row_count, halo):
        rows = slice(first, first + QB)
        cols = slice(start, start + count)
        upstream = do_ref[rows]
        if with_memory:
            wide = upstream.astype(f32)
            gate_sum += jnp.sum(wide * differ_ref[rows].astype(f32), axis=0, keepdims=True)
            mem_grad = (opened * wide).astype(bf16)
            upstream = ((1.0 - opened) * wide).astype(bf16)
        probs = probs_ref[0, rows, width - count :]
        probs_wide = probs.astype(f32)
        grad = nt_dot(upstream, values[cols])
        inner = jnp.sum(probs_wide * grad, axis=-1, keepdims=True)
        score_wide = probs_wide * (grad - inner)
        score = score_wide.astype(bf16)
        table[:, width - count : width] += score_wide
        dq = nn_dot(score, keys[cols])
        dk[cols] += tn_dot(score, q_ref[rows])
        dv[cols] += tn_dot(probs, upstream)
        if with_memory:
            slot_probs = slots_ref[0, rows].astype(f32)
            slot_grad = nt_dot(mem_grad, mem_v[...])
            slot_score = slot_probs * (
                slot_grad - jnp.sum(slot_probs * slot_grad, axis=-1, keepdims=True)
            )
            dq += nn_dot(slot_score.astype(bf16), mem_k[...])
        d_ref[rows, pl.ds(here, head_dim)] = (dq * scale).astype(bf16)
    key_at = pl.multiple_of((heads + head) * head_dim, head_dim)
    value_at = pl.multiple_of((2 * heads + head) * head_dim, head_dim)
    if halo:
        halo_grad[0] = (dk[:halo] * scale).astype(bf16)
        halo_grad[1] = dv[:halo].astype(bf16)
    d_ref[:, pl.ds(key_at, head_dim)] = (dk[halo:] * scale).astype(bf16)
    d_ref[:, pl.ds(value_at, head_dim)] = dv[halo:].astype(bf16)
    turned = jnp.zeros((8, lanes), f32)
    for row in range(0, QB, 8):
        part = table[row : row + 8]
        turned += pltpu.roll(part, lanes - row, axis=1) if row else part
    total = turned[:1]
    for row in range(1, 8):
        total += pltpu.roll(turned, lanes - row, axis=1)[row : row + 1]
    table_ref[0] = total
    if with_memory:
        gate_grad[0] = gate_sum


def head_block(rows, head_dim, offset):
    return pl.BlockSpec((rows, head_dim), lambda h: (0, offset + h))


def plane_block(rows, cols):
    return pl.BlockSpec((1, rows, cols), lambda h: (h, 0, 0))


smem_block = pl.BlockSpec(memory_space=pltpu.SMEM)


def attend(projected, bias_rows, docs_col, docs_row, halo_rows, memory, scale):
    row_count = projected.shape[0]
    head_count, _, lanes = bias_rows.shape
    head_dim = projected.shape[1] // (3 * head_count)
    halo = 0 if halo_rows is None else halo_rows.shape[1]
    width = WIN + QB
    operands = [bias_rows, docs_col, docs_row, projected, projected, projected]
    specs = [
        plane_block(1, lanes),
        pl.BlockSpec(docs_col.shape, lambda h: (0, 0)),
        pl.BlockSpec(docs_row.shape, lambda h: (0, 0)),
        head_block(row_count, head_dim, 0),
        head_block(row_count, head_dim, head_count),
        head_block(row_count, head_dim, 2 * head_count),
    ]
    scratch = []
    if halo:
        operands += [halo_rows[0], halo_rows[1]]
        specs += [head_block(halo, head_dim, 0)] * 2
        scratch = [pltpu.VMEM((halo + row_count, head_dim), bf16)] * 2
    outs = [
        jax.ShapeDtypeStruct((row_count, head_count * head_dim), bf16),
        jax.ShapeDtypeStruct((head_count, row_count, width), bf16),
    ]
    out_specs = [head_block(row_count, head_dim, 0), plane_block(row_count, width)]
    flops = 4 * head_count * row_count * width * head_dim
    if memory is not None:
        mem_keys, mem_values, mask, gate = memory
        slots = mem_keys.shape[0]
        operands += [mem_keys, mem_values, mask, gate]
        specs += [head_block(slots, head_dim, 0)] * 2 + [plane_block(row_count, slots), smem_block]
        outs += [
            jax.ShapeDtypeStruct((head_count, row_count, slots), bf16),
            jax.ShapeDtypeStruct((row_count, head_count * head_dim), bf16),
        ]
        out_specs += [plane_block(row_count, slots), head_block(row_count, head_dim, 0)]
        flops += 4 * head_count * row_count * slots * head_dim
    return pl.pallas_call(
        functools.partial(forward_kernel, halo, memory is not None, scale),
        out_shape=outs,
        grid=(head_count,),
        in_specs=specs,
        out_specs=out_specs,
        scratch_shapes=scratch,
        compiler_params=pltpu.CompilerParams(vmem_limit_bytes=VMEM_LIMIT),
        cost_estimate=pl.CostEstimate(
            flops=flops, transcendentals=head_count * row_count * width, bytes_accessed=16 * 1024 * 1024
        ),
        name="attend",
    )(*operands)


def attend_back(projected, grad, probs, halo_rows, memory, scale):
    row_count = projected.shape[0]
    head_count, _, width = probs.shape
    head_dim = projected.shape[1] // (3 * head_count)
    halo = 0 if halo_rows is None else halo_rows.shape[1]
    lanes = 1024
    operands = [projected, projected, projected, grad, probs]
    specs = [
        head_block(row_count, head_dim, 0),
        head_block(row_count, head_dim, head_count),
        head_block(row_count, head_dim, 2 * head_count),
        head_block(row_count, head_dim, 0),
        plane_block(row_count, width),
    ]
    scratch = [
        pltpu.VMEM((halo + row_count, head_dim), f32),
        pltpu.VMEM((halo + row_count, head_dim), f32),
        pltpu.VMEM((QB, lanes), f32),
    ]
    if halo:
        operands += [halo_rows[0], halo_rows[1]]
        specs += [head_block(halo, head_dim, 0)] * 2
        scratch += [pltpu.VMEM((halo + row_count, head_dim), bf16)] * 2
    outs = [
        jax.ShapeDtypeStruct(projected.shape, bf16),
        jax.ShapeDtypeStruct((head_count, 1, lanes), f32),
    ]
    out_specs = [pl.BlockSpec(projected.shape, lambda h: (0, 0)), plane_block(1, lanes)]
    flops = 8 * head_count * row_count * width * head_dim
    if memory is not None:
        mem_keys, mem_values, slot_probs, differ, gate = memory
        slots = mem_keys.shape[0]
        operands += [mem_keys, mem_values, slot_probs, differ, gate]
        specs += [head_block(slots, head_dim, 0)] * 2
        specs += [plane_block(row_count, slots), head_block(row_count, head_dim, 0), smem_block]
        outs += [jax.ShapeDtypeStruct((head_count, 1, head_dim), f32)]
        out_specs += [plane_block(1, head_dim)]
        flops += 4 * head_count * row_count * slots * head_dim
    if halo:
        outs += [jax.ShapeDtypeStruct((2, halo, head_count * head_dim), bf16)]
        out_specs += [pl.BlockSpec((2, halo, head_dim), lambda h: (0, 0, h))]
    return pl.pallas_call(
        functools.partial(backward_kernel, halo, memory is not None, scale),
        out_shape=outs,
        grid=(head_count,),
        in_specs=specs,
        out_specs=out_specs,
        scratch_shapes=scratch,
        compiler_params=pltpu.CompilerParams(vmem_limit_bytes=VMEM_LIMIT),
        cost_estimate=pl.CostEstimate(
            flops=flops, transcendentals=0, bytes_accessed=20 * 1024 * 1024
        ),
        name="attend_back",
    )(*operands)


def bucket_of(distance):
    beyond = jnp.sum((distance[..., None] >= jnp.asarray(bucket_edges)).astype(jnp.int32), axis=-1)
    return jnp.where(distance < 16, distance, 16 + beyond)


def distance_onehot(bucket_count):
    bucket = bucket_of(jnp.arange(WIN, dtype=jnp.int32))
    return (bucket[:, None] == jnp.arange(bucket_count, dtype=jnp.int32)).astype(f32)


def normalize(values):
    center = values - jnp.mean(values, axis=-1, keepdims=True)
    factor = lax.rsqrt(jnp.mean(center * center, axis=-1, keepdims=True) + norm_eps)
    return center * factor, factor


def norm_back(upstream, values, gain_row):
    normal, factor = normalize(values)
    gain_part = jnp.sum(upstream * normal, axis=0)
    shift_part = jnp.sum(upstream, axis=0)
    scaled = upstream * gain_row
    inner = (
        scaled
        - jnp.mean(scaled, axis=-1, keepdims=True)
        - normal * jnp.mean(scaled * normal, axis=-1, keepdims=True)
    )
    return factor * inner, gain_part, shift_part


def smooth_pair(pre):
    rate = math.sqrt(2.0 / math.pi)
    square = pre * pre
    turn = jnp.tanh(rate * pre * (1.0 + 0.044715 * square))
    half = 0.5 * (1.0 + turn)
    slope = half + 0.5 * pre * (1.0 - turn * turn) * rate * (1.0 + 3 * 0.044715 * square)
    return (pre * half).astype(bf16), slope.astype(bf16)


def paired_sum(partial):
    low = partial.astype(bf16)
    return low.astype(f32) + core_swap(low).astype(f32)


def on_device(
    tokens,
    doc_ids,
    knn_index,
    mem_keys,
    mem_values,
    qkv_weight,
    out_weight,
    in_weight,
    down_weight,
    norm_gain,
    norm_bias,
    rel_table,
    mem_gate,
    cotangent,
):
    seq_count, block_len, model_width = tokens.shape
    bucket_count, head_total = rel_table.shape[1:]
    head_dim = model_width // head_total
    topk_count = knn_index.shape[3]
    gain_cols = norm_gain.shape[2]
    heads = head_total // CORES
    segments = lax.axis_size("segment")
    batches = lax.axis_size("batch")
    stretches = segments // CORES
    per_seq = segments // seq_count
    pairs = per_seq // CORES
    chunk_len = seq_count * block_len
    pair_len = CORES * chunk_len
    halo = WIN if pairs > 1 else 0
    by_chip = segments == seq_count * CORES and batches == 4
    scale = 1.0 / math.sqrt(head_dim)
    here = lax.axis_index("segment")
    batch = lax.axis_index("batch")
    core = here % CORES
    stretch = here // CORES
    low_core = core == 0
    seq_no = here // per_seq
    block_no = here % seq_count

    def target(source, turn):
        group, place = divmod(source, seq_count)
        return ((place + turn) % seq_count) * per_seq + group

    def to_owner(stored):
        got = []
        for turn in range(seq_count):
            block = lax.dynamic_index_in_dim(stored, (block_no + turn) % seq_count, 0, keepdims=False)
            got.append(permuted(block, "segment", lambda i: target(i, turn)))
        return [pick((seq_no - place) % seq_count, got) for place in range(seq_count)]

    def to_stored(rows):
        blocks = rows.reshape((seq_count, block_len) + rows.shape[1:])
        got = []
        for turn in range(seq_count):
            block = lax.dynamic_index_in_dim(blocks, (seq_no - turn) % seq_count, 0, keepdims=False)
            route = {target(i, turn): i for i in range(segments)}
            got.append(permuted(block, "segment", lambda i: route[i]))
        return jnp.stack([pick((number - block_no) % seq_count, got) for number in range(seq_count)])

    def both_chunks(mine):
        other = core_swap(mine)
        first = jnp.where(low_core, mine, other)
        second = jnp.where(low_core, other, mine)
        return jnp.concatenate([first, second], axis=0)

    def own_chunk(rows):
        return jnp.where(low_core, rows[:chunk_len], rows[chunk_len:])

    norm_rows = jnp.stack([norm_gain[0], norm_bias[0]])
    norm_all = lax.all_gather(norm_rows, ("batch", "segment"), axis=0, tiled=False)
    norm_all = norm_all.reshape(batches, stretches, LAYERS, 2, 2, gain_cols)
    norm_all = jnp.transpose(norm_all, (2, 3, 4, 1, 0, 5)).reshape(LAYERS, 2, 2, model_width)
    norm_all = norm_all.astype(f32)

    hidden = both_chunks(jnp.concatenate(to_owner(tokens), axis=0)).astype(f32)

    shards = (qkv_weight[0], out_weight[0], in_weight[0], down_weight[0])
    if by_chip:
        weights = gather_by_chip(shards, core, stretch, batch)
    else:
        weights = gather_plain(shards, core)

    def by_head(index, which):
        split = index.reshape(chunk_len, heads, CORES, topk_count)[:, :, which]
        return jnp.transpose(split, (1, 0, 2))

    index_rows = jnp.concatenate(to_owner(knn_index), axis=0)
    even, odd = by_head(index_rows, 0), by_head(index_rows, 1)
    own_index = jnp.where(low_core, even, odd)
    other_index = core_swap(jnp.where(low_core, odd, even))
    index = jnp.concatenate(
        [jnp.where(low_core, own_index, other_index), jnp.where(low_core, other_index, own_index)], axis=1
    )
    memory_all = lax.all_gather(jnp.stack([mem_keys, mem_values], axis=0), "segment", axis=1, tiled=True)
    slot_total = memory_all.shape[1]
    memory_split = memory_all.reshape(2, slot_total, heads, CORES, head_dim)
    memory_own = jnp.where(low_core, memory_split[:, :, :, 0], memory_split[:, :, :, 1])
    memory_own = memory_own.reshape(2, slot_total, heads * head_dim)
    mask = slot_mask(index, slot_total)

    upper_cotangent = both_chunks(jnp.concatenate(to_owner(cotangent), axis=0))

    docs = lax.dynamic_index_in_dim(doc_ids, seq_no, 0, keepdims=False)
    first_row = (here % per_seq) // CORES * pair_len
    docs_own = lax.dynamic_slice_in_dim(docs, first_row, pair_len, 0)
    docs_col = docs_own.reshape(pair_len, 1)
    docs_padded = jnp.concatenate([jnp.full((halo,), -1, jnp.int32), docs]) if halo else docs
    docs_row = lax.dynamic_slice_in_dim(docs_padded, first_row, halo + pair_len, 0).reshape(1, -1)
    onehot = distance_onehot(bucket_count)
    tables = rel_table.reshape(LAYERS, bucket_count, heads, CORES)
    tables = jnp.where(low_core, tables[..., 0], tables[..., 1])
    near = jnp.einsum("db,lbh->lhd", onehot, tables, precision=highest)
    lanes = 1024
    bias_rows = jnp.full((LAYERS, heads, 1, lanes), big_negative, f32)
    bias_rows = bias_rows.at[:, :, 0, 1 : WIN + 1].set(near[:, :, ::-1])

    gate_all = jax.nn.sigmoid(mem_gate).reshape(heads, CORES)
    gate = jnp.where(low_core, gate_all[:, 0], gate_all[:, 1])

    def halo_of(projected):
        if not halo:
            return None
        tail = projected[pair_len - halo :, heads * head_dim :]
        route = [(i, i + CORES) for i in range(segments - CORES) if (i // CORES + 1) % pairs != 0]
        got = lax.ppermute(tail, "segment", route)
        return jnp.stack([got[:, : heads * head_dim], got[:, heads * head_dim :]])

    def halo_back(d_projected, halo_grad):
        route = [(i + CORES, i) for i in range(segments - CORES) if (i // CORES + 1) % pairs != 0]
        got = lax.ppermute(jnp.concatenate([halo_grad[0], halo_grad[1]], axis=1), "segment", route)
        edge = d_projected[pair_len - halo :, heads * head_dim :].astype(f32) + got.astype(f32)
        return d_projected.at[pair_len - halo :, heads * head_dim :].set(edge.astype(bf16))

    stored = []
    for layer in range(LAYERS):
        qkv, out, inner, down = weights[layer]
        gains, shifts = norm_all[layer, 0], norm_all[layer, 1]
        normal, _ = normalize(hidden)
        normed = (normal * gains[0] + shifts[0]).astype(bf16)
        projected = nt_dot(normed, qkv).astype(bf16)
        halo_rows = halo_of(projected)
        memory = (memory_own[0], memory_own[1], mask, gate) if layer == 1 else None
        kept = attend(projected, bias_rows[layer], docs_col, docs_row, halo_rows, memory, scale)
        attended, probs = kept[:2]
        after = hidden + paired_sum(nt_dot(attended, out))
        normal, _ = normalize(after)
        normed_two = (normal * gains[1] + shifts[1]).astype(bf16)
        active, slope = smooth_pair(nt_dot(normed_two, inner))
        result = after + paired_sum(nt_dot(active, down))
        stored.append(
            (hidden, normed, projected, halo_rows, attended, probs, kept[2:], after, normed_two, active, slope)
        )
        hidden = result

    mixed = to_stored(own_chunk(hidden.astype(bf16)))

    upstream = upper_cotangent.astype(f32)
    grads = [None, None]
    norm_grads = [None, None]
    table_grads = [None, None]
    for layer in (1, 0):
        qkv, out, inner, down = weights[layer]
        gains = norm_all[layer, 0]
        before, normed, projected, halo_rows, attended, probs, kept, after, normed_two, active, slope = stored[layer]

        def reduced(grad):
            low = grad.astype(bf16)
            return scatter_by_chip(low, stretch, batch) if by_chip else low

        upstream_low = upstream.astype(bf16)
        down_grad = reduced(tn_dot(upstream_low, active))
        pre_grad = (nn_dot(upstream_low, down) * slope.astype(f32)).astype(bf16)
        in_grad = reduced(tn_dot(pre_grad, normed_two))
        term, gain_two, shift_two = norm_back(paired_sum(nn_dot(pre_grad, inner)), after, gains[1])
        after_grad = upstream + term
        after_low = after_grad.astype(bf16)
        out_grad = reduced(tn_dot(after_low, attended))
        attended_grad = nn_dot(after_low, out).astype(bf16)
        memory = (memory_own[0], memory_own[1], kept[0], kept[1], gate) if layer == 1 else None
        backs = attend_back(projected, attended_grad, probs, halo_rows, memory, scale)
        d_projected, distances = backs[:2]
        if layer == 1:
            gate_sums = backs[2]
        if halo:
            d_projected = halo_back(d_projected, backs[-1])
        qkv_grad = reduced(tn_dot(d_projected, normed))
        term, gain_one, shift_one = norm_back(paired_sum(nn_dot(d_projected, qkv)), before, gains[0])
        upstream = after_grad + term
        grads[layer] = (qkv_grad, out_grad, in_grad, down_grad)
        norm_grads[layer] = jnp.stack([jnp.stack([gain_one, gain_two]), jnp.stack([shift_one, shift_two])])
        table_grads[layer] = jnp.einsum(
            "db,hd->bh", onehot, distances[:, 0, 1 : WIN + 1][:, ::-1], precision=highest
        )

    input_grad = to_stored(own_chunk(upstream.astype(bf16)))

    def spread(values):
        empty = jnp.zeros_like(values)
        even = jnp.where(low_core, values, empty)
        odd = jnp.where(low_core, empty, values)
        return jnp.stack([even, odd], axis=-1).reshape(values.shape[:-1] + (head_total,))

    gate_part = jnp.sum(gate_sums[:, 0], axis=-1) * gate * (1.0 - gate)
    sums = lax.psum(
        (
            spread(jnp.stack(table_grads)),
            spread(gate_part),
            jnp.stack(norm_grads) * (1.0 / CORES),
        ),
        ("batch", "segment"),
    )
    table_sum, gate_sum, norm_sum = sums
    norm_sum = norm_sum.reshape(LAYERS, 2, 2, stretches, batches, gain_cols)
    norm_sum = jnp.where(low_core, norm_sum[0], norm_sum[1])
    norm_sum = lax.dynamic_index_in_dim(norm_sum, stretch, 2, keepdims=False)
    norm_sum = lax.dynamic_index_in_dim(norm_sum, batch, 2, keepdims=False)

    matrices = finish_by_chip(grads, core) if by_chip else scatter_plain(grads, core)
    return (mixed, input_grad, *matrices, norm_sum[0][None], norm_sum[1][None], table_sum, gate_sum)


def solution(mesh):
    placed = (
        P("batch", "segment", None),
        P("batch", None),
        P("batch", "segment", None, None),
        P("segment", None),
        P("segment", None),
        P("segment", None, "batch"),
        P("segment", None, "batch"),
        P("segment", None, "batch"),
        P("segment", None, "batch"),
        P("segment", None, "batch"),
        P("segment", None, "batch"),
        P(),
        P(),
        P("batch", "segment", None),
    )
    return jax.shard_map(
        on_device,
        mesh=mesh,
        in_specs=placed,
        out_specs=(
            P("batch", "segment", None),
            P("batch", "segment", None),
            P("segment", None, "batch"),
            P("segment", None, "batch"),
            P("segment", None, "batch"),
            P("segment", None, "batch"),
            P("segment", None, "batch"),
            P("segment", None, "batch"),
            P(),
            P(),
        ),
        check_vma=False,
    )
```

time: 2700 us -> 1040 us (0.39)
  matrix products: 841 us -> 148 us
  other arithmetic: 661 us -> 102 us
  waiting for transfers between devices: 635 us -> 307 us
  local copies, waits for them, and re-layouts: 259 us -> 81.9 us
  Pallas kernels: 0 us -> 84.8 us
  starting transfers between devices: 155 us -> 202 us
    dot_general x256 -> x27, matrix products: 841 us -> 148 us  [the longest x8 59.1 us: nt_dot(): lax.dot_general(left, right, (((1,), (1,)), ((), ())), preferred_element_...]
    reduce_sum x166 -> x6, other arithmetic: 387 us -> 15.6 us  [the longest x4 15.4 us: norm_back(): gain_part = jnp.sum(upstream * normal, axis=0)]
    ppermute x77 -> x151, waiting for transfers between devices: 634 us -> 307 us  [permuted(): return lax.ppermute(block, axis, [(i, route(i)) for i in range(count)])]
    pallas_call x0 -> x5, Pallas kernels: none -> 84.8 us  [the longest x2 29.8 us: attend(): pl.pallas_call(functools.partial(forward_kernel, halo, memory is not None...]
    add x255 -> x11, other arithmetic: 92.2 us -> 12.7 us  [the longest x2 7.58 us: on_device(): after_grad = upstream + term]
    convert_element_type x51 -> x37, other arithmetic: 90.3 us -> 26.6 us  [the longest x16 16.3 us: ring_scatter(): travelling = summed.astype(bf16)]
    unnamed x663 -> x282, local copies, waits for them, and re-layouts: 72.4 us -> 9.6 us
    concatenate x46 -> x1, local copies, waits for them, and re-layouts: 51 us -> 1.64 us  [on_device(): jnp.concatenate([jnp.where(low_core, own_index, other_index), jnp.where(l...]
  transfers between devices with their start and end apart: 85 -> 152, of which waited for: 26 -> 56; matrix products, arithmetic and copies ran while one was open for 49% -> 26% of each run, Pallas kernels for 0% -> 8%
where the time goes in v1:
time: 1040 us; the launch traced here: 1020 us
  waiting for transfers between devices  307 us (30%)
  starting transfers between devices  202 us (19%)
  matrix products  148 us (14%)
  other arithmetic  102 us (10%)
  Pallas kernels  84.8 us (8%)
  local copies, waits for them, and re-layouts  81.9 us (8%)
  blocking collectives  81.9 us (8%)
  between operations  17.9 us (2%)
    ppermute x151, waiting for transfers between devices, permuted(): return lax.ppermute(block, axis, [(i, route(i)) for i in range(count)])  307 us
    ppermute x151, starting transfers between devices, permuted(): return lax.ppermute(block, axis, [(i, route(i)) for i in range(count)])  202 us
    dot_general x8, matrix products, nt_dot(): lax.dot_general(left, right, (((1,), (1,)), ((), ())), preferred_element_...  59.1 us
    dot_general x8, matrix products, nn_dot(): lax.dot_general(left, right, (((1,), (0,)), ((), ())), preferred_element_...  46.7 us
    all_gather x1, blocking collectives, on_device(): lax.all_gather(norm_rows, ('batch', 'segment'), axis=0, tiled=False)  42.5 us
    dot_general x8, matrix products, tn_dot(): lax.dot_general(left, right, (((0,), (0,)), ((), ())), preferred_element_...  41.3 us
    psum x1, blocking collectives, on_device(): lax.psum((spread(jnp.stack(table_grads)), spread(gate_part), jnp.stack(no...  39.4 us
    pallas_call x2, Pallas kernels, attend(): pl.pallas_call(functools.partial(forward_kernel, halo, memory is not None...  29.8 us
  transfers between devices with their start and end apart: 152, of which 56 were waited for; matrix products, arithmetic and copies ran while one was open for 26% of the time, Pallas kernels for 8%

profile of v1, /device:TPU:1, one launch (start us, length us, event | category | flops | bytes accessed | tf_op | source)
XLA Modules:
  0.0 1024.8 jit_solution(11807722995511473354)
XLA Ops:
  28.0 42.5 %all-gather = bf16[64,2,64]{2,1,0:T(2,128)(2,1)S(1)} all-gather(bf16[2,2,64]{2,1,0:T(2,128)(2,1)S(1)} %pad_maximum_fusion.40), channel_id=2, replica_groups=mesh['batch'=4,'segment'=8] {'batch','segment'}, dimensions={0}, use_global_device_ids=true | all-gather | bytes 16896 | tf_op jit(solution)/shard_map/all_gather | solution.py:641
  135.0 11.8 %collective-permute-done = bf16[128,1024]{1,0:T(8,128)(2,1)S(1)} collective-permute-done((bf16[128,1024]{1,0:T(8,128)(2,1)}, bf16[128,1024]{1,0:T(8,128)(2,1)S(1)}, u32[]{:S(2)}, u32[]{:S(2)}) %collective-permute-start) | collective-permute-done | bytes 262176 | tf_op jit(solution)/shard_map/ppermute | solution.py:28
  159.8 26.4 %slot_mask.1.refs_8_ = bf16[4,1024,256]{2,1,0:T(8,128)(2,1)S(1)} custom-call(s32[4,1024,32]{2,1,0:T(8,128)S(1)} %copy.77.index_ref), custom_call_target="tpu_custom_call" | custom-call | flops 67108864 | bytes 4194304 | tf_op jit(solution)/shard_map/slot_mask/pallas_call | solution.py:248
  224.4 10.6 %collective-permute-done.24 = bf16[512,256]{1,0:T(8,128)(2,1)S(1)} collective-permute-done((bf16[512,256]{1,0:T(8,128)(2,1)S(1)}, bf16[512,256]{1,0:T(8,128)(2,1)S(1)}, u32[]{:S(2)}, u32[]{:S(2)}) %collective-permute-start.24) | collective-permute-done | bytes 262176 | tf_op jit(solution)/shard_map/ppermute | solution.py:28
  246.5 9.5 collective-permute-done.25
  265.7 8.9 collective-permute-done.9
  280.7 24.7 %collective-permute-done.11 = bf16[192,1024]{1,0:T(8,128)(2,1)S(1)} collective-permute-done((bf16[192,1024]{1,0:T(8,128)(2,1)S(1)}, bf16[192,1024]{1,0:T(8,128)(2,1)S(1)}, u32[]{:S(2)}, u32[]{:S(2)}) %collective-permute-start.11) | collective-permute-done | bytes 393248 | tf_op jit(solution)/shard_map/ppermute | solution.py:28
  312.7 11.8 %attend.2 = (bf16[1024,512]{1,0:T(8,128)(2,1)S(1)}, bf16[4,1024,768]{2,1,0:T(8,128)(2,1)}) custom-call(f32[4,1,1024]{2,1,0:T(1,128)S(1)} %get-tuple-element.302.refs_0_, s32[1024,1]{1,0:T(8,128)S(1)} %copy.71.refs_1_, s32[1,1024]{1,0:T(1,128)S(1)} %constant_dynamic-slice_fusion.34.refs_2_, ...), custom_call_target="tpu_custom_call" | custom-call | flops 1610612736 | bytes 16777216 | tf_op jit(solution)/shard_map/attend/pallas_call | solution.py:457
  343.6 7.8 collective-permute-done.27
  352.1 14.1 %collective-permute-done.28 = bf16[256,1024]{1,0:T(8,128)(2,1)S(1)} collective-permute-done((bf16[256,1024]{1,0:T(8,128)(2,1)S(1)}, bf16[256,1024]{1,0:T(8,128)(2,1)S(1)}, u32[]{:S(2)}, u32[]{:S(2)}) %collective-permute-start.28) | collective-permute-done | bytes 524320 | tf_op jit(solution)/shard_map/ppermute | solution.py:28
  384.8 15.3 %fusion.52 = f32[1024,2048]{1,0:T(8,128)} fusion(bf16[2048,1024]{1,0:T(8,128)(2,1)S(1)} %constant_dynamic-update-slice_fusion.25, f32[1024,1024]{1,0:T(8,128)S(1)} %get-tuple-element.120, f32[1024]{0:T(1024)S(1)} %bitcast.294, f32[1024]{0:T(1024)S(1)} %bitcast.271, f32[1024]{0:T(1024)S(1)} %add_rsqrt_fusion.2, f32[1024]{0:T(1024)S(1)} %broadcast_multiply_fusion.10), kind=kOutput, calls=%fused_computation.438 | convolution fusion | flops 4300210176 | bytes 16793600 | tf_op jit(solution)/shard_map/dot_general | solution.py:263
  400.2 9.8 convolution_convert_fusion.14
  439.3 8.1 convolution_convert_fusion.2.refs_3_.refs_4_.refs_5_.refs_0_.refs_1_.refs_2_
  447.4 18.1 %attend.3 = (bf16[1024,512]{1,0:T(8,128)(2,1)S(1)}, bf16[4,1024,768]{2,1,0:T(8,128)(2,1)}, bf16[4,1024,256]{2,1,0:T(8,128)(2,1)S(1)}, bf16[1024,512]{1,0:T(8,128)(2,1)S(1)}) custom-call(f32[4,1,1024]{2,1,0:T(1,128)S(1)} %get-tuple-element.301.refs_0_, s32[1024,1]{1,0:T(8,128)S(1)} %copy.71.refs_1_, s32[1,1024]{1,0:T(1,128)S(1)} %constant_dynamic-slice_fusion.34.refs_2_, ...), custom_call_target="tpu_custom_call" | custom-call | flops 2147483648 | bytes 16777216 | tf_op jit(solution)/shard_map/attend/pallas_call | solution.py:457
  487.9 11.1 %collective-permute-done.71 = bf16[128,2048]{1,0:T(8,128)(2,1)S(1)} collective-permute-done((bf16[128,2048]{1,0:T(8,128)(2,1)S(1)}, bf16[128,2048]{1,0:T(8,128)(2,1)S(1)}, u32[]{:S(2)}, u32[]{:S(2)}) %collective-permute-start.71) | collective-permute-done | bytes 524320 | tf_op jit(solution)/shard_map/ppermute | solution.py:28
  514.8 9.8 multiply_convert_fusion.1
  545.1 7.5 collective-permute-done.143
  555.4 11.0 %convolution_convert_fusion.12 = bf16[1024,1024]{1,0:T(8,128)(2,1)} fusion(bf16[1024,2048]{1,0:T(8,128)(2,1)} %constant_dynamic-update-slice_fusion, f32[1024,2048]{1,0:T(8,128)} %copy-done.134), kind=kOutput, calls=%fused_computation.83 | convolution fusion | flops 4314890240 | bytes 14680064 | tf_op jit(solution)/shard_map/dot_general | solution.py:263
  566.4 8.7 collective-permute-done.131
  582.6 15.0 %collective-permute-done.146 = bf16[256,2048]{1,0:T(8,128)(2,1)S(1)} collective-permute-done((bf16[256,2048]{1,0:T(8,128)(2,1)S(1)}, bf16[256,2048]{1,0:T(8,128)(2,1)S(1)}, u32[]{:S(2)}, u32[]{:S(2)}) %collective-permute-start.146) | collective-permute-done | bytes 1048608 | tf_op jit(solution)/shard_map/ppermute | solution.py:28
  624.6 16.5 %attend_back.2 = (bf16[1024,1536]{1,0:T(8,128)(2,1)}, f32[4,1,1024]{2,1,0:T(1,128)S(1)}, f32[4,1,128]{2,1,0:T(1,128)S(1)}) custom-call(bf16[1024,1536]{1,0:T(8,128)(2,1)} %convolution_convert_fusion.2.refs_3_.refs_4_.refs_5_.refs_0_.refs_1_.refs_2_, bf16[1024,1536]{1,0:T(8,128)(2,1)} %convolution_convert_fusion.2.refs_3_.refs_4_.refs_5_.refs_0_.refs_1_.refs_2_, ...), custom_call_target="tpu_custom_call" | custom-call | flops 3758096384 | bytes 20971520 | tf_op jit(solution)/shard_map/attend_back/pallas_call | solution.py:513
  641.1 7.7 convolution_convert_fusion.10
  678.1 7.8 collective-permute-done.98
  699.3 16.3 %collective-permute-done.101 = bf16[384,1024]{1,0:T(8,128)(2,1)S(1)} collective-permute-done((bf16[384,1024]{1,0:T(8,128)(2,1)S(1)}, bf16[384,1024]{1,0:T(8,128)(2,1)S(1)}, u32[]{:S(2)}, u32[]{:S(2)}) %collective-permute-start.101) | collective-permute-done | bytes 786464 | tf_op jit(solution)/shard_map/ppermute | solution.py:28
  736.4 9.3 multiply_convert_fusion
  745.7 7.4 convolution_convert_fusion.7
  754.9 8.1 convolution_convert_fusion.5
  783.9 10.1 collective-permute-start.85
  798.2 20.9 %collective-permute-done.139 = bf16[256,2048]{1,0:T(8,128)(2,1)S(1)} collective-permute-done((bf16[256,2048]{1,0:T(8,128)(2,1)S(1)}, bf16[256,2048]{1,0:T(8,128)(2,1)S(1)}, u32[]{:S(2)}, u32[]{:S(2)}) %collective-permute-start.139) | collective-permute-done | bytes 1048608 | tf_op jit(solution)/shard_map/ppermute | solution.py:28
  839.4 12.0 %attend_back.3 = (bf16[1024,1536]{1,0:T(8,128)(2,1)S(1)}, f32[4,1,1024]{2,1,0:T(1,128)S(1)}) custom-call(bf16[1024,1536]{1,0:T(8,128)(2,1)} %copy-done.2, bf16[1024,1536]{1,0:T(8,128)(2,1)} %copy-done.2, bf16[1024,1536]{1,0:T(8,128)(2,1)} %copy-done.2, bf16[1024,512]{1,0:T(8,128)(2,1)S(1)} %convolution_convert_fusion.18.refs_3_, ...), custom_call_target="tpu_custom_call" | custom-call | flops 3221225472 | bytes 20971520 | tf_op jit(solution)/shard_map/attend_back/pallas_call | solution.py:513
  884.8 12.4 %collective-permute-start.135 = (bf16[512,256]{1,0:T(8,128)(2,1)S(1)}, bf16[512,256]{1,0:T(8,128)(2,1)S(1)}, u32[]{:S(2)}, u32[]{:S(2)}) collective-permute-start(bf16[512,256]{1,0:T(8,128)(2,1)S(1)} %get-tuple-element.106), channel_id=1, source_target_pairs={{0,1},{1,0},{2,3},{3,2},{4,5},{5,4},{6,7},{7,6},{8,9},{9,8},{10,11... | collective-permute-start | bytes 786440 | tf_op jit(solution)/shard_map/ppermute | solution.py:28
  976.1 39.4 %all-reduce = (f32[2,2,2,1024]{3,2,1,0:T(2,128)S(1)}, f32[2,32,8]{1,2,0:T(8,128)}, f32[8]{0:T(128)}) all-reduce(f32[2,2,2,1024]{3,2,1,0:T(2,128)S(1)} %maximum_multiply_fusion, f32[2,32,8]{1,2,0:T(8,128)S(1)} %bitcast.281, f32[8]{0:T(128)S(1)} %copy-done.128), channel_id=1, replica_groups=mesh['batch'=4,'segment'=8] {'batch','segment'}, use_global_device_ids=true, to_apply=%region_25.26 | all-reduce | flops 8712 | bytes 69696 | tf_op jit(solution)/shard_map/psum | solution.py:775
  (854 shorter events, 556.5 us)
Async XLA Ops:
  7.3 414.4 %all-gather.3.cloned.1.call-start = ((), (), s32[]{:S(2)}) async-start(), calls=%async_computation | async-start | bytes 1179648 | tf_op jit(solution)/shard_map/all_gather | solution.py:665
  8.9 71.3 %collective-permute-start.13 = (bf16[256,128]{0,1:T(8,128)(2,1)}, bf16[256,128]{0,1:T(8,128)(2,1)S(1)}, u32[]{:S(2)}, u32[]{:S(2)}) collective-permute-start(bf16[256,128]{0,1:T(8,128)(2,1)} %select_bitcast_fusion.11), channel_id=1, source_target_pairs={{0,1},{1,0},{2,3},{3,2},{4,5},{5,4},{6,7},{7,6},{8,9},{9,8},{10,11... | collective-permute-start | bytes 196616 | tf_op jit(solution)/shard_map/ppermute | solution.py:28
  13.6 90.7 %collective-permute-start.5 = (bf16[384,256]{1,0:T(8,128)(2,1)}, bf16[384,256]{1,0:T(8,128)(2,1)S(1)}, u32[]{:S(2)}, u32[]{:S(2)}) collective-permute-start(bf16[384,256]{1,0:T(8,128)(2,1)} %bitcast.17), channel_id=1, source_target_pairs={{0,1},{1,0},{2,3},{3,2},{4,5},{5,4},{6,7},{7,6},{8,9},{9,8},{10,11... | collective-permute-start | bytes 589832 | tf_op jit(solution)/shard_map/ppermute | solution.py:28
  14.9 65.4 %collective-permute-start.47 = (s32[128,8,32]{0,2,1:T(8,128)}, s32[128,8,32]{0,2,1:T(8,128)}, u32[]{:S(2)}, u32[]{:S(2)}) collective-permute-start(s32[128,8,32]{0,2,1:T(8,128)} %get-tuple-element.261), channel_id=1, source_target_pairs={{0,2},{1,4},{2,6},{3,0},{4,3},{5,5},{6,7},{7,1},{8,10},{9,12},{10,... | collective-permute-start | bytes 393224 | tf_op jit(solution)/shard_map/ppermute | solution.py:28
  20.5 61.7 %collective-permute-start.46 = (s32[128,8,32]{0,2,1:T(8,128)}, s32[128,8,32]{0,2,1:T(8,128)}, u32[]{:S(2)}, u32[]{:S(2)}) collective-permute-start(s32[128,8,32]{0,2,1:T(8,128)} %get-tuple-element.262), channel_id=1, source_target_pairs={{0,0},{1,2},{2,4},{3,6},{4,1},{5,3},{6,5},{7,7},{8,8},{9,10},{10,1... | collective-permute-start | bytes 393224 | tf_op jit(solution)/shard_map/ppermute | solution.py:28
  24.0 64.2 %collective-permute-start.49 = (s32[128,8,32]{0,2,1:T(8,128)}, s32[128,8,32]{0,2,1:T(8,128)}, u32[]{:S(2)}, u32[]{:S(2)}) collective-permute-start(s32[128,8,32]{0,2,1:T(8,128)} %get-tuple-element.263), channel_id=1, source_target_pairs={{0,6},{1,0},{2,2},{3,4},{4,7},{5,1},{6,3},{7,5},{8,14},{9,8},{10,1... | collective-permute-start | bytes 393224 | tf_op jit(solution)/shard_map/ppermute | solution.py:28
  82.3 42.5 %collective-permute-start.78 = (bf16[128,1024]{1,0:T(8,128)(2,1)}, bf16[128,1024]{1,0:T(8,128)(2,1)S(1)}, u32[]{:S(2)}, u32[]{:S(2)}) collective-permute-start(bf16[128,1024]{1,0:T(8,128)(2,1)} %get-tuple-element.192), channel_id=1, source_target_pairs={{0,0},{1,2},{2,4},{3,6},{4,1},{5,3},{6,5},{7,7},{8,8},{9,10},{10,1... | collective-permute-start | bytes 786440 | tf_op jit(solution)/shard_map/ppermute | solution.py:28
  209.9 101.1 %collective-permute-start.66 = (bf16[256,512]{1,0:T(8,128)(2,1)S(1)}, bf16[256,512]{1,0:T(8,128)(2,1)S(1)}, u32[]{:S(2)}, u32[]{:S(2)}) collective-permute-start(bf16[256,512]{1,0:T(8,128)(2,1)S(1)} %copy-done.80), channel_id=1, source_target_pairs={{0,2},{1,3},{2,4},{3,5},{4,6},{5,7},{6,0},{7,1},{8,10},{9,11},{10,... | collective-permute-start | bytes 786440 | tf_op jit(solution)/shard_map/ppermute | solution.py:28
  234.9 89.5 %collective-permute-start.60 = (bf16[512,256]{1,0:T(8,128)(2,1)}, bf16[512,256]{1,0:T(8,128)(2,1)}, u32[]{:S(2)}, u32[]{:S(2)}) collective-permute-start(bf16[512,256]{1,0:T(8,128)(2,1)} %collective-permute-done.59), channel_id=1, source_target_pairs={{0,2},{1,3},{2,4},{3,5},{4,6},{5,7},{6,0},{7,1},{8,10},{9,11},{10,... | collective-permute-start | bytes 786440 | tf_op jit(solution)/shard_map/ppermute | solution.py:28
  263.7 87.8 %collective-permute-start.34 = (bf16[256,2048]{1,0:T(8,128)(2,1)}, bf16[256,2048]{1,0:T(8,128)(2,1)S(1)}, u32[]{:S(2)}, u32[]{:S(2)}) collective-permute-start(bf16[256,2048]{1,0:T(8,128)(2,1)} %get-tuple-element.223), channel_id=1, source_target_pairs={{0,8},{8,0},{16,24},{24,16},{1,9},{9,1},{17,25},{25,17},{2,10},{10... | collective-permute-start | bytes 3145736 | tf_op jit(solution)/shard_map/ppermute | solution.py:28
  331.8 47.0 %collective-permute-start.21 = (bf16[1024,1024]{1,0:T(8,128)(2,1)S(1)}, bf16[1024,1024]{1,0:T(8,128)(2,1)S(1)}, u32[]{:S(2)}, u32[]{:S(2)}) collective-permute-start(bf16[1024,1024]{1,0:T(8,128)(2,1)S(1)} %convolution_convert_fusion.15), channel_id=1, source_target_pairs={{0,1},{1,0},{2,3},{3,2},{4,5},{5,4},{6,7},{7,6},{8,9},{9,8},{10,11... | collective-permute-start | bytes 6291464 | tf_op jit(solution)/shard_map/ppermute | solution.py:28
  367.2 100.9 %collective-permute-start.82 = (bf16[512,1024]{1,0:T(8,128)(2,1)}, bf16[512,1024]{1,0:T(8,128)(2,1)S(1)}, u32[]{:S(2)}, u32[]{:S(2)}) collective-permute-start(bf16[512,1024]{1,0:T(8,128)(2,1)} %pad_maximum_fusion.8), channel_id=1, source_target_pairs={{0,1},{1,0},{2,3},{3,2},{4,5},{5,4},{6,7},{7,6},{8,9},{9,8},{10,11... | collective-permute-start | bytes 3145736 | tf_op jit(solution)/shard_map/ppermute | solution.py:28
  370.6 47.0 %collective-permute-start.42 = (bf16[384,1024]{1,0:T(8,128)(2,1)}, bf16[384,1024]{1,0:T(8,128)(2,1)S(1)}, u32[]{:S(2)}, u32[]{:S(2)}) collective-permute-start(bf16[384,1024]{1,0:T(8,128)(2,1)} %get-tuple-element.245), channel_id=1, source_target_pairs={{0,8},{8,0},{16,24},{24,16},{1,9},{9,1},{17,25},{25,17},{2,10},{10... | collective-permute-start | bytes 2359304 | tf_op jit(solution)/shard_map/ppermute | solution.py:28
  378.8 93.2 %collective-permute-start.62 = (bf16[512,1024]{1,0:T(8,128)(2,1)}, bf16[512,1024]{1,0:T(8,128)(2,1)}, u32[]{:S(2)}, u32[]{:S(2)}) collective-permute-start(bf16[512,1024]{1,0:T(8,128)(2,1)} %get-tuple-element.203), channel_id=1, source_target_pairs={{0,8},{8,0},{16,24},{24,16},{1,9},{9,1},{17,25},{25,17},{2,10},{10... | collective-permute-start | bytes 3145736 | tf_op jit(solution)/shard_map/ppermute | solution.py:28
  430.4 43.9 %collective-permute-start.63 = (bf16[512,1024]{1,0:T(8,128)(2,1)}, bf16[512,1024]{1,0:T(8,128)(2,1)}, u32[]{:S(2)}, u32[]{:S(2)}) collective-permute-start(bf16[512,1024]{1,0:T(8,128)(2,1)} %get-tuple-element.203), channel_id=1, source_target_pairs={{0,16},{8,24},{16,0},{24,8},{1,17},{9,25},{17,1},{25,9},{2,18},{10... | collective-permute-start | bytes 3145736 | tf_op jit(solution)/shard_map/ppermute | solution.py:28
  433.1 43.9 %collective-permute-start.69 = (bf16[256,2048]{1,0:T(8,128)(2,1)}, bf16[256,2048]{1,0:T(8,128)(2,1)}, u32[]{:S(2)}, u32[]{:S(2)}) collective-permute-start(bf16[256,2048]{1,0:T(8,128)(2,1)} %get-tuple-element.209), channel_id=1, source_target_pairs={{0,8},{8,0},{16,24},{24,16},{1,9},{9,1},{17,25},{25,17},{2,10},{10... | collective-permute-start | bytes 3145736 | tf_op jit(solution)/shard_map/ppermute | solution.py:28
  434.9 43.8 %collective-permute-start.70 = (bf16[256,2048]{1,0:T(8,128)(2,1)}, bf16[256,2048]{1,0:T(8,128)(2,1)}, u32[]{:S(2)}, u32[]{:S(2)}) collective-permute-start(bf16[256,2048]{1,0:T(8,128)(2,1)} %get-tuple-element.209), channel_id=1, source_target_pairs={{0,16},{8,24},{16,0},{24,8},{1,17},{9,25},{17,1},{25,9},{2,18},{10... | collective-permute-start | bytes 3145736 | tf_op jit(solution)/shard_map/ppermute | solution.py:28
  539.3 71.2 %collective-permute-start.83 = (bf16[1024,1024]{1,0:T(8,128)(2,1)}, bf16[1024,1024]{1,0:T(8,128)(2,1)}, u32[]{:S(2)}, u32[]{:S(2)}) collective-permute-start(bf16[1024,1024]{1,0:T(8,128)(2,1)} %convolution_convert_fusion.11), channel_id=1, source_target_pairs={{0,1},{1,0},{2,3},{3,2},{4,5},{5,4},{6,7},{7,6},{8,9},{9,8},{10,11... | collective-permute-start | bytes 6291464 | tf_op jit(solution)/shard_map/ppermute | solution.py:28
  554.3 43.3 %collective-permute-start.146 = (bf16[256,2048]{1,0:T(8,128)(2,1)S(1)}, bf16[256,2048]{1,0:T(8,128)(2,1)S(1)}, u32[]{:S(2)}, u32[]{:S(2)}) collective-permute-start(bf16[256,2048]{1,0:T(8,128)(2,1)S(1)} %pad_maximum_fusion.18), channel_id=1, source_target_pairs={{0,8},{8,0},{16,24},{24,16},{1,9},{9,1},{17,25},{25,17},{2,10},{10... | collective-permute-start | bytes 3145736 | tf_op jit(solution)/shard_map/ppermute | solution.py:28
  554.8 44.0 %collective-permute-start.144 = (bf16[256,2048]{1,0:T(8,128)(2,1)S(1)}, bf16[256,2048]{1,0:T(8,128)(2,1)S(1)}, u32[]{:S(2)}, u32[]{:S(2)}) collective-permute-start(bf16[256,2048]{1,0:T(8,128)(2,1)S(1)} %pad_maximum_fusion.17), channel_id=1, source_target_pairs={{0,16},{8,24},{16,0},{24,8},{1,17},{9,25},{17,1},{25,9},{2,18},{10... | collective-permute-start | bytes 3145736 | tf_op jit(solution)/shard_map/ppermute | solution.py:28
  604.0 67.8 %collective-permute-start.133 = (bf16[512,256]{1,0:T(8,128)(2,1)}, bf16[512,256]{1,0:T(8,128)(2,1)S(1)}, u32[]{:S(2)}, u32[]{:S(2)}) collective-permute-start(bf16[512,256]{1,0:T(8,128)(2,1)} %add_convert_fusion.23), channel_id=1, source_target_pairs={{0,2},{1,3},{2,4},{3,5},{4,6},{5,7},{6,0},{7,1},{8,10},{9,11},{10,... | collective-permute-start | bytes 786440 | tf_op jit(solution)/shard_map/ppermute | solution.py:28
  610.5 62.5 %collective-permute-start.148 = (bf16[256,512]{1,0:T(8,128)(2,1)}, bf16[256,512]{1,0:T(8,128)(2,1)}, u32[]{:S(2)}, u32[]{:S(2)}) collective-permute-start(bf16[256,512]{1,0:T(8,128)(2,1)} %add_convert_fusion.19), channel_id=1, source_target_pairs={{0,2},{1,3},{2,4},{3,5},{4,6},{5,7},{6,0},{7,1},{8,10},{9,11},{10,... | collective-permute-start | bytes 786440 | tf_op jit(solution)/shard_map/ppermute | solution.py:28
  775.5 43.6 %collective-permute-start.139 = (bf16[256,2048]{1,0:T(8,128)(2,1)S(1)}, bf16[256,2048]{1,0:T(8,128)(2,1)S(1)}, u32[]{:S(2)}, u32[]{:S(2)}) collective-permute-start(bf16[256,2048]{1,0:T(8,128)(2,1)S(1)} %pad_maximum_fusion.16), channel_id=1, source_target_pairs={{0,8},{8,0},{16,24},{24,16},{1,9},{9,1},{17,25},{25,17},{2,10},{10... | collective-permute-start | bytes 3145736 | tf_op jit(solution)/shard_map/ppermute | solution.py:28
  776.1 43.9 %collective-permute-start.137 = (bf16[256,2048]{1,0:T(8,128)(2,1)S(1)}, bf16[256,2048]{1,0:T(8,128)(2,1)S(1)}, u32[]{:S(2)}, u32[]{:S(2)}) collective-permute-start(bf16[256,2048]{1,0:T(8,128)(2,1)S(1)} %pad_maximum_fusion.15), channel_id=1, source_target_pairs={{0,16},{8,24},{16,0},{24,8},{1,17},{9,25},{17,1},{25,9},{2,18},{10... | collective-permute-start | bytes 3145736 | tf_op jit(solution)/shard_map/ppermute | solution.py:28
  783.9 46.7 %collective-permute-start.85 = (bf16[1024,1024]{1,0:T(8,128)(2,1)S(1)}, bf16[1024,1024]{1,0:T(8,128)(2,1)S(1)}, u32[]{:S(2)}, u32[]{:S(2)}) collective-permute-start(bf16[1024,1024]{1,0:T(8,128)(2,1)S(1)} %convolution_convert_fusion.9), channel_id=1, source_target_pairs={{0,1},{1,0},{2,3},{3,2},{4,5},{5,4},{6,7},{7,6},{8,9},{9,8},{10,11... | collective-permute-start | bytes 6291464 | tf_op jit(solution)/shard_map/ppermute | solution.py:28
  796.7 77.1 %collective-permute-start.134 = (bf16[512,256]{1,0:T(8,128)(2,1)}, bf16[512,256]{1,0:T(8,128)(2,1)}, u32[]{:S(2)}, u32[]{:S(2)}) collective-permute-start(bf16[512,256]{1,0:T(8,128)(2,1)} %add_convert_fusion.22), channel_id=1, source_target_pairs={{0,2},{1,3},{2,4},{3,5},{4,6},{5,7},{6,0},{7,1},{8,10},{9,11},{10,... | collective-permute-start | bytes 786440 | tf_op jit(solution)/shard_map/ppermute | solution.py:28
  797.5 107.4 %collective-permute-start.149 = (bf16[256,512]{1,0:T(8,128)(2,1)}, bf16[256,512]{1,0:T(8,128)(2,1)S(1)}, u32[]{:S(2)}, u32[]{:S(2)}) collective-permute-start(bf16[256,512]{1,0:T(8,128)(2,1)} %add_convert_fusion.18), channel_id=1, source_target_pairs={{0,2},{1,3},{2,4},{3,5},{4,6},{5,7},{6,0},{7,1},{8,10},{9,11},{10,... | collective-permute-start | bytes 786440 | tf_op jit(solution)/shard_map/ppermute | solution.py:28
  826.2 114.5 %collective-permute-start.119 = (bf16[256,128]{0,1:T(8,128)(2,1)}, bf16[256,128]{0,1:T(8,128)(2,1)}, u32[]{:S(2)}, u32[]{:S(2)}) collective-permute-start(bf16[256,128]{0,1:T(8,128)(2,1)} %add_convert_fusion.34), channel_id=1, source_target_pairs={{0,2},{1,3},{2,4},{3,5},{4,6},{5,7},{6,0},{7,1},{8,10},{9,11},{10,... | collective-permute-start | bytes 196616 | tf_op jit(solution)/shard_map/ppermute | solution.py:28
  910.7 46.0 %collective-permute-start.86 = (bf16[1024,1024]{1,0:T(8,128)(2,1)}, bf16[1024,1024]{1,0:T(8,128)(2,1)}, u32[]{:S(2)}, u32[]{:S(2)}) collective-permute-start(bf16[1024,1024]{1,0:T(8,128)(2,1)} %convolution_convert_fusion.8), channel_id=1, source_target_pairs={{0,1},{1,0},{2,3},{3,2},{4,5},{5,4},{6,7},{7,6},{8,9},{9,8},{10,11... | collective-permute-start | bytes 6291464 | tf_op jit(solution)/shard_map/ppermute | solution.py:28
  966.4 49.8 %collective-permute-start.88 = (bf16[128,1024]{1,0:T(8,128)(2,1)S(1)}, bf16[128,1024]{1,0:T(8,128)(2,1)S(1)}, u32[]{:S(2)}, u32[]{:S(2)}) collective-permute-start(bf16[128,1024]{1,0:T(8,128)(2,1)S(1)} %get-tuple-element.183), channel_id=1, source_target_pairs={{0,3},{1,7},{2,0},{3,4},{4,1},{5,5},{6,2},{7,6},{8,11},{9,15},{10,... | collective-permute-start | bytes 786440 | tf_op jit(solution)/shard_map/ppermute | solution.py:28
  968.9 47.3 %collective-permute-start.90 = (bf16[128,1024]{1,0:T(8,128)(2,1)S(1)}, bf16[128,1024]{1,0:T(8,128)(2,1)S(1)}, u32[]{:S(2)}, u32[]{:S(2)}) collective-permute-start(bf16[128,1024]{1,0:T(8,128)(2,1)S(1)} %get-tuple-element.184), channel_id=1, source_target_pairs={{0,1},{1,5},{2,2},{3,6},{4,3},{5,7},{6,0},{7,4},{8,9},{9,13},{10,1... | collective-permute-start | bytes 786440 | tf_op jit(solution)/shard_map/ppermute | solution.py:28
  970.8 45.4 %collective-permute-start.89 = (bf16[128,1024]{1,0:T(8,128)(2,1)S(1)}, bf16[128,1024]{1,0:T(8,128)(2,1)S(1)}, u32[]{:S(2)}, u32[]{:S(2)}) collective-permute-start(bf16[128,1024]{1,0:T(8,128)(2,1)S(1)} %get-tuple-element.185), channel_id=1, source_target_pairs={{0,2},{1,6},{2,3},{3,7},{4,0},{5,4},{6,1},{7,5},{8,10},{9,14},{10,... | collective-permute-start | bytes 786440 | tf_op jit(solution)/shard_map/ppermute | solution.py:28
  (257 other events, 5547.6 us)
Sparse Core Ops, SparseCore 0:
  10.7 29.8 all-gather.2

commit v2 on v1

v2 whole, which is shorter than its diff:
```python
import functools
import math

import jax
import jax.numpy as jnp
import numpy as np
from jax import lax
from jax.experimental import pallas as pl
from jax.experimental.pallas import tpu as pltpu
from jax.sharding import PartitionSpec as P

SEG, BAT = "segment", "batch"
WIN = 512
LAYERS = 2
CORES = 2
QB = 256

norm_eps = 1e-05
big_negative = -1e30
bucket_edges = np.ceil(16.0 * 8.0 ** (np.arange(1, 16) / 16.0)).astype(np.int32)
highest = lax.Precision.HIGHEST
f32 = jnp.float32
bf16 = jnp.bfloat16
VMEM_LIMIT = 20 * 1024 * 1024


def permuted(block, axis, route):
    count = lax.axis_size(axis)
    return lax.ppermute(block, axis, [(i, route(i)) for i in range(count)])


def core_swap(block):
    return permuted(block, SEG, lambda i: i ^ 1)


def room(tick):
    return pl.pallas_call(
        lambda source, result: None,
        out_shape=jax.ShapeDtypeStruct(tick.shape, tick.dtype),
        in_specs=[pl.BlockSpec(memory_space=pl.ANY)],
        out_specs=pl.BlockSpec(memory_space=pl.ANY),
        input_output_aliases={0: 0},
        cost_estimate=pl.CostEstimate(flops=200_000_000_000, transcendentals=0, bytes_accessed=0),
        name="room",
    )(tick)


def key(*parts):
    return "".join(map(str, parts))


class Steps:
    def __init__(self):
        self.steps = {}
        self.values = {}
        self.mark = ()
        self.tick = jnp.zeros((8, 128), f32)

    def given(self, name, value):
        self.values[name] = value
        return name

    def run(self, name, step, *sources):
        assert name not in self.steps, name
        self.steps[name] = ("run", step, sources)
        return name

    def send(self, name, link, transfer, *sources):
        assert name not in self.steps, name
        self.steps[name] = (link, transfer, sources)
        return name

    def value(self, source):
        if isinstance(source, tuple):
            return self.values[source[0]][source[1]]
        return self.values[source]

    def behind(self, values):
        leaves, tree = jax.tree.flatten(values)
        held = lax.optimization_barrier(tuple(leaves) + tuple(self.mark))
        return jax.tree.unflatten(tree, held[: len(leaves)])

    def wait(self, name):
        tick = room(self.behind(self.tick))
        leaves, tree = jax.tree.flatten(self.values[name])
        held = lax.optimization_barrier(tuple(leaves) + tuple(self.mark) + (tick,))
        self.tick = held[-1]
        self.mark = held[: len(leaves)]
        self.values[name] = jax.tree.unflatten(tree, self.mark)

    def carry_out(self, order):
        waited = set()
        names = list(self.steps)
        for number in order:
            name = names[number] if number >= 0 else names[-1 - number]
            if number < 0:
                waited.add(name)
                self.wait(name)
                continue
            kind, step, sources = self.steps[name]
            for source in sources:
                source = source[0] if isinstance(source, tuple) else source
                if source in self.steps and self.steps[source][0] != "run" and source not in waited:
                    waited.add(source)
                    self.wait(source)
            with jax.named_scope(name):
                result = step(*self.behind([self.value(source) for source in sources]))
            self.values[name] = result
            if kind == "run":
                self.mark = tuple(jax.tree.leaves(result))
        assert set(range(len(names))) <= set(order)


def pick(index, parts):
    return lax.select_n(index, *parts)


def total(*terms):
    return functools.reduce(jnp.add, [t.astype(f32) for t in terms])


def ring_step(block):
    count = lax.axis_size(SEG)
    return permuted(block, SEG, lambda i: (i + CORES) % count)


def in_order(parts, stretch):
    return [pick((stretch - k) % len(parts), parts) for k in range(len(parts))]


def swap_across(block):
    return permuted(block, BAT, lambda i: i ^ 1)


def swap_along(block):
    return permuted(block, BAT, lambda i: i ^ 2)


def cut_of(rows):
    return rows // 2 // 128 * 128


def qkv_half(matrix, core):
    rows, cols = matrix.shape
    return matrix.reshape(rows, cols // 256, 2, 128)[:, :, core].reshape(rows, cols // 2).T


def out_half(matrix, core):
    rows, cols = matrix.shape
    return matrix.reshape(rows // 256, 2, 128, cols)[:, core].reshape(rows // 2, cols)


def in_half(matrix, core, parts):
    rows, cols = matrix.shape
    return matrix.reshape(rows, parts, 2, cols // parts // 2)[:, :, core].reshape(rows, cols // 2).T


def down_half(matrix, core, parts):
    rows, cols = matrix.shape
    return matrix.reshape(parts, 2, rows // parts // 2, cols)[:, core].reshape(rows // 2, cols).T


def qkv_whole(halves):
    cols, rows = halves[0].shape
    stacked = jnp.stack([h.T.reshape(rows, cols // 128, 128) for h in halves], axis=2)
    return stacked.reshape(rows, 2 * cols)


def out_whole(halves):
    rows, cols = halves[0].shape
    stacked = jnp.stack([h.reshape(rows // 128, 128, cols) for h in halves], axis=1)
    return stacked.reshape(2 * rows, cols)


def in_whole(halves, parts):
    cols, rows = halves[0].shape
    stacked = jnp.stack([h.T.reshape(rows, parts, cols // parts) for h in halves], axis=2)
    return stacked.reshape(rows, 2 * cols)


def down_whole(halves, parts):
    cols, rows = halves[0].shape
    stacked = jnp.stack([h.T.reshape(parts, rows // parts, cols) for h in halves], axis=1)
    return stacked.reshape(2 * rows, cols)


def halves_of(parts):
    return (
        qkv_half,
        out_half,
        functools.partial(in_half, parts=parts),
        functools.partial(down_half, parts=parts),
    )


def gather_plain(shards, core):
    layers = ([], [])
    for shard, half in zip(shards, halves_of(4)):
        rows = lax.all_gather(shard, BAT, axis=1, tiled=True)
        slots = lax.all_gather(rows, SEG, axis=0, tiled=False)
        for layer in range(LAYERS):
            matrix = slots[layer::LAYERS].reshape(-1, rows.shape[1])
            layers[layer].append(jnp.where(core == 0, half(matrix, 0), half(matrix, 1)))
    return layers


def scatter_plain(parts, core):
    done = []
    slots = lax.axis_size(SEG)
    wholes = (qkv_whole, out_whole, functools.partial(in_whole, parts=4), functools.partial(down_whole, parts=4))
    for lower, upper, whole in zip(parts[0], parts[1], wholes):
        layers = []
        for half in (lower, upper):
            empty = jnp.zeros_like(half)
            matrix = whole((jnp.where(core == 0, half, empty), jnp.where(core == 0, empty, half)))
            layers.append(matrix.reshape(slots // LAYERS, -1, matrix.shape[1]))
        stacked = jnp.stack(layers, axis=1).reshape(slots, -1, layers[0].shape[2])
        rows = lax.psum_scatter(stacked, SEG, scatter_dimension=0, tiled=True)
        columns = lax.psum_scatter(rows, BAT, scatter_dimension=2, tiled=True)
        done.append(columns.astype(f32))
    return done


def spans(row_count, halo):
    for first in range(0, row_count, QB):
        start = max(0, first + halo - WIN)
        yield first, start, first + halo + QB - start


def mask_kernel(first_lane, chosen, index_ref, mask_ref):
    rows, slots = mask_ref.shape[1], mask_ref.shape[2]
    chunk = 64
    width = 256

    def body(first):
        index = index_ref[pl.ds(first, chunk), first_lane : first_lane + chosen]
        for low in range(0, slots, width):
            slot_ids = lax.broadcasted_iota(jnp.int32, (chunk, width), 1) + low
            bias = jnp.full((chunk, width), big_negative, f32)
            for t in range(chosen):
                bias = jnp.where(index[:, t : t + 1] == slot_ids, 0.0, bias)
            mask_ref[0, pl.ds(first, chunk), low : low + width] = bias.astype(bf16)

    chunks(rows, chunk, body)


def slot_mask(index, head, chosen, slots):
    out = jax.ShapeDtypeStruct((1, index.shape[0], slots), bf16)
    kernel = functools.partial(mask_kernel, head * chosen, chosen)
    return in_vmem(kernel, [out], None, [index], "slot_mask", 10_000_000_000)[0]


def nt_dot(left, right):
    return lax.dot_general(left, right, (((1,), (1,)), ((), ())), preferred_element_type=f32)


def tn_dot(left, right):
    return lax.dot_general(left, right, (((0,), (0,)), ((), ())), preferred_element_type=f32)


def nn_dot(left, right):
    return lax.dot_general(left, right, (((1,), (0,)), ((), ())), preferred_element_type=f32)


def forward_kernel(halo, with_memory, scale, *refs):
    refs = list(refs)
    bias_ref, docs_col, docs_row, q_ref, k_ref, v_ref = refs[:6]
    del refs[:6]
    if halo:
        k_halo, v_halo = refs[:2]
        del refs[:2]
    if with_memory:
        mem_k, mem_v, mask_ref, gate_ref = refs[:4]
        del refs[:4]
        o_ref, probs_ref, slots_ref, differ_ref = refs[:4]
        del refs[:4]
    else:
        o_ref, probs_ref = refs[:2]
        del refs[:2]
    if halo:
        keys, values = refs
        keys[:halo] = k_halo[...]
        keys[halo:] = k_ref[...]
        values[:halo] = v_halo[...]
        values[halo:] = v_ref[...]
    else:
        keys, values = k_ref, v_ref
    width = WIN + QB
    lanes = bias_ref.shape[2]
    tile = pltpu.roll(
        jnp.broadcast_to(bias_ref[0], (QB, lanes)), 0, axis=1, stride=1, stride_axis=0
    )[:, :width]
    if with_memory:
        opened = gate_ref[pl.program_id(0)]
    for first, start, count in spans(q_ref.shape[0], halo):
        rows = slice(first, first + QB)
        query = q_ref[rows]
        scores = nt_dot(query, keys[start : start + count]) * scale + tile[:, width - count :]
        same = docs_col[rows] == docs_row[:, start : start + count]
        scores = jnp.where(same, scores, big_negative)
        raised = jnp.exp(scores - jnp.max(scores, axis=-1, keepdims=True))
        probs = (raised * (1.0 / jnp.sum(raised, axis=-1, keepdims=True))).astype(bf16)
        probs_ref[0, rows, width - count :] = probs
        local = nn_dot(probs, values[start : start + count])
        if with_memory:
            picked = nt_dot(query, mem_k[...]) * scale + mask_ref[0, rows].astype(f32)
            raised = jnp.exp(picked - jnp.max(picked, axis=-1, keepdims=True))
            slot_probs = (raised * (1.0 / jnp.sum(raised, axis=-1, keepdims=True))).astype(bf16)
            slots_ref[0, rows] = slot_probs
            differ = nn_dot(slot_probs, mem_v[...]) - local
            differ_ref[rows] = differ.astype(bf16)
            local = local + opened * differ
        o_ref[rows] = local.astype(bf16)


def backward_kernel(halo, with_memory, scale, *refs):
    refs = list(refs)
    q_ref, k_ref, v_ref, do_ref, probs_ref = refs[:5]
    del refs[:5]
    if halo:
        k_halo, v_halo = refs[:2]
        del refs[:2]
    if with_memory:
        mem_k, mem_v, slots_ref, differ_ref, gate_ref = refs[:5]
        del refs[:5]
    d_ref, table_ref = refs[:2]
    del refs[:2]
    if with_memory:
        gate_grad = refs.pop(0)
    if halo:
        halo_grad = refs.pop(0)
    dk, dv, table = refs[:3]
    del refs[:3]
    if halo:
        keys, values = refs
        keys[:halo] = k_halo[...]
        keys[halo:] = k_ref[...]
        values[:halo] = v_halo[...]
        values[halo:] = v_ref[...]
    else:
        keys, values = k_ref, v_ref
    head = pl.program_id(0)
    heads = pl.num_programs(0)
    row_count, head_dim = q_ref.shape
    width = WIN + QB
    lanes = table.shape[1]
    dk[...] = jnp.zeros_like(dk)
    dv[...] = jnp.zeros_like(dv)
    table[...] = jnp.zeros_like(table)
    if with_memory:
        opened = gate_ref[head]
        gate_sum = jnp.zeros((1, head_dim), f32)
    here = pl.multiple_of(head * head_dim, head_dim)
    for first, start, count in spans(row_count, halo):
        rows = slice(first, first + QB)
        cols = slice(start, start + count)
        upstream = do_ref[rows]
        if with_memory:
            wide = upstream.astype(f32)
            gate_sum += jnp.sum(wide * differ_ref[rows].astype(f32), axis=0, keepdims=True)
            mem_grad = (opened * wide).astype(bf16)
            upstream = ((1.0 - opened) * wide).astype(bf16)
        probs = probs_ref[0, rows, width - count :]
        probs_wide = probs.astype(f32)
        grad = nt_dot(upstream, values[cols])
        inner = jnp.sum(probs_wide * grad, axis=-1, keepdims=True)
        score_wide = probs_wide * (grad - inner)
        score = score_wide.astype(bf16)
        table[:, width - count : width] += score_wide
        dq = nn_dot(score, keys[cols])
        dk[cols] += tn_dot(score, q_ref[rows])
        dv[cols] += tn_dot(probs, upstream)
        if with_memory:
            slot_probs = slots_ref[0, rows].astype(f32)
            slot_grad = nt_dot(mem_grad, mem_v[...])
            slot_score = slot_probs * (
                slot_grad - jnp.sum(slot_probs * slot_grad, axis=-1, keepdims=True)
            )
            dq += nn_dot(slot_score.astype(bf16), mem_k[...])
        d_ref[rows, pl.ds(here, head_dim)] = (dq * scale).astype(bf16)
    key_at = pl.multiple_of((heads + head) * head_dim, head_dim)
    value_at = pl.multiple_of((2 * heads + head) * head_dim, head_dim)
    if halo:
        halo_grad[0] = (dk[:halo] * scale).astype(bf16)
        halo_grad[1] = dv[:halo].astype(bf16)
    d_ref[:, pl.ds(key_at, head_dim)] = (dk[halo:] * scale).astype(bf16)
    d_ref[:, pl.ds(value_at, head_dim)] = dv[halo:].astype(bf16)
    turned = jnp.zeros((8, lanes), f32)
    for row in range(0, QB, 8):
        part = table[row : row + 8]
        turned += pltpu.roll(part, lanes - row, axis=1) if row else part
    total = turned[:1]
    for row in range(1, 8):
        total += pltpu.roll(turned, lanes - row, axis=1)[row : row + 1]
    table_ref[0] = total
    if with_memory:
        gate_grad[0] = gate_sum


def smooth_pair(pre):
    rate = math.sqrt(2.0 / math.pi)
    square = pre * pre
    turn = jnp.tanh(pre * (rate + (rate * 0.044715) * square))
    half = 0.5 + 0.5 * turn
    bend = pre * (rate + (rate * 3 * 0.044715) * square)
    return (pre * half).astype(bf16), (half + bend * (half - half * half) * 2.0).astype(bf16)


def norm_rows_of(values):
    center = values - jnp.mean(values, axis=-1, keepdims=True)
    factor = lax.rsqrt(jnp.mean(center * center, axis=-1, keepdims=True) + norm_eps)
    return center * factor, factor


def in_vmem(kernel, outs, scalars, operands, name, flops):
    vmem = pl.BlockSpec(memory_space=pltpu.VMEM)
    return pl.pallas_call(
        kernel,
        out_shape=outs,
        in_specs=([smem_block] if scalars is not None else []) + [vmem] * len(operands),
        out_specs=[vmem] * len(outs),
        compiler_params=pltpu.CompilerParams(vmem_limit_bytes=8 * 1024 * 1024),
        cost_estimate=pl.CostEstimate(flops=3 * flops, transcendentals=0, bytes_accessed=0),
        name=name,
    )(*([scalars] if scalars is not None else []), *operands)


smem_block = pl.BlockSpec(memory_space=pltpu.SMEM)


def chunks(count, size, body):
    def step(turn, carry):
        body(pl.multiple_of(turn * size, size))
        return carry

    lax.fori_loop(0, count // size, step, 0)


def segments(refs, low, high):
    for which, ref in enumerate(refs[:3]):
        yield which, 0, ref, low, high
    cut = refs[3].shape[0]
    if low < cut:
        yield 3, 0, refs[3], low, min(high, cut)
    if high > cut:
        yield 3, max(cut - low, 0), refs[4], max(low - cut, 0), high - cut


def place_of(at_ref, which, width, offset=0):
    return pl.multiple_of((at_ref[0] ^ which) * width + offset, 128)


def norm_kernel(row, part, at_ref, own_ref, across_ref, along_ref, low_ref, high_ref, out_ref):
    rows = [ref[row : row + 1, :].astype(f32) for ref in (own_ref, across_ref, along_ref)]
    rows.append(high_ref[row - low_ref.shape[0] : row - low_ref.shape[0] + 1, :].astype(f32))
    width = 4 * part
    chips = rows[0].shape[1] // width
    for k in range(4):
        which = at_ref[0] ^ k
        row_k = jnp.where(
            which < 2, jnp.where(which == 0, rows[0], rows[1]), jnp.where(which == 2, rows[2], rows[3])
        )
        for z in range(chips):
            for kind in range(4):
                first = z * width + kind * part
                out_ref[kind : kind + 1, z * width + k * part : z * width + (k + 1) * part] = row_k[:, first : first + part]


def norm_rows_by_pieces(at, row, part, pieces):
    out = jax.ShapeDtypeStruct((4, pieces[0].shape[1]), f32)
    return in_vmem(functools.partial(norm_kernel, row, part), [out], at, list(pieces), "norm", 1000)[0]


def head_kernel(joins, width, at_ref, *refs):
    hidden_ref, *refs = refs
    if joins:
        own_ref, got_ref, *refs = refs
    gain_ref, shift_ref, *refs = refs
    pieces, (normed_ref, out_ref), refs = refs[:5], refs[5:7], refs[7:]
    parts = list(segments(pieces, 0, width))

    def body(first):
        rows = pl.ds(first, 256)
        values = hidden_ref[rows, :]
        if joins:
            values = values + (own_ref[rows, :].astype(f32) + got_ref[rows, :].astype(f32))
            refs[0][rows, :] = values
        normal, _ = norm_rows_of(values)
        normed = (normal * gain_ref[...] + shift_ref[...]).astype(bf16)
        normed_ref[rows, :] = normed
        for which, offset, ref, low, high in parts:
            cols = pl.ds(place_of(at_ref, which, width, offset), high - low)
            out_ref[rows, cols] = nt_dot(normed, ref[low:high]).astype(bf16)

    chunks(hidden_ref.shape[0], 256, body)


def head_by_pieces(at, width, hidden, joins, gain, shift, pieces):
    rows, inner = hidden.shape
    outs = [jax.ShapeDtypeStruct((rows, inner), bf16), jax.ShapeDtypeStruct((rows, 4 * width), bf16)]
    if joins:
        outs.append(jax.ShapeDtypeStruct((rows, inner), f32))
    operands = [hidden, *joins, gain, shift, *pieces]
    return in_vmem(
        functools.partial(head_kernel, bool(joins), width), outs, at, operands, "head", 8 * rows * inner * width
    )


def by_columns_kernel(smooth, at_ref, rows_ref, *refs):
    pieces, outs = refs[:5], refs[5:]
    width = pieces[0].shape[0]
    parts = list(segments(pieces, 0, width))

    def body(first):
        rows = pl.ds(first, 256)
        for which, offset, ref, low, high in parts:
            cols = pl.ds(place_of(at_ref, which, width, offset), high - low)
            product = nt_dot(rows_ref[rows, :], ref[low:high])
            if smooth:
                outs[0][rows, cols], outs[1][rows, cols] = smooth_pair(product)
            else:
                outs[0][rows, cols] = product.astype(bf16)

    chunks(rows_ref.shape[0], 256, body)


def by_columns(at, rows, pieces, smooth):
    count, inner = rows.shape
    width = pieces[0].shape[0]
    outs = [jax.ShapeDtypeStruct((count, 4 * width), bf16)] * (2 if smooth else 1)
    return in_vmem(
        functools.partial(by_columns_kernel, smooth), outs, at, [rows, *pieces], "expand" if smooth else "down",
        8 * count * inner * width,
    )


def out_kernel(first, rows_per, width, at_ref, rows_ref, *refs):
    pieces, out_ref = refs[:5], refs[5]
    parts = list(segments(pieces, first, first + rows_per))

    def body(start):
        rows = pl.ds(start, 256)
        for which, _, ref, low, high in parts:
            acc = None
            for z in range(rows_ref.shape[1] // rows_per):
                part = nn_dot(
                    rows_ref[rows, z * rows_per : (z + 1) * rows_per], ref[low:high, z * width : (z + 1) * width]
                )
                acc = part if acc is None else acc + part
            out_ref[rows, pl.ds(place_of(at_ref, which, width), width)] = acc.astype(bf16)

    chunks(rows_ref.shape[0], 256, body)


def out_by_pieces(at, first, rows_per, width, attended, pieces):
    count = attended.shape[0]
    outs = [jax.ShapeDtypeStruct((count, 4 * width), bf16)]
    return in_vmem(
        functools.partial(out_kernel, first, rows_per, width), outs, at, [attended, *pieces], "out",
        8 * count * attended.shape[1] * width,
    )[0]


def by_rows_kernel(low, high, scaled, at_ref, rows_ref, *refs):
    pieces, refs = refs[:5], refs[5:]
    out_ref = refs[-1]
    span = high - low
    parts = list(segments(pieces, low, high))
    block = 512

    def body(start):
        rows = pl.ds(start, 256)
        for n in range(0, out_ref.shape[1], block):
            cols = slice(n, n + block)
            acc = None
            for which, offset, ref, first, last in parts:
                inner = pl.ds(place_of(at_ref, which, span, offset), last - first)
                part = nn_dot(rows_ref[rows, inner], ref[first:last, cols])
                acc = part if acc is None else acc + part
            if scaled:
                acc = acc * refs[0][rows, cols].astype(f32)
            out_ref[rows, cols] = acc.astype(bf16)

    chunks(rows_ref.shape[0], 256, body)


def by_rows(at, low, high, grad, pieces, slope=None):
    count = grad.shape[0]
    cols = pieces[0].shape[1]
    operands = [grad, *pieces] + ([] if slope is None else [slope])
    return in_vmem(
        functools.partial(by_rows_kernel, low, high, slope is not None),
        [jax.ShapeDtypeStruct((count, cols), bf16)], at, operands, "by_rows", 2 * count * grad.shape[1] * cols,
    )[0]


def attended_back_kernel(first, rows_per, width, at_ref, grad_ref, *refs):
    pieces, out_ref = refs[:5], refs[5]
    parts = list(segments(pieces, first, first + rows_per))

    def body(start):
        rows = pl.ds(start, 256)
        for z in range(out_ref.shape[1] // rows_per):
            acc = None
            for which, _, ref, low, high in parts:
                grad = grad_ref[rows, pl.ds(place_of(at_ref, which, width), width)]
                part = nt_dot(grad, ref[low:high, z * width : (z + 1) * width])
                acc = part if acc is None else acc + part
            out_ref[rows, z * rows_per : (z + 1) * rows_per] = acc.astype(bf16)

    chunks(grad_ref.shape[0], 256, body)


def attended_back(at, first, rows_per, width, grad, pieces):
    count = grad.shape[0]
    chips = pieces[0].shape[1] // width
    return in_vmem(
        functools.partial(attended_back_kernel, first, rows_per, width),
        [jax.ShapeDtypeStruct((count, chips * rows_per), bf16)], at, [grad, *pieces], "attended_back",
        2 * count * grad.shape[1] * chips * rows_per,
    )[0]


def share_kernel(which, heads, adds, at_ref, *refs):
    left_ref, right_ref, *refs = refs
    if heads:
        attended_ref, grad_ref, *refs = refs
    count = {"": 0, "low": 1, "high": 1, "both": 2}[adds]
    got, outs = refs[:count], refs[count:]
    chips = 4
    rows, width = left_ref.shape[1] // 4, right_ref.shape[1] // chips
    own = which == 0
    left = left_ref[:, pl.ds(place_of(at_ref, which, rows), rows)]
    if heads:
        more = attended_ref.shape[1] // chips
        grad = grad_ref[:, pl.ds(place_of(at_ref, which, grad_ref.shape[1] // 4), grad_ref.shape[1] // 4)]

    def body(n):
        column = lax.rem(at_ref[1] + (3 * chips - 1) - n, chips) if own else n
        cols = pl.ds(pl.multiple_of(column * width, width), width)
        value = tn_dot(left, right_ref[:, cols])
        if heads:
            part = tn_dot(attended_ref[:, pl.ds(pl.multiple_of(column * more, more), more)], grad)
            value = jnp.concatenate([value, part], axis=0)
        half = value.shape[0] // 2
        if adds == "low":
            value = jnp.concatenate([value[:half] + got[0][:, cols].astype(f32), value[half:]], axis=0)
        elif adds == "high":
            value = jnp.concatenate([value[:half], value[half:] + got[0][:, cols].astype(f32)], axis=0)
        elif adds == "both":
            value = value + got[0][:, cols].astype(f32) + got[1][:, cols].astype(f32)
        value = value.astype(bf16)
        if which == 3:
            outs[0][:, cols], outs[1][:, cols] = value[:half], value[half:]
        elif own:
            outs[0][n] = value
        else:
            outs[0][:, cols] = value

    def step(n, carry):
        body(n)
        return carry

    lax.fori_loop(0, chips, step, 0)


def share_grad(at, which, left, right, head_pair=(), adds="", got=()):
    chips = 4
    rows, cols = left.shape[1] // 4, right.shape[1]
    if head_pair:
        rows += head_pair[0].shape[1] // chips
    if which == 3:
        outs = [jax.ShapeDtypeStruct((rows // 2, cols), bf16)] * 2
    elif which == 0:
        outs = [jax.ShapeDtypeStruct((chips, rows, cols // chips), bf16)]
    else:
        outs = [jax.ShapeDtypeStruct((rows, cols), bf16)]
    return in_vmem(
        functools.partial(share_kernel, which, bool(head_pair), adds), outs, at, [left, right, *head_pair, *got],
        "share", 2 * left.shape[0] * rows * cols,
    )


def join_norm_kernel(hidden_ref, own_ref, got_ref, gain_ref, shift_ref, result_ref, normed_ref):
    def body(first):
        rows = pl.ds(first, 128)
        values = hidden_ref[rows, :] + (own_ref[rows, :].astype(f32) + got_ref[rows, :].astype(f32))
        result_ref[rows, :] = values
        normal, _ = norm_rows_of(values)
        normed_ref[rows, :] = (normal * gain_ref[...] + shift_ref[...]).astype(bf16)

    chunks(hidden_ref.shape[0], 128, body)


def join_norm(hidden, own, got, gain, shift):
    outs = [jax.ShapeDtypeStruct(hidden.shape, f32), jax.ShapeDtypeStruct(hidden.shape, bf16)]
    return in_vmem(join_norm_kernel, outs, None, [hidden, own, got, gain, shift], "join_norm", 10 * hidden.size)


def join_back_kernel(up_ref, own_ref, got_ref, values_ref, gain_ref, result_ref, low_ref, gain_grad, shift_grad):
    gain_grad[...] = jnp.zeros_like(gain_grad)
    shift_grad[...] = jnp.zeros_like(shift_grad)

    def body(first):
        rows = pl.ds(first, 128)
        upstream = own_ref[rows, :].astype(f32) + got_ref[rows, :].astype(f32)
        normal, factor = norm_rows_of(values_ref[rows, :])
        gain_grad[...] += jnp.sum(upstream * normal, axis=0, keepdims=True)
        shift_grad[...] += jnp.sum(upstream, axis=0, keepdims=True)
        scaled = upstream * gain_ref[...]
        inner = (
            scaled
            - jnp.mean(scaled, axis=-1, keepdims=True)
            - normal * jnp.mean(scaled * normal, axis=-1, keepdims=True)
        )
        result = up_ref[rows, :].astype(f32) + factor * inner
        result_ref[rows, :] = result
        low_ref[rows, :] = result.astype(bf16)

    chunks(values_ref.shape[0], 128, body)


def join_back(upstream, own, got, values, gain):
    row = jax.ShapeDtypeStruct((1, values.shape[1]), f32)
    outs = [jax.ShapeDtypeStruct(values.shape, f32), jax.ShapeDtypeStruct(values.shape, bf16), row, row]
    return in_vmem(join_back_kernel, outs, None, [upstream, own, got, values, gain], "join_back", 20 * values.size)


def head_block(rows, head_dim, offset):
    return pl.BlockSpec((rows, head_dim), lambda h: (0, offset + h))


def plane_block(rows, cols):
    return pl.BlockSpec((1, rows, cols), lambda h: (h, 0, 0))


def attend(projected, bias_rows, docs_col, docs_row, halo_rows, memory, scale):
    row_count = projected.shape[0]
    head_count, _, lanes = bias_rows.shape
    head_dim = projected.shape[1] // (3 * head_count)
    halo = 0 if halo_rows is None else halo_rows.shape[1]
    width = WIN + QB
    operands = [bias_rows, docs_col, docs_row, projected, projected, projected]
    specs = [
        plane_block(1, lanes),
        pl.BlockSpec(docs_col.shape, lambda h: (0, 0)),
        pl.BlockSpec(docs_row.shape, lambda h: (0, 0)),
        head_block(row_count, head_dim, 0),
        head_block(row_count, head_dim, head_count),
        head_block(row_count, head_dim, 2 * head_count),
    ]
    scratch = []
    if halo:
        operands += [halo_rows[0], halo_rows[1]]
        specs += [head_block(halo, head_dim, 0)] * 2
        scratch = [pltpu.VMEM((halo + row_count, head_dim), bf16)] * 2
    outs = [
        jax.ShapeDtypeStruct((row_count, head_count * head_dim), bf16),
        jax.ShapeDtypeStruct((head_count, row_count, width), bf16),
    ]
    out_specs = [head_block(row_count, head_dim, 0), plane_block(row_count, width)]
    flops = 4 * head_count * row_count * width * head_dim
    if memory is not None:
        mem_keys, mem_values, masks, gate = memory
        slots = mem_keys.shape[0]
        mask = jnp.concatenate(masks, axis=0)
        operands += [mem_keys, mem_values, mask, gate]
        specs += [head_block(slots, head_dim, 0)] * 2 + [plane_block(row_count, slots), smem_block]
        outs += [
            jax.ShapeDtypeStruct((head_count, row_count, slots), bf16),
            jax.ShapeDtypeStruct((row_count, head_count * head_dim), bf16),
        ]
        out_specs += [plane_block(row_count, slots), head_block(row_count, head_dim, 0)]
        flops += 4 * head_count * row_count * slots * head_dim
    return pl.pallas_call(
        functools.partial(forward_kernel, halo, memory is not None, scale),
        out_shape=outs,
        grid=(head_count,),
        in_specs=specs,
        out_specs=out_specs,
        scratch_shapes=scratch,
        compiler_params=pltpu.CompilerParams(vmem_limit_bytes=VMEM_LIMIT),
        cost_estimate=pl.CostEstimate(
            flops=flops, transcendentals=head_count * row_count * width, bytes_accessed=16 * 1024 * 1024
        ),
        name="attend",
    )(*operands)


def attend_back(projected, grad, probs, halo_rows, memory, scale):
    row_count = projected.shape[0]
    head_count, _, width = probs.shape
    head_dim = projected.shape[1] // (3 * head_count)
    halo = 0 if halo_rows is None else halo_rows.shape[1]
    lanes = 1024
    operands = [projected, projected, projected, grad, probs]
    specs = [
        head_block(row_count, head_dim, 0),
        head_block(row_count, head_dim, head_count),
        head_block(row_count, head_dim, 2 * head_count),
        head_block(row_count, head_dim, 0),
        plane_block(row_count, width),
    ]
    scratch = [
        pltpu.VMEM((halo + row_count, head_dim), f32),
        pltpu.VMEM((halo + row_count, head_dim), f32),
        pltpu.VMEM((QB, lanes), f32),
    ]
    if halo:
        operands += [halo_rows[0], halo_rows[1]]
        specs += [head_block(halo, head_dim, 0)] * 2
        scratch += [pltpu.VMEM((halo + row_count, head_dim), bf16)] * 2
    outs = [
        jax.ShapeDtypeStruct(projected.shape, bf16),
        jax.ShapeDtypeStruct((head_count, 1, lanes), f32),
    ]
    out_specs = [pl.BlockSpec(projected.shape, lambda h: (0, 0)), plane_block(1, lanes)]
    flops = 8 * head_count * row_count * width * head_dim
    if memory is not None:
        mem_keys, mem_values, slot_probs, differ, gate = memory
        slots = mem_keys.shape[0]
        operands += [mem_keys, mem_values, slot_probs, differ, gate]
        specs += [head_block(slots, head_dim, 0)] * 2
        specs += [plane_block(row_count, slots), head_block(row_count, head_dim, 0), smem_block]
        outs += [jax.ShapeDtypeStruct((head_count, 1, head_dim), f32)]
        out_specs += [plane_block(1, head_dim)]
        flops += 4 * head_count * row_count * slots * head_dim
    if halo:
        outs += [jax.ShapeDtypeStruct((2, halo, head_count * head_dim), bf16)]
        out_specs += [pl.BlockSpec((2, halo, head_dim), lambda h: (0, 0, h))]
    return pl.pallas_call(
        functools.partial(backward_kernel, halo, memory is not None, scale),
        out_shape=outs,
        grid=(head_count,),
        in_specs=specs,
        out_specs=out_specs,
        scratch_shapes=scratch,
        compiler_params=pltpu.CompilerParams(vmem_limit_bytes=VMEM_LIMIT),
        cost_estimate=pl.CostEstimate(
            flops=flops, transcendentals=0, bytes_accessed=20 * 1024 * 1024
        ),
        name="attend_back",
    )(*operands)


def bucket_of(distance):
    beyond = jnp.sum((distance[..., None] >= jnp.asarray(bucket_edges)).astype(jnp.int32), axis=-1)
    return jnp.where(distance < 16, distance, 16 + beyond)


def distance_onehot(bucket_count):
    bucket = bucket_of(jnp.arange(WIN, dtype=jnp.int32))
    return (bucket[:, None] == jnp.arange(bucket_count, dtype=jnp.int32)).astype(f32)


def normalize(values):
    center = values - jnp.mean(values, axis=-1, keepdims=True)
    factor = lax.rsqrt(jnp.mean(center * center, axis=-1, keepdims=True) + norm_eps)
    return center * factor, factor


def head_in(hidden, gain, shift, qkv):
    normal, _ = normalize(hidden)
    normed = (normal * gain + shift).astype(bf16)
    return normed, nt_dot(normed, qkv).astype(bf16)


def out_part(attended, out):
    return nn_dot(attended, out).astype(bf16)


def down_part(active, down):
    return nt_dot(active, down).astype(bf16)


def joined(hidden, own, got):
    return hidden + (own.astype(f32) + got.astype(f32))


def weight_grad(left, right):
    return tn_dot(left, right).astype(bf16)


def expand_back(upstream, down, slope):
    return (nn_dot(upstream, down) * slope.astype(f32)).astype(bf16)


def input_part(grad, weight):
    return nn_dot(grad, weight).astype(bf16)


class Place:
    def __init__(self, seq_count):
        self.segments = lax.axis_size(SEG)
        self.batches = lax.axis_size(BAT)
        self.chips = self.segments // CORES
        self.seqs = seq_count
        self.pairs = self.chips // seq_count
        here = lax.axis_index(SEG)
        self.batch = lax.axis_index(BAT)
        self.core = here % CORES
        self.stretch = here // CORES
        self.low = self.core == 0
        self.seq_no = self.stretch // self.pairs
        self.place_no = self.stretch % seq_count

    def both(self, own, got):
        return jnp.where(self.low, own, got), jnp.where(self.low, got, own)


    def route(self, turn):
        pairs = []
        for source in range(self.segments):
            chip, lane = divmod(source, CORES)
            group, place = divmod(chip, self.seqs)
            pairs.append((source, (((place + turn) % self.seqs) * self.pairs + group) * CORES + lane))
        return pairs

    def local(self, turn):
        return self.pairs == 1 and turn == 0

    def out_block(self, stored, turn):
        return lax.dynamic_index_in_dim(stored, (self.place_no + turn) % self.seqs, 0, keepdims=False)

    def back_block(self, blocks, turn):
        return lax.dynamic_index_in_dim(blocks, (self.seq_no - turn) % self.seqs, 0, keepdims=False)

    def owned(self, *got):
        return jnp.stack([pick((self.seq_no - place) % self.seqs, got) for place in range(self.seqs)])

    def stored(self, *got):
        return jnp.stack([pick((number - self.place_no) % self.seqs, got) for number in range(self.seqs)])

    def sequence(self, own, got):
        pair = jnp.stack(self.both(own, got), axis=1)
        return pair.reshape((-1,) + own.shape[2:])

    def own_blocks(self, rows):
        split = rows.reshape(self.seqs, CORES, -1, rows.shape[1])
        return jnp.where(self.low, split[:, 0], split[:, 1])


def route_blocks(steps, place, name, source, back=False):
    got = []
    for turn in range(place.seqs):
        block = steps.run(key(name, "b", turn), lambda v, t=turn: (place.back_block if back else place.out_block)(v, t), source)
        if not place.local(turn):
            route = place.route(turn)
            if back:
                route = [(there, here) for here, there in route]
            block = steps.send(
                key(name, turn), key("z", turn), lambda v, route=tuple(route): lax.ppermute(v, SEG, route), block
            )
        got.append(block)
    return steps.run(key(name, "own"), place.stored if back else place.owned, *got)


def swap(steps, name, source):
    return steps.send(name, "core", core_swap, source)


def gather_steps(steps, place, shards, norm_rows, memory):
    qkv, out, inner, down = shards
    width = qkv.shape[0]
    gain_cols = norm_rows.shape[-1]
    slots = memory.shape[3]
    head, outs, hidden = qkv.shape[1] // 2, out.shape[0] // 2, inner.shape[1] // 2
    ends = np.cumsum([head + outs + 16, hidden, 2 * down.shape[1], memory[0].size // width])
    chips = place.chips

    def packed(core, qkv, out, inner, down, norm_rows, memory):
        down_rows = down_half(down, core, 1)
        return jnp.concatenate(
            [
                qkv_half(qkv, core),
                out_half(out, core),
                jnp.pad(norm_rows.reshape(1, width), ((0, 15), (0, 0))),
                in_half(inner, core, 1),
                down_rows[:, :width],
                down_rows[:, width:],
                memory_rows_of(memory[core]),
            ],
            axis=0,
        )

    def memory_rows_of(memory):
        return jnp.concatenate(
            [memory[kind, 0, :, at : at + width] for kind in range(2) for at in range(0, memory.shape[3], width)], axis=0
        )

    def first(*arrays):
        low, high = packed(0, *arrays), packed(1, *arrays)
        return jnp.where(place.low, low, high), jnp.where(place.low, high, low)

    for name, array in zip(("qkv", "out", "inner", "down", "norm", "mem"), (*shards, norm_rows, memory)):
        steps.given(name, array)
    steps.run("pack", first, "qkv", "out", "inner", "down", "norm", "mem")
    swap(steps, "wswap", ("pack", 1))

    def blocks(own, got):
        lower, upper = place.both(own, got)
        kept = []
        for layer in (lower, upper):
            kept += [layer[: ends[0]], layer[ends[0] : ends[1]], layer[ends[1] : ends[2]]]
        memory_rows = jnp.concatenate([lower[ends[2] :], upper[ends[2] :]], axis=0)
        kept[3] = jnp.concatenate([kept[3], memory_rows], axis=0)
        return kept

    steps.run("blocks", blocks, ("pack", 0), "wswap")

    def formed(unit, *ring):
        parts = in_order(ring, place.stretch)
        if unit[0] == "A":
            rows = jnp.concatenate([p[: ends[0]] for p in parts], axis=1)
            if unit == "A0":
                return (rows,)
            halves = memory.shape[4] // width
            block = 2 * halves * slots
            whole = []
            for kind in range(2):
                cols = []
                for half in range(halves):
                    first = ends[0] + (kind * halves + half) * slots
                    cols.append(
                        jnp.concatenate(
                            [p[first + c * block : first + c * block + slots] for p in parts for c in range(CORES)], axis=0
                        )
                    )
                whole.append(jnp.concatenate(cols, axis=1))
            return rows, jnp.stack(whole)
        if unit[0] == "I":
            return (jnp.concatenate(parts, axis=1),)
        half = parts[0].shape[0] // 2
        return (jnp.concatenate([q for p in parts for q in (p[:half], p[half:])], axis=1),)

    def norm_of(at, *pieces):
        return norm_rows_by_pieces(at, head + outs, gain_cols, pieces)

    pieces = {}
    for number, unit in enumerate(("A0", "I0", "D0", "A1", "I1", "D1")):
        ring = [("blocks", number)]
        for turn in range(1, chips):
            ring.append(steps.send(key("z", turn, unit), "z", ring_step, ring[-1]))
        steps.run(key("form", unit), functools.partial(formed, unit), *ring)
        block = (key("form", unit), 0)
        steps.send(key("px", unit), "x", swap_across, block)
        steps.send(key("py", unit), "y", swap_along, block)
        steps.send(key("fx", unit), "x", lambda along: swap_across(along[: cut_of(along.shape[0])]), key("py", unit))
        steps.send(key("fy", unit), "y", lambda across: swap_along(across[cut_of(across.shape[0]) :]), key("px", unit))
        pieces[unit] = (block, key("px", unit), key("py", unit), key("fx", unit), key("fy", unit))
        if unit[0] == "A":
            steps.run(key("norm", unit[1]), norm_of, "at", *pieces[unit])
    return pieces, ("formA1", 1), (head, outs, width)


def scatter_steps(steps, place, unit, left, right, *head_pair):
    heads = bool(head_pair)

    def shares(which, adds):
        def step(at, left, right, *rest):
            pair, got = (rest[:2], rest[2:]) if heads else ((), rest)
            return share_grad(at, which, left, right, pair, adds, got)

        return step

    sources = ("place", left, right, *head_pair)
    steps.run(key("ra", unit), shares(3, ""), *sources)
    steps.send(key("rx", unit), "x", swap_across, (key("ra", unit), 0))
    steps.send(key("ry", unit), "y", swap_along, (key("ra", unit), 1))
    steps.run(key("rb", unit), shares(1, "high"), *sources, key("ry", unit))
    steps.run(key("rc", unit), shares(2, "low"), *sources, key("rx", unit))
    steps.send(key("sx", unit), "x", swap_across, (key("rb", unit), 0))
    steps.send(key("sy", unit), "y", swap_along, (key("rc", unit), 0))
    steps.run(key("rd", unit), shares(0, "both"), *sources, key("sx", unit), key("sy", unit))
    own = (key("rd", unit), 0)
    travelling = steps.run(key("a0", unit), lambda parts: parts[0], own)
    for turn in range(1, place.chips):
        steps.send(key("q", turn, unit), "z", ring_step, travelling)
        last = turn == place.chips - 1
        travelling = steps.run(
            key("a", turn, unit),
            lambda got, parts, turn=turn, last=last: total(got, parts[turn]) if last else total(got, parts[turn]).astype(bf16),
            key("q", turn, unit),
            own,
        )
    return travelling


def finish_steps(steps, place, kind, lower, upper):
    steps.run(key("e", kind), lambda a, b: jnp.where(place.low, b, a).astype(bf16), lower, upper)
    swap(steps, key("eswap", kind), key("e", kind))

    def both(lower, upper, got):
        return place.both(jnp.where(place.low, lower, upper), got.astype(f32))

    return steps.run(key("done", kind), both, lower, upper, key("eswap", kind))


def on_device(
    tokens,
    doc_ids,
    knn_index,
    mem_keys,
    mem_values,
    qkv_weight,
    out_weight,
    in_weight,
    down_weight,
    norm_gain,
    norm_bias,
    rel_table,
    mem_gate,
    cotangent,
):
    seq_count, block_len, model_width = tokens.shape
    bucket_count, head_total = rel_table.shape[1:]
    head_dim = model_width // head_total
    topk_count = knn_index.shape[3]
    heads = head_total // CORES
    inner_width = heads * head_dim
    scale = 1.0 / math.sqrt(head_dim)
    place = Place(seq_count)
    steps = Steps()
    low_core = place.low
    pair_len = CORES * seq_count * block_len
    halo = WIN if place.pairs > 1 else 0
    by_chip = place.pairs == 1 and place.batches == 4

    norm_rows = jnp.stack([norm_gain[0], norm_bias[0]])
    shards = (qkv_weight[0], out_weight[0], in_weight[0], down_weight[0])
    memory = jnp.stack([mem_keys, mem_values]).reshape(2, mem_keys.shape[0], heads, CORES, head_dim)
    memory = jnp.transpose(memory, (3, 0, 1, 2, 4)).reshape(CORES, 2, 1, mem_keys.shape[0], inner_width)
    if by_chip:
        pieces, memory_at, sizes = gather_steps(steps, place, shards, norm_rows, memory)
    else:
        norms = lax.all_gather(norm_rows, (BAT, SEG), axis=0, tiled=False)
        norms = norms.reshape(place.batches, place.chips, LAYERS, 2, 2, norm_rows.shape[-1])
        norms = jnp.transpose(norms, (2, 3, 4, 1, 0, 5)).reshape(LAYERS, 2, 2, -1).astype(f32)
        weights = []
        for layer, matrices in enumerate(gather_plain(shards, place.core)):
            named = zip(("qkv", "out", "inner", "down", "norm"), (*matrices, norms[layer]))
            weights.append(tuple(steps.given(key(name, layer), array) for name, array in named))
        whole = lax.all_gather(memory, SEG, axis=3, tiled=True)
        memory_at = steps.given("memory", jnp.where(low_core, whole[0], whole[1])[:, 0])

    docs = lax.dynamic_index_in_dim(doc_ids, place.seq_no, 0, keepdims=False)
    first_row = place.stretch % place.pairs * pair_len
    docs_col = lax.dynamic_slice_in_dim(docs, first_row, pair_len, 0).reshape(pair_len, 1)
    docs_padded = jnp.concatenate([jnp.full((halo,), -1, jnp.int32), docs]) if halo else docs
    docs_row = lax.dynamic_slice_in_dim(docs_padded, first_row, halo + pair_len, 0).reshape(1, -1)
    steps.given("cols", docs_col)
    steps.given("rows", docs_row)
    onehot = distance_onehot(bucket_count)
    lanes = 1024

    def biases(table):
        tables = table.reshape(LAYERS, bucket_count, heads, CORES)
        tables = jnp.where(low_core, tables[..., 0], tables[..., 1])
        near = jnp.einsum("db,lbh->lhd", onehot[::-1], tables, precision=highest)[:, :, None]
        before = jnp.full((LAYERS, heads, 1, 1), big_negative, f32)
        beyond = jnp.full((LAYERS, heads, 1, lanes - WIN - 1), big_negative, f32)
        joined = jnp.concatenate([before, near, beyond], axis=3)
        return [joined[layer] for layer in range(LAYERS)]

    steps.run("bias", biases, steps.given("table", rel_table))
    gate_all = jax.nn.sigmoid(mem_gate).reshape(heads, CORES)
    gate = jnp.where(low_core, gate_all[:, 0], gate_all[:, 1])
    steps.given("gate", gate)

    def routed(name, array):
        return route_blocks(steps, place, name, steps.given(key(name, "in"), array))

    def by_head(blocks):
        rows = blocks.reshape(seq_count * block_len, head_total * topk_count)
        parts = [rows[:, h * topk_count : (h + 1) * topk_count] for h in range(head_total)]
        even, odd = jnp.concatenate(parts[::CORES], axis=1), jnp.concatenate(parts[1::CORES], axis=1)
        return jnp.where(low_core, even, odd), jnp.where(low_core, odd, even)

    slot_total = mem_keys.shape[0] * place.segments
    steps.run("flat", lambda v: v.reshape(seq_count, block_len, head_total * topk_count), steps.given("knn", knn_index))
    steps.run("kh", by_head, route_blocks(steps, place, "k", "flat"))
    swap(steps, "kswap", ("kh", 1))

    def whole_index(own, got):
        shape = (seq_count, block_len, heads * topk_count)
        pair = jnp.stack(place.both(own.reshape(shape), got.reshape(shape)), axis=1)
        return pair.reshape(pair_len, heads * topk_count)

    steps.run("index", whole_index, ("kh", 0), "kswap")
    masks = [
        steps.run(key("mask", head), lambda index, head=head: slot_mask(index, head, topk_count, slot_total), "index")
        for head in range(heads)
    ]

    own = routed("t", tokens)
    swap(steps, "tswap", own)
    hidden = steps.run("hid0", lambda own, got: place.sequence(own, got).astype(f32), own, "tswap")
    own = routed("c", cotangent)
    swap(steps, "cswap", own)
    upstream_low = steps.run("up", place.sequence, own, "cswap")
    upstream = upstream_low

    def halo_of(projected):
        if not halo:
            return None
        tail = projected[pair_len - halo :, inner_width:]
        route = [(i, i + CORES) for i in range(place.segments - CORES) if (i // CORES + 1) % place.pairs != 0]
        got = lax.ppermute(tail, SEG, route)
        return jnp.stack([got[:, :inner_width], got[:, inner_width:]])

    def halo_back(d_projected, halo_grad):
        route = [(i + CORES, i) for i in range(place.segments - CORES) if (i // CORES + 1) % place.pairs != 0]
        got = lax.ppermute(jnp.concatenate([halo_grad[0], halo_grad[1]], axis=1), SEG, route)
        edge = d_projected[pair_len - halo :, inner_width:].astype(f32) + got.astype(f32)
        return d_projected.at[pair_len - halo :, inner_width:].set(edge.astype(bf16))

    def attention(projected, bias, cols, rows, *rest):
        halo_rows = halo_of(projected)
        extra = (rest[0][0], rest[0][1], rest[1:-1], rest[-1]) if rest else None
        return attend(projected, bias, cols, rows, halo_rows, extra, scale)

    def attention_back(projected, grad, probs, *rest):
        halo_rows = halo_of(projected)
        extra = (rest[0][0], rest[0][1], *rest[1:]) if rest else None
        backs = attend_back(projected, grad, probs, halo_rows, extra, scale)
        if halo:
            backs = [halo_back(backs[0], backs[-1]), *backs[1:-1]]
        return backs

    if by_chip:
        head_rows, out_rows, width = sizes
        steps.given("at", place.batch.reshape(1))
        steps.given("place", jnp.stack([place.batch, place.stretch]))

    def row(norm, kind, which):
        return norm[2 * kind + which].reshape(1, -1) if by_chip else norm[kind, which].reshape(1, -1)

    def head_step(n, hidden):
        if not by_chip:
            qkv, norm = weights[n][0], weights[n][4]
            if n == 1:
                hidden = steps.run("hid1", joined, *hidden)
            steps.run(key("head", n), lambda h, norm, w: head_in(h, norm[0, 0], norm[1, 0], w), hidden, norm, qkv)
            return hidden

        def step(at, norm, hidden, *rest):
            joins, parts = rest[:-5], rest[-5:]
            return head_by_pieces(at, head_rows, hidden, joins, row(norm, 0, 0), row(norm, 1, 0), parts)

        steps.run(key("head", n), step, "at", key("norm", n), *(hidden if n == 1 else (hidden,)), *pieces[key("A", n)])
        return ("head1", 2) if n == 1 else hidden

    hidden_at = []
    for n in range(LAYERS):
        norm = key("norm", n) if by_chip else weights[n][4]
        hidden = head_step(n, hidden)
        hidden_at.append(hidden)
        extra = (memory_at, *masks, "gate") if n == 1 else ()
        steps.run(key("att", n), attention, (key("head", n), 1), ("bias", n), "cols", "rows", *extra)
        if by_chip:
            steps.run(
                key("op", n), lambda at, a, *parts: out_by_pieces(at, head_rows, out_rows, width, a, parts),
                "at", (key("att", n), 0), *pieces[key("A", n)],
            )
        else:
            steps.run(key("op", n), out_part, (key("att", n), 0), weights[n][1])
        swap(steps, key("oswap", n), key("op", n))
        steps.run(
            key("jn", n), lambda h, own, got, norm: join_norm(h, own, got, row(norm, 0, 1), row(norm, 1, 1)),
            hidden, key("op", n), key("oswap", n), norm,
        )
        if by_chip:
            steps.run(key("ex", n), lambda at, a, *parts: by_columns(at, a, parts, True), "at", (key("jn", n), 1), *pieces[key("I", n)])
            steps.run(key("dp", n), lambda at, a, *parts: by_columns(at, a, parts, False)[0], "at", (key("ex", n), 0), *pieces[key("D", n)])
        else:
            steps.run(key("ex", n), lambda a, w: smooth_pair(nt_dot(a, w)), (key("jn", n), 1), weights[n][2])
            steps.run(key("dp", n), down_part, (key("ex", n), 0), weights[n][3])
        swap(steps, key("dswap", n), key("dp", n))
        hidden = (("jn0", 0), "dp0", "dswap0")

    def last_rows(*a):
        return place.own_blocks(joined(*a).astype(bf16))

    steps.run("last", last_rows, ("jn1", 0), "dp1", "dswap1")
    mixed_at = route_blocks(steps, place, "m", "last", True)

    norm_parts, table_parts, reduced = [None, None], [None, None], [{}, {}]
    for n in (1, 0):
        norm = key("norm", n) if by_chip else weights[n][4]
        if by_chip:
            reduced[n]["D"] = scatter_steps(steps, place, key("D", n), upstream_low, (key("ex", n), 0))
            steps.run(
                key("pg", n), lambda at, g, slope, *parts: by_rows(at, 0, parts[0].shape[0], g, parts, slope),
                "at", upstream_low, (key("ex", n), 1), *pieces[key("D", n)],
            )
            steps.run(
                key("ip", n), lambda at, g, *parts: by_rows(at, 0, parts[0].shape[0], g, parts), "at", key("pg", n), *pieces[key("I", n)]
            )
            swap(steps, key("iswap", n), key("ip", n))
            reduced[n]["I"] = scatter_steps(steps, place, key("I", n), key("pg", n), (key("jn", n), 1))
        else:
            steps.run(key("gD", n), weight_grad, upstream_low, (key("ex", n), 0))
            steps.run(key("pg", n), expand_back, upstream_low, weights[n][3], (key("ex", n), 1))
            steps.run(key("ip", n), input_part, key("pg", n), weights[n][2])
            swap(steps, key("iswap", n), key("ip", n))
            steps.run(key("gI", n), weight_grad, key("pg", n), (key("jn", n), 1))
        steps.run(
            key("jb", n), lambda up, own, got, h, norm: join_back(up, own, got, h, row(norm, 0, 1)),
            upstream, key("ip", n), key("iswap", n), (key("jn", n), 0), norm,
        )
        if by_chip:
            steps.run(
                key("ag", n), lambda at, g, *parts: attended_back(at, head_rows, out_rows, width, g, parts),
                "at", (key("jb", n), 1), *pieces[key("A", n)],
            )
        else:
            steps.run(key("ag", n), lambda g, w: nt_dot(g, w).astype(bf16), (key("jb", n), 1), weights[n][1])
        extra = (memory_at, ("att1", 2), ("att1", 3), "gate") if n == 1 else ()
        steps.run(key("ab", n), attention_back, (key("head", n), 1), key("ag", n), (key("att", n), 1), *extra)
        if by_chip:
            steps.run(
                key("iq", n), lambda at, g, *parts: by_rows(at, 0, head_rows, g, parts), "at", (key("ab", n), 0), *pieces[key("A", n)]
            )
            swap(steps, key("qswap", n), key("iq", n))
            reduced[n]["A"] = scatter_steps(
                steps, place, key("A", n), (key("ab", n), 0), (key("head", n), 0), (key("att", n), 0), (key("jb", n), 1)
            )
        else:
            steps.run(key("iq", n), input_part, (key("ab", n), 0), weights[n][0])
            swap(steps, key("qswap", n), key("iq", n))
            steps.run(key("gQ", n), weight_grad, (key("ab", n), 0), (key("head", n), 0))
            steps.run(key("gO", n), weight_grad, (key("att", n), 0), (key("jb", n), 1))
        steps.run(
            key("jk", n), lambda up, own, got, h, norm: join_back(up, own, got, h, row(norm, 0, 0)),
            (key("jb", n), 0), key("iq", n), key("qswap", n), hidden_at[n], norm,
        )
        upstream, upstream_low = (key("jk", n), 0), (key("jk", n), 1)
        norm_parts[n] = steps.run(
            key("np", n), lambda a, b, c, d: jnp.stack([jnp.stack([a[0], b[0]]), jnp.stack([c[0], d[0]])]),
            (key("jk", n), 2), (key("jb", n), 2), (key("jk", n), 3), (key("jb", n), 3),
        )
        table_parts[n] = steps.run(
            key("tp", n),
            lambda d: jnp.einsum("db,hd->bh", onehot[::-1], d[:, 0, 1 : WIN + 1], precision=highest),
            (key("ab", n), 1),
        )

    steps.run("inlast", place.own_blocks, upstream_low)
    input_at = route_blocks(steps, place, "i", "inlast", True)

    def spread(values):
        empty = jnp.zeros_like(values)
        even = jnp.where(low_core, values, empty)
        odd = jnp.where(low_core, empty, values)
        return jnp.stack([even, odd], axis=-1).reshape(-1)

    sizes = [rel_table.size, head_total, LAYERS * 4 * model_width]
    ends = np.cumsum(sizes)
    room_total = -(-int(ends[-1]) // 1024) * 1024

    def flat(lower_table, upper_table, gates, gate, lower_norm, upper_norm):
        gate_part = jnp.sum(gates[:, 0], axis=-1) * gate * (1.0 - gate)
        parts = [
            spread(jnp.stack([lower_table, upper_table])),
            spread(gate_part),
            jnp.stack([lower_norm, upper_norm]).reshape(-1) * (1.0 / CORES),
        ]
        return jnp.concatenate(parts + [jnp.zeros((room_total - int(ends[-1]),), f32)]).reshape(-1, 128)

    sums = steps.run("sums", flat, table_parts[0], table_parts[1], ("ab1", 2), "gate", norm_parts[0], norm_parts[1])
    links = {(SEG, 1): "core", (BAT, 1): "x", (BAT, 2): "y"}
    for axis, count in ((SEG, place.segments), (BAT, place.batches)):
        bit = 1
        while bit < count:
            got = steps.send(
                key("u", axis[0], bit), links.get((axis, bit), "z"), lambda v, axis=axis, bit=bit: permuted(v, axis, lambda i: i ^ bit), sums
            )
            sums = steps.run(key("v", axis[0], bit), jnp.add, sums, got)
            bit *= 2

    if by_chip:
        done = {kind: finish_steps(steps, place, kind, reduced[0][kind], reduced[1][kind]) for kind in "DIA"}

    steps.carry_out(ORDER if by_chip and ORDER else range(len(steps.steps)))

    final = steps.value(sums).reshape(-1)
    table_sum = final[: ends[0]].reshape(rel_table.shape)
    gate_sum = final[ends[0] : ends[1]]
    norm_sum = final[ends[1] : ends[2]].reshape(LAYERS, 2, 2, place.chips, place.batches, norm_gain.shape[2])
    norm_sum = jnp.where(low_core, norm_sum[0], norm_sum[1])
    norm_sum = lax.dynamic_index_in_dim(norm_sum, place.stretch, 2, keepdims=False)
    norm_sum = lax.dynamic_index_in_dim(norm_sum, place.batch, 2, keepdims=False)
    if by_chip:
        halves = {kind: steps.value(name) for kind, name in done.items()}
        head = qkv_weight.shape[2] // 2
        matrices = [
            qkv_whole([h[:head] for h in halves["A"]])[None],
            out_whole([h[head:] for h in halves["A"]])[None],
            in_whole(halves["I"], 1)[None],
            down_whole(halves["D"], 1)[None],
        ]
    else:
        parts = [[steps.value(key("g", kind, n)) for kind in "QOID"] for n in range(LAYERS)]
        matrices = scatter_plain(parts, place.core)
    return (
        steps.value(mixed_at), steps.value(input_at), *matrices, norm_sum[0][None], norm_sum[1][None], table_sum, gate_sum,
    )


ORDER = (
    54, 0, 1, 56, 57, 58, 59, -2, 2, 60, -58, 3, 55, 70, 85, 75, 81, -60, 76, 73, 53, -4, 4, 83, 71, 80, -77, 72, -5,
    5, -73, 20, -6, 61, 6, 8, 7, -21, 21, -62, 74, 62, 63, 64, -65, 65, 66, -22, 12, 67, -75, 22, -9, 9, -8, -13, 10,
    13, 68, -23, 28, 23, -14, 24, -10, 25, 14, 69, -11, 11, 77, 78, -29, 29, -15, 37, -79, 15, 17, 79, 90, -25, 16,
    91, -26, -30, -38, 27, 30, 26, 92, -18, 93, -31, 82, -17, -94, 18, 19, -28, 45, 31, -27, -83, -46, 32, 33, 46,
    -19, 84, -20, 94, 95, -47, 38, 96, -33, -85, 35, -34, -39, 39, 34, 97, 86, -98, -40, 47, 40, 42, -36, -87, 41, 87,
    -35, 88, 36, 98, -48, -89, 48, 49, 50, 99, -43, -42, 44, 43, 100, 101, 89, -50, -51, 52, -102, 51, 102, -45, -44,
    103, -53, -52, 104, 105, 130, -106, 133, 135, 134, 131, 132, 115, 117, 116, -136, -133, 148, -135, 136, 138, 137,
    139, -118, 118, -117, 120, 119, 121, 106, 110, 111, 112, 108, 107, 149, 150, -139, -140, -112, 113, 109, 151,
    -121, -122, 152, 153, 155, 154, -153, 168, -114, -110, 170, 171, 173, 172, -156, 140, -155, 157, 159, 141, 142,
    156, 158, -174, -173, 174, 176, -143, 143, 144, 186, -145, 145, 146, 189, 191, -160, 122, -147, 147, 123, 124,
    175, 177, 187, -192, -125, 188, 125, 126, 192, -159, 194, -189, 160, -177, -127, 190, 161, 162, 127, 128, 204,
    -178, 205, 178, -163, 179, -129, 180, 163, 164, 206, -191, -181, 181, 182, -165, 209, -195, 211, 210, 165, 166,
    207, -183, 208, 183, 184, 193, -167, 195, -212, -209, 224, -211, -185, 227, 212, 214, 231, 232, 213, 215, 167,
    185, 228, 225, 233, 234, 229, 226, -233, 230, -196, 196, 197, 169, 236, -235, 237, 198, -215, 129, -238, 238,
    -231, 239, 235, 114, 247, -240, 248, 240, 241, -199, 199, -216, -249, 200, 216, -242, 217, 218, 242, 243, 249,
    -201, 201, 202, -244, 244, 245, -219, 219, 220, -246, 246, -203, 203, 250, 251, -221, 221, 222, -252, 252, -223,
    223, 253, 254, -255, 255,
)


def solution(mesh):
    placed = (
        P(BAT, SEG, None),
        P(BAT, None),
        P(BAT, SEG, None, None),
        P(SEG, None),
        P(SEG, None),
        P(SEG, None, BAT),
        P(SEG, None, BAT),
        P(SEG, None, BAT),
        P(SEG, None, BAT),
        P(SEG, None, BAT),
        P(SEG, None, BAT),
        P(),
        P(),
        P(BAT, SEG, None),
    )
    return jax.shard_map(
        on_device,
        mesh=mesh,
        in_specs=placed,
        out_specs=(
            P(BAT, SEG, None),
            P(BAT, SEG, None),
            P(SEG, None, BAT),
            P(SEG, None, BAT),
            P(SEG, None, BAT),
            P(SEG, None, BAT),
            P(SEG, None, BAT),
            P(SEG, None, BAT),
            P(),
            P(),
        ),
        check_vma=False,
    )
```

time: 1040 us -> 774 us (0.74)
  Pallas kernels: 84.8 us -> 268 us
  matrix products: 148 us -> 0.45 us
  waiting for transfers between devices: 307 us -> 220 us
  blocking collectives: 81.9 us -> 0 us
  starting transfers between devices: 202 us -> 138 us
  other arithmetic: 102 us -> 41.9 us
  between operations: 17.9 us -> 4.69 us
    pallas_call x1 -> x52, Pallas kernels: 26.4 us -> 216 us  [in_vmem(): pl.pallas_call(kernel, out_shape=outs, in_specs=([smem_block] if scalars...]
    dot_general x27 -> x3, matrix products: 148 us -> 0.45 us  [the longest x2 0.29 us: on_device(): jnp.einsum('db,hd->bh', onehot[::-1], d[:, 0, 1:WIN + 1], precision=highest)]
    ppermute x151 -> x104, waiting for transfers between devices: 307 us -> 195 us  [permuted(): return lax.ppermute(block, axis, [(i, route(i)) for i in range(count)])]
    ppermute x151 -> x104, starting transfers between devices: 202 us -> 120 us  [permuted(): return lax.ppermute(block, axis, [(i, route(i)) for i in range(count)])]
    all_gather x1 -> x0, blocking collectives: 42.5 us -> none  [on_device(): lax.all_gather(norm_rows, ('batch', 'segment'), axis=0, tiled=False)]
    unnamed x282 -> x392, local copies, waits for them, and re-layouts: 9.6 us -> 50.4 us
    psum x1 -> x0, blocking collectives: 39.4 us -> none  [on_device(): lax.psum((spread(jnp.stack(table_grads)), spread(gate_part), jnp.stack(no...]
    ppermute x0 -> x15, waiting for transfers between devices: none -> 25.4 us  [route_blocks(): lax.ppermute(v, SEG, route)]
  transfers between devices with their start and end apart: 152 -> 119, of which waited for: 56 -> 42; matrix products, arithmetic and copies ran while one was open for 26% -> 11% of each run, Pallas kernels for 8% -> 31%
where the time goes in v2:
time: 774 us; the launch traced here: 765 us
  Pallas kernels  268 us (35%)
  waiting for transfers between devices  220 us (28%)
  starting transfers between devices  138 us (18%)
  local copies, waits for them, and re-layouts  91.3 us (12%)
  other arithmetic  41.9 us (5%)
    pallas_call x52, Pallas kernels, in_vmem(): pl.pallas_call(kernel, out_shape=outs, in_specs=([smem_block] if scalars...  216 us
    ppermute x104, waiting for transfers between devices, permuted(): return lax.ppermute(block, axis, [(i, route(i)) for i in range(count)])  195 us
    ppermute x104, starting transfers between devices, permuted(): return lax.ppermute(block, axis, [(i, route(i)) for i in range(count)])  120 us
    unnamed x392, local copies, waits for them, and re-layouts  50.4 us
    pallas_call x2, Pallas kernels, attend(): pl.pallas_call(functools.partial(forward_kernel, halo, memory is not None...  27 us
    ppermute x15, waiting for transfers between devices, route_blocks(): lax.ppermute(v, SEG, route)  25.4 us
    pallas_call x2, Pallas kernels, attend_back(): pl.pallas_call(functools.partial(backward_kernel, halo, memory is not Non...  25.3 us
    ppermute x15, starting transfers between devices, route_blocks(): lax.ppermute(v, SEG, route)  18.1 us
  transfers between devices with their start and end apart: 119, of which 42 were waited for; matrix products, arithmetic and copies ran while one was open for 11% of the time, Pallas kernels for 31%

profile of v2, /device:TPU:1, one launch (start us, length us, event | category | flops | bytes accessed | tf_op | source)
XLA Modules:
  0.0 764.6 jit_solution(3871083391895580613)
XLA Ops:
  40.5 9.3 %collective-permute-done.6 = bf16[528,256]{1,0:T(8,128)(2,1)S(1)} collective-permute-done((bf16[528,256]{1,0:T(8,128)(2,1)}, bf16[528,256]{1,0:T(8,128)(2,1)S(1)}, u32[]{:S(2)}, u32[]{:S(2)}) %collective-permute-start.6) | collective-permute-done | bytes 270368 | tf_op jit(solution)/shard_map/z2A0/ppermute | solution.py:29
  55.4 8.4 %collective-permute-done.8 = bf16[528,256]{1,0:T(8,128)(2,1)S(1)} collective-permute-done((bf16[528,256]{1,0:T(8,128)(2,1)S(1)}, bf16[528,256]{1,0:T(8,128)(2,1)S(1)}, u32[]{:S(2)}, u32[]{:S(2)}) %collective-permute-start.8) | collective-permute-done | bytes 270368 | tf_op jit(solution)/shard_map/z3A0/ppermute | solution.py:29
  75.9 7.3 collective-permute-start.11
  84.5 6.4 slot_mask.4
  151.2 10.5 %attend.2 = (bf16[1024,512]{1,0:T(8,128)(2,1)S(1)}, bf16[4,1024,768]{2,1,0:T(8,128)(2,1)S(1)}) custom-call(f32[4,1,1024]{2,1,0:T(1,128)S(1)} %get-tuple-element.1131.refs_0_, s32[1024,1]{1,0:T(8,128)S(1)} %copy-done.34, s32[1,1024]{1,0:T(1,128)S(1)} %constant_dynamic-slice_fusion.2.refs_2_, ...), custom_call_target="tpu_custom_call" | custom-call | flops 1610612736 | bytes 16777216 | tf_op jit(solution)/shard_map/att0/attend/pallas_call | solution.py:775
  170.9 12.7 %collective-permute-done.28.refs_2_ = bf16[512,1024]{1,0:T(8,128)(2,1)S(1)} collective-permute-done((bf16[512,1024]{1,0:T(8,128)(2,1)S(1)}, bf16[512,1024]{1,0:T(8,128)(2,1)S(1)}, u32[]{:S(2)}, u32[]{:S(2)}) %collective-permute-start.28) | collective-permute-done | bytes 1048608 | tf_op jit(solution)/shard_map/pyI0/ppermute | solution.py:29
  183.6 9.4 %collective-permute-start.30 = (bf16[1024,1024]{1,0:T(8,128)(2,1)S(1)}, bf16[1024,1024]{1,0:T(8,128)(2,1)S(1)}, u32[]{:S(2)}, u32[]{:S(2)}) collective-permute-start(bf16[1024,1024]{1,0:T(8,128)(2,1)S(1)} %out.2.own_ref), channel_id=1, source_target_pairs={{0,1},{1,0},{2,3},{3,2},{4,5},{5,4},{6,7},{7,6},{8,9},{9,8},{10,11... | collective-permute-start | bytes 6291464 | tf_op jit(solution)/shard_map/oswap0/ppermute | solution.py:29
  209.7 8.0 %collective-permute-done.37.refs_3_ = bf16[256,1024]{1,0:T(8,128)(2,1)S(1)} collective-permute-done((bf16[256,1024]{1,0:T(8,128)(2,1)S(1)}, bf16[256,1024]{1,0:T(8,128)(2,1)S(1)}, u32[]{:S(2)}, u32[]{:S(2)}) %collective-permute-start.37) | collective-permute-done | bytes 524320 | tf_op jit(solution)/shard_map/fxI0/ppermute | solution.py:29
  220.7 9.1 %expand.2 = (bf16[1024,2048]{1,0:T(8,128)(2,1)S(1)}, bf16[1024,2048]{1,0:T(8,128)(2,1)S(1)}) custom-call(s32[1]{0:T(128)} %bitcast.at_ref, bf16[1024,1024]{1,0:T(8,128)(2,1)S(1)} %get-tuple-element.1818.rows_ref.refs_1_, bf16[512,1024]{1,0:T(8,128)(2,1)S(1)} %copy-done.39, bf16[512,1024]{1,0:T(8,128)(2,1)S(1)} %collective-permute-done.31.refs_1_, ...), custom_call_target="tpu_custom_call" | custom-call | flops 12884901888 | tf_op jit(solution)/shard_map/ex0/expand/pallas_call | solution.py:417
  234.4 8.3 %down.2.refs_1_ = bf16[1024,1024]{1,0:T(8,128)(2,1)S(1)} custom-call(s32[1]{0:T(128)} %bitcast.at_ref, bf16[1024,2048]{1,0:T(8,128)(2,1)S(1)} %get-tuple-element.1690.rows_ref.refs_1_, bf16[256,2048]{1,0:T(8,128)(2,1)} %constant_dynamic-update-slice_fusion.18.refs_0_, bf16[256,2048]{1,0:T(8,128)(2,1)} %collective-permute-done.25.refs_1_, ...), custom_call_target="tpu_custom_call" | custom-call | flops 12884901888 | tf_op jit(solution)/shard_map/dp0/down/pallas_call | solution.py:417
  242.7 8.9 %collective-permute-done.40 = bf16[128,1024]{1,0:T(8,128)(2,1)S(1)} collective-permute-done((bf16[128,1024]{1,0:T(8,128)(2,1)S(1)}, bf16[128,1024]{1,0:T(8,128)(2,1)S(1)}, u32[]{:S(2)}, u32[]{:S(2)}) %collective-permute-start.40) | collective-permute-done | bytes 262176 | tf_op jit(solution)/shard_map/c2/ppermute | solution.py:952
  256.5 10.5 %collective-permute-done.45 = bf16[512,256]{1,0:T(8,128)(2,1)S(1)} collective-permute-done((bf16[512,256]{1,0:T(8,128)(2,1)S(1)}, bf16[512,256]{1,0:T(8,128)(2,1)S(1)}, u32[]{:S(2)}, u32[]{:S(2)}) %collective-permute-start.45) | collective-permute-done | bytes 262176 | tf_op jit(solution)/shard_map/z3I1/ppermute | solution.py:29
  273.7 6.7 head.3
  295.1 16.5 %attend.3 = (bf16[1024,512]{1,0:T(8,128)(2,1)S(1)}, bf16[4,1024,768]{2,1,0:T(8,128)(2,1)S(1)}, bf16[4,1024,256]{2,1,0:T(8,128)(2,1)S(1)}, bf16[1024,512]{1,0:T(8,128)(2,1)S(1)}) custom-call(f32[4,1,1024]{2,1,0:T(1,128)S(1)} %get-tuple-element.1298.refs_0_, s32[1024,1]{1,0:T(8,128)S(1)} %copy-done.33, s32[1,1024]{1,0:T(1,128)S(1)} %constant_dynamic-slice_fusion.2.refs_2_, ...), custom_call_target="tpu_custom_call" | custom-call | flops 2147483648 | bytes 16777216 | tf_op jit(solution)/shard_map/att1/attend/pallas_call | solution.py:775
  330.7 10.9 %expand.3 = (bf16[1024,2048]{1,0:T(8,128)(2,1)S(1)}, bf16[1024,2048]{1,0:T(8,128)(2,1)S(1)}) custom-call(s32[1]{0:T(128)} %bitcast.at_ref, bf16[1024,1024]{1,0:T(8,128)(2,1)S(1)} %get-tuple-element.1543.rows_ref.refs_1_, bf16[512,1024]{1,0:T(8,128)(2,1)} %pad_maximum_fusion.7.refs_0_, bf16[512,1024]{1,0:T(8,128)(2,1)} %collective-permute-done.49.refs_1_, ...), custom_call_target="tpu_custom_call" | custom-call | flops 12884901888 | tf_op jit(solution)/shard_map/ex1/expand/pallas_call | solution.py:417
  343.6 9.8 %down.3 = bf16[1024,1024]{1,0:T(8,128)(2,1)S(1)} custom-call(s32[1]{0:T(128)} %bitcast.at_ref, bf16[1024,2048]{1,0:T(8,128)(2,1)S(1)} %get-tuple-element.1606.rows_ref.refs_1_, bf16[256,2048]{1,0:T(8,128)(2,1)} %constant_dynamic-update-slice_fusion.58.refs_0_, bf16[256,2048]{1,0:T(8,128)(2,1)} %collective-permute-done.53.refs_1_, ...), custom_call_target="tpu_custom_call" | custom-call | flops 12884901888 | tf_op jit(solution)/shard_map/dp1/down/pallas_call | solution.py:417
  353.4 8.1 %by_rows.6.refs_0_.rows_ref = bf16[1024,2048]{1,0:T(8,128)(2,1)S(1)} custom-call(s32[1]{0:T(128)} %bitcast.at_ref, bf16[1024,1024]{1,0:T(8,128)(2,1)S(1)} %bitcast.334, bf16[256,2048]{1,0:T(8,128)(2,1)} %constant_dynamic-update-slice_fusion.58.refs_0_, bf16[256,2048]{1,0:T(8,128)(2,1)} %collective-permute-done.53.refs_1_, ...), custom_call_target="tpu_custom_call" | custom-call | flops 12884901888 | tf_op jit(solution)/shard_map/pg1/by_rows/pallas_call | solution.py:417
  370.2 7.0 by_rows.7.own_ref
  384.3 6.4 collective-permute-done.63.refs_2_
  424.2 14.3 %attend_back.2 = (bf16[1024,1536]{1,0:T(8,128)(2,1)S(1)}, f32[4,1,1024]{2,1,0:T(1,128)S(1)}, f32[4,1,128]{2,1,0:T(1,128)S(1)}) custom-call(bf16[1024,1536]{1,0:T(8,128)(2,1)S(1)} %copy-done.3, bf16[1024,1536]{1,0:T(8,128)(2,1)S(1)} %copy-done.3, bf16[1024,1536]{1,0:T(8,128)(2,1)S(1)} %copy-done.3, bf16[1024,512]{1,0:T(8,128)(2,1)S(1)} %attended_back.2.refs_3_, ...), custom_call_target="tpu_custom_call" | custom-call | flops 3758096384 | bytes 20971520 | tf_op jit(solution)/shard_map/ab1/attend_back/pallas_call | solution.py:831
  441.5 18.8 %collective-permute-done.66.refs_2_ = bf16[512,1024]{1,0:T(8,128)(2,1)S(1)} collective-permute-done((bf16[512,1024]{1,0:T(8,128)(2,1)S(1)}, bf16[512,1024]{1,0:T(8,128)(2,1)S(1)}, u32[]{:S(2)}, u32[]{:S(2)}) %collective-permute-start.66) | collective-permute-done | bytes 1048608 | tf_op jit(solution)/shard_map/sxI1/ppermute | solution.py:29
  460.3 23.1 %collective-permute-done.65.refs_3_ = bf16[512,1024]{1,0:T(8,128)(2,1)S(1)} collective-permute-done((bf16[512,1024]{1,0:T(8,128)(2,1)S(1)}, bf16[512,1024]{1,0:T(8,128)(2,1)S(1)}, u32[]{:S(2)}, u32[]{:S(2)}) %collective-permute-start.65) | collective-permute-done | bytes 1048608 | tf_op jit(solution)/shard_map/syI1/ppermute | solution.py:29
  523.6 9.4 %collective-permute-done.75.refs_2_ = bf16[128,2048]{1,0:T(8,128)(2,1)S(1)} collective-permute-done((bf16[128,2048]{1,0:T(8,128)(2,1)S(1)}, bf16[128,2048]{1,0:T(8,128)(2,1)S(1)}, u32[]{:S(2)}, u32[]{:S(2)}) %collective-permute-start.75) | collective-permute-done | bytes 524320 | tf_op jit(solution)/shard_map/ryD0/ppermute | solution.py:29
  536.7 8.3 %by_rows.9.refs_0_.rows_ref = bf16[1024,2048]{1,0:T(8,128)(2,1)S(1)} custom-call(s32[1]{0:T(128)} %bitcast.at_ref, bf16[1024,1024]{1,0:T(8,128)(2,1)S(1)} %get-tuple-element.1689.refs_0_.rows_ref, bf16[256,2048]{1,0:T(8,128)(2,1)} %constant_dynamic-update-slice_fusion.18.refs_0_, bf16[256,2048]{1,0:T(8,128)(2,1)} %collective-permute-done.25.refs_1_, ...), custom_call_target="tpu_custom_call" | custom-call | flops 12884901888 | tf_op jit(solution)/shard_map/pg0/by_rows/pallas_call | solution.py:417
  545.6 6.4 collective-permute-done.78
  573.3 7.6 collective-permute-start.82
  601.9 7.2 collective-permute-done.87
  609.8 11.0 %attend_back.3 = (bf16[1024,1536]{1,0:T(8,128)(2,1)S(1)}, f32[4,1,1024]{2,1,0:T(1,128)S(1)}) custom-call(bf16[1024,1536]{1,0:T(8,128)(2,1)S(1)} %get-tuple-element.1703.refs_3_.refs_4_.refs_5_.refs_0_.refs_1_.refs_2_, bf16[1024,1536]{1,0:T(8,128)(2,1)S(1)} %get-tuple-element.1703.refs_3_.refs_4_.refs_5_.refs_0_.refs_1_.refs_2_, ...), custom_call_target="tpu_custom_call" | custom-call | flops 3221225472 | bytes 20971520 | tf_op jit(solution)/shard_map/ab0/attend_back/pallas_call | solution.py:831
  649.0 7.8 %join_back.7 = (f32[1024,1024]{1,0:T(8,128)}, bf16[1024,1024]{1,0:T(8,128)(2,1)S(1)}, f32[1,1024]{1,0:T(1,128)S(1)}, f32[1,1024]{1,0:T(1,128)S(1)}) custom-call(f32[1024,1024]{1,0:T(8,128)S(1)} %copy-done.18, bf16[1024,1024]{1,0:T(8,128)(2,1)S(1)} %by_rows.11.own_ref, bf16[1024,1024]{1,0:T(8,128)(2,1)} %collective-permute-done.94.got_ref, ...), custom_call_target="tpu_custom_call" | custom-call | flops 62914560 | tf_op jit(solution)/shard_map/jk0/join_back/pallas_call | solution.py:417
  688.1 9.3 %collective-permute-done.104.refs_4_ = bf16[512,1024]{1,0:T(8,128)(2,1)} collective-permute-done((bf16[512,1024]{1,0:T(8,128)(2,1)}, bf16[512,1024]{1,0:T(8,128)(2,1)}, u32[]{:S(2)}, u32[]{:S(2)}) %collective-permute-start.104) | collective-permute-done | bytes 1048608 | tf_op jit(solution)/shard_map/sxA0/ppermute | solution.py:29
  717.6 11.3 %collective-permute-done.112 = bf16[512,256]{1,0:T(8,128)(2,1)S(1)} collective-permute-done((bf16[512,256]{1,0:T(8,128)(2,1)S(1)}, bf16[512,256]{1,0:T(8,128)(2,1)S(1)}, u32[]{:S(2)}, u32[]{:S(2)}) %collective-permute-start.112) | collective-permute-done | bytes 262176 | tf_op jit(solution)/shard_map/q2I0/ppermute | solution.py:29
  748.4 7.6 collective-permute-done.116
  (864 shorter events, 443.8 us)
Async XLA Ops:
  65.1 35.4 %collective-permute-start.16 = (bf16[528,1024]{1,0:T(8,128)(2,1)S(1)}, bf16[528,1024]{1,0:T(8,128)(2,1)S(1)}, u32[]{:S(2)}, u32[]{:S(2)}) collective-permute-start(bf16[528,1024]{1,0:T(8,128)(2,1)S(1)} %pad_maximum_fusion.3.own_ref.refs_3_.refs_0_), channel_id=1, source_target_pairs={{0,16},{8,24},{16,0},{24,8},{1,17},{9,25},{17,1},{25,9},{2,18},{10... | collective-permute-start | bytes 3244040 | tf_op jit(solution)/shard_map/pyA0/ppermute | solution.py:29
  66.3 34.1 %collective-permute-start.15 = (bf16[528,1024]{1,0:T(8,128)(2,1)S(1)}, bf16[528,1024]{1,0:T(8,128)(2,1)S(1)}, u32[]{:S(2)}, u32[]{:S(2)}) collective-permute-start(bf16[528,1024]{1,0:T(8,128)(2,1)S(1)} %pad_maximum_fusion.3.own_ref.refs_3_.refs_0_), channel_id=1, source_target_pairs={{0,8},{8,0},{16,24},{24,16},{1,9},{9,1},{17,25},{25,17},{2,10},{10... | collective-permute-start | bytes 3244040 | tf_op jit(solution)/shard_map/pxA0/ppermute | solution.py:29
  74.8 22.6 %collective-permute-start.12 = (bf16[128,1024]{1,0:T(8,128)(2,1)S(1)}, bf16[128,1024]{1,0:T(8,128)(2,1)S(1)}, u32[]{:S(2)}, u32[]{:S(2)}) collective-permute-start(bf16[128,1024]{1,0:T(8,128)(2,1)S(1)} %dynamic-slice_bitcast_fusion.11), channel_id=1, source_target_pairs={{0,4},{1,5},{2,6},{3,7},{4,0},{5,1},{6,2},{7,3},{8,12},{9,13},{10,... | collective-permute-start | bytes 786440 | tf_op jit(solution)/shard_map/t2/ppermute | solution.py:952
  116.7 32.4 %collective-permute-start.25 = (bf16[256,2048]{1,0:T(8,128)(2,1)}, bf16[256,2048]{1,0:T(8,128)(2,1)}, u32[]{:S(2)}, u32[]{:S(2)}) collective-permute-start(bf16[256,2048]{1,0:T(8,128)(2,1)} %constant_dynamic-update-slice_fusion.18.refs_0_), channel_id=1, source_target_pairs={{0,8},{8,0},{16,24},{24,16},{1,9},{9,1},{17,25},{25,17},{2,10},{10... | collective-permute-start | bytes 3145736 | tf_op jit(solution)/shard_map/pxD0/ppermute | solution.py:29
  128.1 33.6 %collective-permute-start.22 = (bf16[256,2048]{1,0:T(8,128)(2,1)}, bf16[256,2048]{1,0:T(8,128)(2,1)}, u32[]{:S(2)}, u32[]{:S(2)}) collective-permute-start(bf16[256,2048]{1,0:T(8,128)(2,1)} %constant_dynamic-update-slice_fusion.18.refs_0_), channel_id=1, source_target_pairs={{0,16},{8,24},{16,0},{24,8},{1,17},{9,25},{17,1},{25,9},{2,18},{10... | collective-permute-start | bytes 3145736 | tf_op jit(solution)/shard_map/pyD0/ppermute | solution.py:29
  129.7 32.1 %collective-permute-start.21 = (bf16[784,256]{1,0:T(8,128)(2,1)}, bf16[784,256]{1,0:T(8,128)(2,1)}, u32[]{:S(2)}, u32[]{:S(2)}) collective-permute-start(bf16[784,256]{1,0:T(8,128)(2,1)} %collective-permute-done.17), channel_id=1, source_target_pairs={{0,2},{1,3},{2,4},{3,5},{4,6},{5,7},{6,0},{7,1},{8,10},{9,11},{10,... | collective-permute-start | bytes 1204232 | tf_op jit(solution)/shard_map/z2A1/ppermute | solution.py:29
  137.1 24.7 %collective-permute-start.26 = (bf16[512,256]{1,0:T(8,128)(2,1)S(1)}, bf16[512,256]{1,0:T(8,128)(2,1)}, u32[]{:S(2)}, u32[]{:S(2)}) collective-permute-start(bf16[512,256]{1,0:T(8,128)(2,1)S(1)} %copy-done.148), channel_id=1, source_target_pairs={{0,2},{1,3},{2,4},{3,5},{4,6},{5,7},{6,0},{7,1},{8,10},{9,11},{10,... | collective-permute-start | bytes 786440 | tf_op jit(solution)/shard_map/z1I1/ppermute | solution.py:29
  166.4 39.5 %collective-permute-start.34 = (bf16[128,2048]{1,0:T(8,128)(2,1)S(1)}, bf16[128,2048]{1,0:T(8,128)(2,1)S(1)}, u32[]{:S(2)}, u32[]{:S(2)}) collective-permute-start(bf16[128,2048]{1,0:T(8,128)(2,1)S(1)} %slice.567), channel_id=1, source_target_pairs={{0,8},{8,0},{16,24},{24,16},{1,9},{9,1},{17,25},{25,17},{2,10},{10... | collective-permute-start | bytes 1572872 | tf_op jit(solution)/shard_map/fxD0/ppermute | solution.py:29
  167.4 29.4 %collective-permute-start.29 = (bf16[128,2048]{1,0:T(8,128)(2,1)S(1)}, bf16[128,2048]{1,0:T(8,128)(2,1)S(1)}, u32[]{:S(2)}, u32[]{:S(2)}) collective-permute-start(bf16[128,2048]{1,0:T(8,128)(2,1)S(1)} %slice.562), channel_id=1, source_target_pairs={{0,16},{8,24},{16,0},{24,8},{1,17},{9,25},{17,1},{25,9},{2,18},{10... | collective-permute-start | bytes 1572872 | tf_op jit(solution)/shard_map/fyD0/ppermute | solution.py:29
  208.0 43.6 %collective-permute-start.39 = (bf16[528,1024]{1,0:T(8,128)(2,1)S(1)}, bf16[528,1024]{1,0:T(8,128)(2,1)S(1)}, u32[]{:S(2)}, u32[]{:S(2)}) collective-permute-start(bf16[528,1024]{1,0:T(8,128)(2,1)S(1)} %pad_maximum_fusion.4.own_ref.refs_5_.refs_0_), channel_id=1, source_target_pairs={{0,16},{8,24},{16,0},{24,8},{1,17},{9,25},{17,1},{25,9},{2,18},{10... | collective-permute-start | bytes 3244040 | tf_op jit(solution)/shard_map/pyA1/ppermute | solution.py:29
  208.6 34.1 %collective-permute-start.35 = (bf16[528,1024]{1,0:T(8,128)(2,1)S(1)}, bf16[528,1024]{1,0:T(8,128)(2,1)S(1)}, u32[]{:S(2)}, u32[]{:S(2)}) collective-permute-start(bf16[528,1024]{1,0:T(8,128)(2,1)S(1)} %pad_maximum_fusion.4.own_ref.refs_5_.refs_0_), channel_id=1, source_target_pairs={{0,8},{8,0},{16,24},{24,16},{1,9},{9,1},{17,25},{25,17},{2,10},{10... | collective-permute-start | bytes 3244040 | tf_op jit(solution)/shard_map/pxA1/ppermute | solution.py:29
  209.0 22.8 %collective-permute-start.38 = (bf16[512,256]{1,0:T(8,128)(2,1)S(1)}, bf16[512,256]{1,0:T(8,128)(2,1)S(1)}, u32[]{:S(2)}, u32[]{:S(2)}) collective-permute-start(bf16[512,256]{1,0:T(8,128)(2,1)S(1)} %collective-permute-done.32), channel_id=1, source_target_pairs={{0,2},{1,3},{2,4},{3,5},{4,6},{5,7},{6,0},{7,1},{8,10},{9,11},{10,... | collective-permute-start | bytes 786440 | tf_op jit(solution)/shard_map/z2D1/ppermute | solution.py:29
  271.3 40.3 %collective-permute-start.49 = (bf16[512,1024]{1,0:T(8,128)(2,1)}, bf16[512,1024]{1,0:T(8,128)(2,1)}, u32[]{:S(2)}, u32[]{:S(2)}) collective-permute-start(bf16[512,1024]{1,0:T(8,128)(2,1)} %pad_maximum_fusion.7.refs_0_), channel_id=1, source_target_pairs={{0,8},{8,0},{16,24},{24,16},{1,9},{9,1},{17,25},{25,17},{2,10},{10... | collective-permute-start | bytes 3145736 | tf_op jit(solution)/shard_map/pxI1/ppermute | solution.py:29
  272.2 39.4 %collective-permute-start.50 = (bf16[512,1024]{1,0:T(8,128)(2,1)}, bf16[512,1024]{1,0:T(8,128)(2,1)}, u32[]{:S(2)}, u32[]{:S(2)}) collective-permute-start(bf16[512,1024]{1,0:T(8,128)(2,1)} %pad_maximum_fusion.7.refs_0_), channel_id=1, source_target_pairs={{0,16},{8,24},{16,0},{24,8},{1,17},{9,25},{17,1},{25,9},{2,18},{10... | collective-permute-start | bytes 3145736 | tf_op jit(solution)/shard_map/pyI1/ppermute | solution.py:29
  289.7 32.5 %collective-permute-start.53 = (bf16[256,2048]{1,0:T(8,128)(2,1)}, bf16[256,2048]{1,0:T(8,128)(2,1)}, u32[]{:S(2)}, u32[]{:S(2)}) collective-permute-start(bf16[256,2048]{1,0:T(8,128)(2,1)} %constant_dynamic-update-slice_fusion.58.refs_0_), channel_id=1, source_target_pairs={{0,8},{8,0},{16,24},{24,16},{1,9},{9,1},{17,25},{25,17},{2,10},{10... | collective-permute-start | bytes 3145736 | tf_op jit(solution)/shard_map/pxD1/ppermute | solution.py:29
  290.1 32.2 %collective-permute-start.52 = (bf16[256,2048]{1,0:T(8,128)(2,1)}, bf16[256,2048]{1,0:T(8,128)(2,1)}, u32[]{:S(2)}, u32[]{:S(2)}) collective-permute-start(bf16[256,2048]{1,0:T(8,128)(2,1)} %constant_dynamic-update-slice_fusion.58.refs_0_), channel_id=1, source_target_pairs={{0,16},{8,24},{16,0},{24,8},{1,17},{9,25},{17,1},{25,9},{2,18},{10... | collective-permute-start | bytes 3145736 | tf_op jit(solution)/shard_map/pyD1/ppermute | solution.py:29
  381.5 28.5 %collective-permute-start.59 = (bf16[128,2048]{1,0:T(8,128)(2,1)S(1)}, bf16[128,2048]{1,0:T(8,128)(2,1)S(1)}, u32[]{:S(2)}, u32[]{:S(2)}) collective-permute-start(bf16[128,2048]{1,0:T(8,128)(2,1)S(1)} %get-tuple-element.1407), channel_id=1, source_target_pairs={{0,8},{8,0},{16,24},{24,16},{1,9},{9,1},{17,25},{25,17},{2,10},{10... | collective-permute-start | bytes 1572872 | tf_op jit(solution)/shard_map/rxD1/ppermute | solution.py:29
  382.7 23.8 %collective-permute-start.60 = (bf16[128,2048]{1,0:T(8,128)(2,1)S(1)}, bf16[128,2048]{1,0:T(8,128)(2,1)S(1)}, u32[]{:S(2)}, u32[]{:S(2)}) collective-permute-start(bf16[128,2048]{1,0:T(8,128)(2,1)S(1)} %get-tuple-element.1408), channel_id=1, source_target_pairs={{0,16},{8,24},{16,0},{24,8},{1,17},{9,25},{17,1},{25,9},{2,18},{10... | collective-permute-start | bytes 1572872 | tf_op jit(solution)/shard_map/ryD1/ppermute | solution.py:29
  419.6 63.8 %collective-permute-start.64 = (bf16[128,1024]{1,0:T(8,128)(2,1)S(1)}, bf16[128,1024]{1,0:T(8,128)(2,1)S(1)}, u32[]{:S(2)}, u32[]{:S(2)}) collective-permute-start(bf16[128,1024]{1,0:T(8,128)(2,1)S(1)} %dynamic-slice_bitcast_fusion.7), channel_id=1, source_target_pairs={{4,0},{5,1},{6,2},{7,3},{0,4},{1,5},{2,6},{3,7},{12,8},{13,9},{14,... | collective-permute-start | bytes 786440 | tf_op jit(solution)/shard_map/m2/ppermute | solution.py:952
  438.5 21.8 %collective-permute-start.66 = (bf16[512,1024]{1,0:T(8,128)(2,1)S(1)}, bf16[512,1024]{1,0:T(8,128)(2,1)S(1)}, u32[]{:S(2)}, u32[]{:S(2)}) collective-permute-start(bf16[512,1024]{1,0:T(8,128)(2,1)S(1)} %copy-done.91), channel_id=1, source_target_pairs={{0,8},{8,0},{16,24},{24,16},{1,9},{9,1},{17,25},{25,17},{2,10},{10... | collective-permute-start | bytes 3145736 | tf_op jit(solution)/shard_map/sxI1/ppermute | solution.py:29
  439.5 49.0 %collective-permute-start.69 = (bf16[256,2048]{1,0:T(8,128)(2,1)S(1)}, bf16[256,2048]{1,0:T(8,128)(2,1)S(1)}, u32[]{:S(2)}, u32[]{:S(2)}) collective-permute-start(bf16[256,2048]{1,0:T(8,128)(2,1)S(1)} %copy-done.87), channel_id=1, source_target_pairs={{0,16},{8,24},{16,0},{24,8},{1,17},{9,25},{17,1},{25,9},{2,18},{10... | collective-permute-start | bytes 3145736 | tf_op jit(solution)/shard_map/syD1/ppermute | solution.py:29
  440.9 47.7 %collective-permute-start.70 = (bf16[256,2048]{1,0:T(8,128)(2,1)S(1)}, bf16[256,2048]{1,0:T(8,128)(2,1)S(1)}, u32[]{:S(2)}, u32[]{:S(2)}) collective-permute-start(bf16[256,2048]{1,0:T(8,128)(2,1)S(1)} %copy-done.85), channel_id=1, source_target_pairs={{0,8},{8,0},{16,24},{24,16},{1,9},{9,1},{17,25},{25,17},{2,10},{10... | collective-permute-start | bytes 3145736 | tf_op jit(solution)/shard_map/sxD1/ppermute | solution.py:29
  441.2 42.2 %collective-permute-start.65 = (bf16[512,1024]{1,0:T(8,128)(2,1)S(1)}, bf16[512,1024]{1,0:T(8,128)(2,1)S(1)}, u32[]{:S(2)}, u32[]{:S(2)}) collective-permute-start(bf16[512,1024]{1,0:T(8,128)(2,1)S(1)} %copy-done.89), channel_id=1, source_target_pairs={{0,16},{8,24},{16,0},{24,8},{1,17},{9,25},{17,1},{25,9},{2,18},{10... | collective-permute-start | bytes 3145736 | tf_op jit(solution)/shard_map/syI1/ppermute | solution.py:29
  522.4 50.9 %collective-permute-start.83 = (bf16[512,1024]{1,0:T(8,128)(2,1)S(1)}, bf16[512,1024]{1,0:T(8,128)(2,1)S(1)}, u32[]{:S(2)}, u32[]{:S(2)}) collective-permute-start(bf16[512,1024]{1,0:T(8,128)(2,1)S(1)} %share.34), channel_id=1, source_target_pairs={{0,8},{8,0},{16,24},{24,16},{1,9},{9,1},{17,25},{25,17},{2,10},{10... | collective-permute-start | bytes 3145736 | tf_op jit(solution)/shard_map/sxA1/ppermute | solution.py:29
  523.5 31.9 %collective-permute-start.77 = (bf16[512,1024]{1,0:T(8,128)(2,1)S(1)}, bf16[512,1024]{1,0:T(8,128)(2,1)S(1)}, u32[]{:S(2)}, u32[]{:S(2)}) collective-permute-start(bf16[512,1024]{1,0:T(8,128)(2,1)S(1)} %share.33), channel_id=1, source_target_pairs={{0,16},{8,24},{16,0},{24,8},{1,17},{9,25},{17,1},{25,9},{2,18},{10... | collective-permute-start | bytes 3145736 | tf_op jit(solution)/shard_map/syA1/ppermute | solution.py:29
  545.3 42.0 %collective-permute-start.85 = (bf16[256,2048]{1,0:T(8,128)(2,1)S(1)}, bf16[256,2048]{1,0:T(8,128)(2,1)S(1)}, u32[]{:S(2)}, u32[]{:S(2)}) collective-permute-start(bf16[256,2048]{1,0:T(8,128)(2,1)S(1)} %share.35), channel_id=1, source_target_pairs={{0,8},{8,0},{16,24},{24,16},{1,9},{9,1},{17,25},{25,17},{2,10},{10... | collective-permute-start | bytes 3145736 | tf_op jit(solution)/shard_map/sxD0/ppermute | solution.py:29
  568.2 25.4 %collective-permute-start.86 = (bf16[256,2048]{1,0:T(8,128)(2,1)S(1)}, bf16[256,2048]{1,0:T(8,128)(2,1)S(1)}, u32[]{:S(2)}, u32[]{:S(2)}) collective-permute-start(bf16[256,2048]{1,0:T(8,128)(2,1)S(1)} %share.38), channel_id=1, source_target_pairs={{0,16},{8,24},{16,0},{24,8},{1,17},{9,25},{17,1},{25,9},{2,18},{10... | collective-permute-start | bytes 3145736 | tf_op jit(solution)/shard_map/syD0/ppermute | solution.py:29
  580.9 45.5 %collective-permute-start.92 = (bf16[512,1024]{1,0:T(8,128)(2,1)S(1)}, bf16[512,1024]{1,0:T(8,128)(2,1)S(1)}, u32[]{:S(2)}, u32[]{:S(2)}) collective-permute-start(bf16[512,1024]{1,0:T(8,128)(2,1)S(1)} %share.39), channel_id=1, source_target_pairs={{0,8},{8,0},{16,24},{24,16},{1,9},{9,1},{17,25},{25,17},{2,10},{10... | collective-permute-start | bytes 3145736 | tf_op jit(solution)/shard_map/sxI0/ppermute | solution.py:29
  595.3 25.5 %collective-permute-start.91 = (bf16[256,1024]{1,0:T(8,128)(2,1)S(1)}, bf16[256,1024]{1,0:T(8,128)(2,1)S(1)}, u32[]{:S(2)}, u32[]{:S(2)}) collective-permute-start(bf16[256,1024]{1,0:T(8,128)(2,1)S(1)} %get-tuple-element.1709), channel_id=1, source_target_pairs={{0,8},{8,0},{16,24},{24,16},{1,9},{9,1},{17,25},{25,17},{2,10},{10... | collective-permute-start | bytes 1572872 | tf_op jit(solution)/shard_map/rxI0/ppermute | solution.py:29
  645.4 32.6 %collective-permute-start.101 = (bf16[512,1024]{1,0:T(8,128)(2,1)S(1)}, bf16[512,1024]{1,0:T(8,128)(2,1)S(1)}, u32[]{:S(2)}, u32[]{:S(2)}) collective-permute-start(bf16[512,1024]{1,0:T(8,128)(2,1)S(1)} %share.43), channel_id=1, source_target_pairs={{0,16},{8,24},{16,0},{24,8},{1,17},{9,25},{17,1},{25,9},{2,18},{10... | collective-permute-start | bytes 3145736 | tf_op jit(solution)/shard_map/syI0/ppermute | solution.py:29
  673.8 35.7 %collective-permute-start.105 = (bf16[512,1024]{1,0:T(8,128)(2,1)S(1)}, bf16[512,1024]{1,0:T(8,128)(2,1)S(1)}, u32[]{:S(2)}, u32[]{:S(2)}) collective-permute-start(bf16[512,1024]{1,0:T(8,128)(2,1)S(1)} %share.45), channel_id=1, source_target_pairs={{0,16},{8,24},{16,0},{24,8},{1,17},{9,25},{17,1},{25,9},{2,18},{10... | collective-permute-start | bytes 3145736 | tf_op jit(solution)/shard_map/syA0/ppermute | solution.py:29
  674.5 22.8 %collective-permute-start.104 = (bf16[512,1024]{1,0:T(8,128)(2,1)}, bf16[512,1024]{1,0:T(8,128)(2,1)}, u32[]{:S(2)}, u32[]{:S(2)}) collective-permute-start(bf16[512,1024]{1,0:T(8,128)(2,1)} %share.44), channel_id=1, source_target_pairs={{0,8},{8,0},{16,24},{24,16},{1,9},{9,1},{17,25},{25,17},{2,10},{10... | collective-permute-start | bytes 3145736 | tf_op jit(solution)/shard_map/sxA0/ppermute | solution.py:29
  (262 other events, 3469.0 us)

commit v3 on v2

--- a/solution.py
+++ b/solution.py
@@ -1407,25 +1407,7 @@
     )
 
 
-ORDER = (
-    54, 0, 1, 56, 57, 58, 59, -2, 2, 60, -58, 3, 55, 70, 85, 75, 81, -60, 76, 73, 53, -4, 4, 83, 71, 80, -77, 72, -5,
-    5, -73, 20, -6, 61, 6, 8, 7, -21, 21, -62, 74, 62, 63, 64, -65, 65, 66, -22, 12, 67, -75, 22, -9, 9, -8, -13, 10,
-    13, 68, -23, 28, 23, -14, 24, -10, 25, 14, 69, -11, 11, 77, 78, -29, 29, -15, 37, -79, 15, 17, 79, 90, -25, 16,
-    91, -26, -30, -38, 27, 30, 26, 92, -18, 93, -31, 82, -17, -94, 18, 19, -28, 45, 31, -27, -83, -46, 32, 33, 46,
-    -19, 84, -20, 94, 95, -47, 38, 96, -33, -85, 35, -34, -39, 39, 34, 97, 86, -98, -40, 47, 40, 42, -36, -87, 41, 87,
-    -35, 88, 36, 98, -48, -89, 48, 49, 50, 99, -43, -42, 44, 43, 100, 101, 89, -50, -51, 52, -102, 51, 102, -45, -44,
-    103, -53, -52, 104, 105, 130, -106, 133, 135, 134, 131, 132, 115, 117, 116, -136, -133, 148, -135, 136, 138, 137,
-    139, -118, 118, -117, 120, 119, 121, 106, 110, 111, 112, 108, 107, 149, 150, -139, -140, -112, 113, 109, 151,
-    -121, -122, 152, 153, 155, 154, -153, 168, -114, -110, 170, 171, 173, 172, -156, 140, -155, 157, 159, 141, 142,
-    156, 158, -174, -173, 174, 176, -143, 143, 144, 186, -145, 145, 146, 189, 191, -160, 122, -147, 147, 123, 124,
-    175, 177, 187, -192, -125, 188, 125, 126, 192, -159, 194, -189, 160, -177, -127, 190, 161, 162, 127, 128, 204,
-    -178, 205, 178, -163, 179, -129, 180, 163, 164, 206, -191, -181, 181, 182, -165, 209, -195, 211, 210, 165, 166,
-    207, -183, 208, 183, 184, 193, -167, 195, -212, -209, 224, -211, -185, 227, 212, 214, 231, 232, 213, 215, 167,
-    185, 228, 225, 233, 234, 229, 226, -233, 230, -196, 196, 197, 169, 236, -235, 237, 198, -215, 129, -238, 238,
-    -231, 239, 235, 114, 247, -240, 248, 240, 241, -199, 199, -216, -249, 200, 216, -242, 217, 218, 242, 243, 249,
-    -201, 201, 202, -244, 244, 245, -219, 219, 220, -246, 246, -203, 203, 250, 251, -221, 221, 222, -252, 252, -223,
-    223, 253, 254, -255, 255,
-)
+ORDER = (75, 76, 80, 71, 72, 85, 81, 83, 73, 53, 54, -77, 74, 60, 70, 56, -73, 61, 55, 0, -75, 1, 57, 58, 77, -62, 59, 78, -2, 2, -58, -79, 3, 79, -60, 37, 62, 63, 64, -4, 4, -65, 65, 68, -38, 12, 67, -5, 5, 69, -13, 13, -6, 20, 6, 7, 8, 66, -14, 14, -21, 21, -15, 28, 15, 16, -22, 17, -8, 22, -9, 10, -29, 9, -23, 82, 23, -83, 29, -17, 24, -18, 19, -30, 30, -10, 18, -11, 25, 11, 90, -31, 86, 31, -20, -87, 33, 45, -25, 32, 91, -46, -19, -26, 26, 27, 38, 92, -39, 93, -33, 39, -34, 35, -94, 34, 94, -40, 46, -27, 84, 40, -28, 41, 95, -47, -35, -36, 42, 47, 96, -85, -48, 97, 87, 88, 48, -42, -98, -89, 49, 44, -43, 50, 43, 89, 36, 98, -45, 99, -50, -44, 52, -51, 51, 100, 101, -102, 102, -53, 103, -52, 130, 131, 132, 115, 116, 117, 133, -133, 134, 135, 148, 149, -117, 119, -118, 121, 118, 120, -135, 137, -136, 139, 136, 138, 150, -122, -121, 153, 154, 155, 122, 151, 152, 104, -140, -139, -153, 105, 140, -156, -155, 141, 142, 157, -106, 159, 156, 158, -143, 143, 144, 123, 124, 170, 106, -145, 145, 146, 110, 108, 107, 168, -125, 111, 186, -147, -160, -159, 109, 187, -112, 188, 189, 190, 191, -110, 160, -189, 204, 161, 162, 171, -191, -192, 172, 173, -163, 192, 194, 163, 164, 193, -173, -165, -174, 195, 174, 176, 175, 177, 125, 126, 165, 205, 206, -127, -195, -196, 166, 196, 207, -167, 208, 197, 198, 209, -177, 210, -209, 211, 226, 167, -178, -199, 199, 200, 127, 128, 147, 178, 179, 224, -201, -211, -212, -129, 180, 213, 215, 212, -181, 214, 129, 201, 202, 181, 182, 227, 233, 231, 228, 229, 225, 169, 236, 237, 112, -203, 234, 203, -238, 250, 251, 238, -183, 230, -252, 252, -216, 183, -235, 184, -215, 216, -231, 232, 217, -185, 218, 185, 247, 248, -249, 249, -233, 113, 235, -219, 239, 219, -114, 220, -240, 114, 240, 241, -221, 221, -242, 222, 242, 243, -244, 244, 245, -223, 223, 253, 254, -246, 246, -255, 255)
 
 
 def solution(mesh):

time: 774 us -> 754 us (0.974)
  waiting for transfers between devices: 220 us -> 186 us
  local copies, waits for them, and re-layouts: 91.3 us -> 109 us
  Pallas kernels: 268 us -> 277 us
    ppermute x104, waiting for transfers between devices: 195 us -> 141 us  [permuted(): return lax.ppermute(block, axis, [(i, route(i)) for i in range(count)])]
    ppermute x15, waiting for transfers between devices: 25.4 us -> 45.3 us  [route_blocks(): lax.ppermute(v, SEG, route)]
    unnamed x392 -> x420, local copies, waits for them, and re-layouts: 50.4 us -> 65.2 us
    ppermute x104, starting transfers between devices: 120 us -> 109 us  [permuted(): return lax.ppermute(block, axis, [(i, route(i)) for i in range(count)])]
    pallas_call x52, Pallas kernels: 216 us -> 224 us  [in_vmem(): pl.pallas_call(kernel, out_shape=outs, in_specs=([smem_block] if scalars...]
  transfers between devices with their start and end apart: 119 -> 119, of which waited for: 42 -> 42; matrix products, arithmetic and copies ran while one was open for 11% -> 12% of each run, Pallas kernels for 31% -> 34%
where the time goes in v3:
time: 754 us; the launch traced here: 743 us
  Pallas kernels  277 us (37%)
  waiting for transfers between devices  186 us (25%)
  starting transfers between devices  131 us (17%)
  local copies, waits for them, and re-layouts  109 us (14%)
  other arithmetic  35.7 us (5%)
    pallas_call x52, Pallas kernels, in_vmem(): pl.pallas_call(kernel, out_shape=outs, in_specs=([smem_block] if scalars...  224 us
    ppermute x104, waiting for transfers between devices, permuted(): return lax.ppermute(block, axis, [(i, route(i)) for i in range(count)])  141 us
    ppermute x104, starting transfers between devices, permuted(): return lax.ppermute(block, axis, [(i, route(i)) for i in range(count)])  109 us
    unnamed x420, local copies, waits for them, and re-layouts  65.2 us
    ppermute x15, waiting for transfers between devices, route_blocks(): lax.ppermute(v, SEG, route)  45.3 us
    pallas_call x2, Pallas kernels, attend(): pl.pallas_call(functools.partial(forward_kernel, halo, memory is not None...  27 us
    pallas_call x2, Pallas kernels, attend_back(): pl.pallas_call(functools.partial(backward_kernel, halo, memory is not Non...  25.1 us
    ppermute x15, starting transfers between devices, route_blocks(): lax.ppermute(v, SEG, route)  21.5 us
  transfers between devices with their start and end apart: 119, of which 42 were waited for; matrix products, arithmetic and copies ran while one was open for 12% of the time, Pallas kernels for 34%

profile of v3, /device:TPU:1, one launch (start us, length us, event | category | flops | bytes accessed | tf_op | source)
XLA Modules:
  0.0 743.5 jit_solution(2155462042973228033)
XLA Ops:
  54.9 6.7 collective-permute-done.10
  61.7 6.4 slot_mask.4
  68.3 6.4 slot_mask.5
  75.9 6.4 slot_mask.6
  90.1 6.4 slot_mask.7
  97.3 7.0 collective-permute-done.16
  107.9 8.7 %collective-permute-done.20 = bf16[512,256]{1,0:T(8,128)(2,1)S(1)} collective-permute-done((bf16[512,256]{1,0:T(8,128)(2,1)S(1)}, bf16[512,256]{1,0:T(8,128)(2,1)S(1)}, u32[]{:S(2)}, u32[]{:S(2)}) %collective-permute-start.20) | collective-permute-done | bytes 262176 | tf_op jit(solution)/shard_map/z2D0/ppermute | solution.py:29
  137.8 9.4 %collective-permute-done.23 = bf16[784,256]{1,0:T(8,128)(2,1)S(1)} collective-permute-done((bf16[784,256]{1,0:T(8,128)(2,1)S(1)}, bf16[784,256]{1,0:T(8,128)(2,1)S(1)}, u32[]{:S(2)}, u32[]{:S(2)}) %collective-permute-start.23) | collective-permute-done | bytes 401440 | tf_op jit(solution)/shard_map/z2A1/ppermute | solution.py:29
  174.5 10.5 %attend.2 = (bf16[1024,512]{1,0:T(8,128)(2,1)S(1)}, bf16[4,1024,768]{2,1,0:T(8,128)(2,1)S(1)}) custom-call(f32[4,1,1024]{2,1,0:T(1,128)S(1)} %get-tuple-element.1171.refs_0_, s32[1024,1]{1,0:T(8,128)S(1)} %copy-done.34, s32[1,1024]{1,0:T(1,128)S(1)} %constant_dynamic-slice_fusion.2.refs_2_, ...), custom_call_target="tpu_custom_call" | custom-call | flops 1610612736 | bytes 16777216 | tf_op jit(solution)/shard_map/att0/attend/pallas_call | solution.py:775
  196.5 19.1 %collective-permute-start.38 = (bf16[1024,1024]{1,0:T(8,128)(2,1)S(1)}, bf16[1024,1024]{1,0:T(8,128)(2,1)S(1)}, u32[]{:S(2)}, u32[]{:S(2)}) collective-permute-start(bf16[1024,1024]{1,0:T(8,128)(2,1)S(1)} %out.2.own_ref), channel_id=1, source_target_pairs={{0,1},{1,0},{2,3},{3,2},{4,5},{5,4},{6,7},{7,6},{8,9},{9,8},{10,11... | collective-permute-start | bytes 6291464 | tf_op jit(solution)/shard_map/oswap0/ppermute | solution.py:29
  228.2 10.2 %expand.2 = (bf16[1024,2048]{1,0:T(8,128)(2,1)S(1)}, bf16[1024,2048]{1,0:T(8,128)(2,1)S(1)}) custom-call(s32[1]{0:T(128)} %bitcast.at_ref, bf16[1024,1024]{1,0:T(8,128)(2,1)S(1)} %get-tuple-element.1709.rows_ref.refs_1_, bf16[512,1024]{1,0:T(8,128)(2,1)S(1)} %copy-done.42, bf16[512,1024]{1,0:T(8,128)(2,1)S(1)} %copy-done.61, ...), custom_call_target="tpu_custom_call" | custom-call | flops 12884901888 | tf_op jit(solution)/shard_map/ex0/expand/pallas_call | solution.py:417
  244.6 8.3 %down.2.refs_1_ = bf16[1024,1024]{1,0:T(8,128)(2,1)S(1)} custom-call(s32[1]{0:T(128)} %bitcast.at_ref, bf16[1024,2048]{1,0:T(8,128)(2,1)S(1)} %get-tuple-element.1758.rows_ref.refs_1_, bf16[256,2048]{1,0:T(8,128)(2,1)} %constant_dynamic-update-slice_fusion.18.refs_0_, bf16[256,2048]{1,0:T(8,128)(2,1)} %collective-permute-done.29.refs_1_, ...), custom_call_target="tpu_custom_call" | custom-call | flops 12884901888 | tf_op jit(solution)/shard_map/dp0/down/pallas_call | solution.py:417
  274.0 6.5 head.3
  291.0 16.5 %attend.3 = (bf16[1024,512]{1,0:T(8,128)(2,1)S(1)}, bf16[4,1024,768]{2,1,0:T(8,128)(2,1)S(1)}, bf16[4,1024,256]{2,1,0:T(8,128)(2,1)S(1)}, bf16[1024,512]{1,0:T(8,128)(2,1)S(1)}) custom-call(f32[4,1,1024]{2,1,0:T(1,128)S(1)} %get-tuple-element.1315.refs_0_, s32[1024,1]{1,0:T(8,128)S(1)} %copy-done.33, s32[1,1024]{1,0:T(1,128)S(1)} %constant_dynamic-slice_fusion.2.refs_2_, ...), custom_call_target="tpu_custom_call" | custom-call | flops 2147483648 | bytes 16777216 | tf_op jit(solution)/shard_map/att1/attend/pallas_call | solution.py:775
  324.7 10.8 %expand.3 = (bf16[1024,2048]{1,0:T(8,128)(2,1)S(1)}, bf16[1024,2048]{1,0:T(8,128)(2,1)S(1)}) custom-call(s32[1]{0:T(128)} %bitcast.at_ref, bf16[1024,1024]{1,0:T(8,128)(2,1)S(1)} %get-tuple-element.1513.rows_ref.refs_1_, bf16[512,1024]{1,0:T(8,128)(2,1)S(1)} %copy-done.45, bf16[512,1024]{1,0:T(8,128)(2,1)S(1)} %copy-done.67, ...), custom_call_target="tpu_custom_call" | custom-call | flops 12884901888 | tf_op jit(solution)/shard_map/ex1/expand/pallas_call | solution.py:417
  337.6 8.7 %by_rows.6.rows_ref.refs_0_ = bf16[1024,2048]{1,0:T(8,128)(2,1)S(1)} custom-call(s32[1]{0:T(128)} %bitcast.at_ref, bf16[1024,1024]{1,0:T(8,128)(2,1)S(1)} %bitcast.334, bf16[256,2048]{1,0:T(8,128)(2,1)} %constant_dynamic-update-slice_fusion.58.refs_0_, bf16[256,2048]{1,0:T(8,128)(2,1)} %collective-permute-done.54.refs_1_, ...), custom_call_target="tpu_custom_call" | custom-call | flops 12884901888 | tf_op jit(solution)/shard_map/pg1/by_rows/pallas_call | solution.py:417
  346.3 6.3 by_rows.7.own_ref
  392.8 14.3 %attend_back.2 = (bf16[1024,1536]{1,0:T(8,128)(2,1)S(1)}, f32[4,1,1024]{2,1,0:T(1,128)S(1)}, f32[4,1,128]{2,1,0:T(1,128)S(1)}) custom-call(bf16[1024,1536]{1,0:T(8,128)(2,1)S(1)} %copy-done.3, bf16[1024,1536]{1,0:T(8,128)(2,1)S(1)} %copy-done.3, bf16[1024,1536]{1,0:T(8,128)(2,1)S(1)} %copy-done.3, bf16[1024,512]{1,0:T(8,128)(2,1)S(1)} %attended_back.2.refs_3_, ...), custom_call_target="tpu_custom_call" | custom-call | flops 3758096384 | bytes 20971520 | tf_op jit(solution)/shard_map/ab1/attend_back/pallas_call | solution.py:831
  423.2 8.6 %down.3 = bf16[1024,1024]{1,0:T(8,128)(2,1)S(1)} custom-call(s32[1]{0:T(128)} %bitcast.at_ref, bf16[1024,2048]{1,0:T(8,128)(2,1)S(1)} %copy-done.131, bf16[256,2048]{1,0:T(8,128)(2,1)} %constant_dynamic-update-slice_fusion.58.refs_0_, bf16[256,2048]{1,0:T(8,128)(2,1)} %collective-permute-done.54.refs_1_, bf16[256,2048]{1,0:T(8,128)(2,1)} %collective-permute-done.52.refs_2_, ...), custom_call_target="tpu_custom_call" | custom-call | flops 12884901888 | tf_op jit(solution)/shard_map/dp1/down/pallas_call | solution.py:417
  463.0 6.2 collective-permute-done.72
  474.9 8.6 %by_rows.9.rows_ref.refs_0_ = bf16[1024,2048]{1,0:T(8,128)(2,1)S(1)} custom-call(s32[1]{0:T(128)} %bitcast.at_ref, bf16[1024,1024]{1,0:T(8,128)(2,1)S(1)} %get-tuple-element.1757.rows_ref.refs_0_, bf16[256,2048]{1,0:T(8,128)(2,1)} %constant_dynamic-update-slice_fusion.18.refs_0_, bf16[256,2048]{1,0:T(8,128)(2,1)} %collective-permute-done.29.refs_1_, ...), custom_call_target="tpu_custom_call" | custom-call | flops 12884901888 | tf_op jit(solution)/shard_map/pg0/by_rows/pallas_call | solution.py:417
  485.1 6.5 collective-permute-done.75
  491.6 6.2 by_rows.10.own_ref
  550.6 10.8 %attend_back.3 = (bf16[1024,1536]{1,0:T(8,128)(2,1)S(1)}, f32[4,1,1024]{2,1,0:T(1,128)S(1)}) custom-call(bf16[1024,1536]{1,0:T(8,128)(2,1)S(1)} %get-tuple-element.1690.refs_3_.refs_4_.refs_5_.refs_0_.refs_1_.refs_2_, bf16[1024,1536]{1,0:T(8,128)(2,1)S(1)} %get-tuple-element.1690.refs_3_.refs_4_.refs_5_.refs_0_.refs_1_.refs_2_, ...), custom_call_target="tpu_custom_call" | custom-call | flops 3221225472 | bytes 20971520 | tf_op jit(solution)/shard_map/ab0/attend_back/pallas_call | solution.py:831
  561.4 6.8 collective-permute-done.88.refs_3_
  593.6 14.6 %collective-permute-done.91.refs_2_ = bf16[256,2048]{1,0:T(8,128)(2,1)} collective-permute-done((bf16[256,2048]{1,0:T(8,128)(2,1)}, bf16[256,2048]{1,0:T(8,128)(2,1)}, u32[]{:S(2)}, u32[]{:S(2)}) %collective-permute-start.91) | collective-permute-done | bytes 1048608 | tf_op jit(solution)/shard_map/sxD0/ppermute | solution.py:29
  617.9 7.8 %join_back.7 = (f32[1024,1024]{1,0:T(8,128)}, bf16[1024,1024]{1,0:T(8,128)(2,1)S(1)}, f32[1,1024]{1,0:T(1,128)S(1)}, f32[1,1024]{1,0:T(1,128)S(1)}) custom-call(f32[1024,1024]{1,0:T(8,128)S(1)} %copy-done.19, bf16[1024,1024]{1,0:T(8,128)(2,1)S(1)} %by_rows.11.own_ref, bf16[1024,1024]{1,0:T(8,128)(2,1)} %collective-permute-done.90.got_ref, ...), custom_call_target="tpu_custom_call" | custom-call | flops 62914560 | tf_op jit(solution)/shard_map/jk0/join_back/pallas_call | solution.py:417
  652.9 6.8 collective-permute-start.106
  664.2 7.0 collective-permute-done.104
  686.8 16.9 %collective-permute-done.107 = bf16[128,1024]{1,0:T(8,128)(2,1)S(1)} collective-permute-done((bf16[128,1024]{1,0:T(8,128)(2,1)}, bf16[128,1024]{1,0:T(8,128)(2,1)S(1)}, u32[]{:S(2)}, u32[]{:S(2)}) %collective-permute-start.107) | collective-permute-done | bytes 262176 | tf_op jit(solution)/shard_map/i2/ppermute | solution.py:952
  706.0 6.5 collective-permute-done.110
  715.8 8.0 %collective-permute-done.113 = bf16[512,256]{1,0:T(8,128)(2,1)S(1)} collective-permute-done((bf16[512,256]{1,0:T(8,128)(2,1)S(1)}, bf16[512,256]{1,0:T(8,128)(2,1)S(1)}, u32[]{:S(2)}, u32[]{:S(2)}) %collective-permute-start.113) | collective-permute-done | bytes 262176 | tf_op jit(solution)/shard_map/q2A0/ppermute | solution.py:29
  (892 shorter events, 449.0 us)
Async XLA Ops:
  87.6 29.3 %collective-permute-start.19 = (bf16[528,1024]{1,0:T(8,128)(2,1)S(1)}, bf16[528,1024]{1,0:T(8,128)(2,1)S(1)}, u32[]{:S(2)}, u32[]{:S(2)}) collective-permute-start(bf16[528,1024]{1,0:T(8,128)(2,1)S(1)} %pad_maximum_fusion.3.own_ref.refs_3_.refs_0_), channel_id=1, source_target_pairs={{0,8},{8,0},{16,24},{24,16},{1,9},{9,1},{17,25},{25,17},{2,10},{10... | collective-permute-start | bytes 3244040 | tf_op jit(solution)/shard_map/pxA0/ppermute | solution.py:29
  88.8 28.0 %collective-permute-start.18 = (bf16[528,1024]{1,0:T(8,128)(2,1)S(1)}, bf16[528,1024]{1,0:T(8,128)(2,1)S(1)}, u32[]{:S(2)}, u32[]{:S(2)}) collective-permute-start(bf16[528,1024]{1,0:T(8,128)(2,1)S(1)} %pad_maximum_fusion.3.own_ref.refs_3_.refs_0_), channel_id=1, source_target_pairs={{0,16},{8,24},{16,0},{24,8},{1,17},{9,25},{17,1},{25,9},{2,18},{10... | collective-permute-start | bytes 3244040 | tf_op jit(solution)/shard_map/pyA0/ppermute | solution.py:29
  107.6 27.7 %collective-permute-start.25 = (bf16[512,1024]{1,0:T(8,128)(2,1)S(1)}, bf16[512,1024]{1,0:T(8,128)(2,1)S(1)}, u32[]{:S(2)}, u32[]{:S(2)}) collective-permute-start(bf16[512,1024]{1,0:T(8,128)(2,1)S(1)} %pad_maximum_fusion.6.refs_0_), channel_id=1, source_target_pairs={{0,8},{8,0},{16,24},{24,16},{1,9},{9,1},{17,25},{25,17},{2,10},{10... | collective-permute-start | bytes 3145736 | tf_op jit(solution)/shard_map/pxI0/ppermute | solution.py:29
  121.0 26.2 %collective-permute-start.27 = (bf16[256,1024]{1,0:T(8,128)(2,1)S(1)}, bf16[256,1024]{1,0:T(8,128)(2,1)S(1)}, u32[]{:S(2)}, u32[]{:S(2)}) collective-permute-start(bf16[256,1024]{1,0:T(8,128)(2,1)S(1)} %slice.558), channel_id=1, source_target_pairs={{0,8},{8,0},{16,24},{24,16},{1,9},{9,1},{17,25},{25,17},{2,10},{10... | collective-permute-start | bytes 1572872 | tf_op jit(solution)/shard_map/fxA0/ppermute | solution.py:29
  121.3 25.9 %collective-permute-start.28 = (bf16[272,1024]{1,0:T(8,128)(2,1)S(1)}, bf16[272,1024]{1,0:T(8,128)(2,1)S(1)}, u32[]{:S(2)}, u32[]{:S(2)}) collective-permute-start(bf16[272,1024]{1,0:T(8,128)(2,1)S(1)} %slice.559), channel_id=1, source_target_pairs={{0,16},{8,24},{16,0},{24,8},{1,17},{9,25},{17,1},{25,9},{2,18},{10... | collective-permute-start | bytes 1671176 | tf_op jit(solution)/shard_map/fyA0/ppermute | solution.py:29
  136.0 33.6 %collective-permute-start.31 = (bf16[256,1024]{1,0:T(8,128)(2,1)S(1)}, bf16[256,1024]{1,0:T(8,128)(2,1)S(1)}, u32[]{:S(2)}, u32[]{:S(2)}) collective-permute-start(bf16[256,1024]{1,0:T(8,128)(2,1)S(1)} %slice.566), channel_id=1, source_target_pairs={{0,16},{8,24},{16,0},{24,8},{1,17},{9,25},{17,1},{25,9},{2,18},{10... | collective-permute-start | bytes 1572872 | tf_op jit(solution)/shard_map/fyI0/ppermute | solution.py:29
  137.6 33.6 %collective-permute-start.29 = (bf16[256,2048]{1,0:T(8,128)(2,1)}, bf16[256,2048]{1,0:T(8,128)(2,1)}, u32[]{:S(2)}, u32[]{:S(2)}) collective-permute-start(bf16[256,2048]{1,0:T(8,128)(2,1)} %constant_dynamic-update-slice_fusion.18.refs_0_), channel_id=1, source_target_pairs={{0,8},{8,0},{16,24},{24,16},{1,9},{9,1},{17,25},{25,17},{2,10},{10... | collective-permute-start | bytes 3145736 | tf_op jit(solution)/shard_map/pxD0/ppermute | solution.py:29
  148.4 39.2 %collective-permute-start.34 = (bf16[256,1024]{1,0:T(8,128)(2,1)}, bf16[256,1024]{1,0:T(8,128)(2,1)}, u32[]{:S(2)}, u32[]{:S(2)}) collective-permute-start(bf16[256,1024]{1,0:T(8,128)(2,1)} %slice.599), channel_id=1, source_target_pairs={{0,8},{8,0},{16,24},{24,16},{1,9},{9,1},{17,25},{25,17},{2,10},{10... | collective-permute-start | bytes 1572872 | tf_op jit(solution)/shard_map/fxI0/ppermute | solution.py:29
  148.7 39.0 %collective-permute-start.33 = (bf16[256,2048]{1,0:T(8,128)(2,1)}, bf16[256,2048]{1,0:T(8,128)(2,1)}, u32[]{:S(2)}, u32[]{:S(2)}) collective-permute-start(bf16[256,2048]{1,0:T(8,128)(2,1)} %constant_dynamic-update-slice_fusion.18.refs_0_), channel_id=1, source_target_pairs={{0,16},{8,24},{16,0},{24,8},{1,17},{9,25},{17,1},{25,9},{2,18},{10... | collective-permute-start | bytes 3145736 | tf_op jit(solution)/shard_map/pyD0/ppermute | solution.py:29
  172.2 43.4 %collective-permute-start.37 = (bf16[528,1024]{1,0:T(8,128)(2,1)}, bf16[528,1024]{1,0:T(8,128)(2,1)S(1)}, u32[]{:S(2)}, u32[]{:S(2)}) collective-permute-start(bf16[528,1024]{1,0:T(8,128)(2,1)} %pad_maximum_fusion.4.own_ref.refs_5_.refs_0_), channel_id=1, source_target_pairs={{0,16},{8,24},{16,0},{24,8},{1,17},{9,25},{17,1},{25,9},{2,18},{10... | collective-permute-start | bytes 3244040 | tf_op jit(solution)/shard_map/pyA1/ppermute | solution.py:29
  172.2 43.4 %collective-permute-start.32 = (bf16[528,1024]{1,0:T(8,128)(2,1)}, bf16[528,1024]{1,0:T(8,128)(2,1)S(1)}, u32[]{:S(2)}, u32[]{:S(2)}) collective-permute-start(bf16[528,1024]{1,0:T(8,128)(2,1)} %pad_maximum_fusion.4.own_ref.refs_5_.refs_0_), channel_id=1, source_target_pairs={{0,8},{8,0},{16,24},{24,16},{1,9},{9,1},{17,25},{25,17},{2,10},{10... | collective-permute-start | bytes 3244040 | tf_op jit(solution)/shard_map/pxA1/ppermute | solution.py:29
  190.3 34.0 %collective-permute-start.43 = (bf16[128,2048]{1,0:T(8,128)(2,1)S(1)}, bf16[128,2048]{1,0:T(8,128)(2,1)S(1)}, u32[]{:S(2)}, u32[]{:S(2)}) collective-permute-start(bf16[128,2048]{1,0:T(8,128)(2,1)S(1)} %slice.604), channel_id=1, source_target_pairs={{0,8},{8,0},{16,24},{24,16},{1,9},{9,1},{17,25},{25,17},{2,10},{10... | collective-permute-start | bytes 1572872 | tf_op jit(solution)/shard_map/fxD0/ppermute | solution.py:29
  190.7 34.0 %collective-permute-start.42 = (bf16[128,2048]{1,0:T(8,128)(2,1)S(1)}, bf16[128,2048]{1,0:T(8,128)(2,1)S(1)}, u32[]{:S(2)}, u32[]{:S(2)}) collective-permute-start(bf16[128,2048]{1,0:T(8,128)(2,1)S(1)} %slice.603), channel_id=1, source_target_pairs={{0,16},{8,24},{16,0},{24,8},{1,17},{9,25},{17,1},{25,9},{2,18},{10... | collective-permute-start | bytes 1572872 | tf_op jit(solution)/shard_map/fyD0/ppermute | solution.py:29
  215.7 26.0 %collective-permute-start.44 = (bf16[272,1024]{1,0:T(8,128)(2,1)S(1)}, bf16[272,1024]{1,0:T(8,128)(2,1)S(1)}, u32[]{:S(2)}, u32[]{:S(2)}) collective-permute-start(bf16[272,1024]{1,0:T(8,128)(2,1)S(1)} %slice.605), channel_id=1, source_target_pairs={{0,16},{8,24},{16,0},{24,8},{1,17},{9,25},{17,1},{25,9},{2,18},{10... | collective-permute-start | bytes 1671176 | tf_op jit(solution)/shard_map/fyA1/ppermute | solution.py:29
  225.6 27.3 %collective-permute-start.45 = (bf16[128,1024]{1,0:T(8,128)(2,1)S(1)}, bf16[128,1024]{1,0:T(8,128)(2,1)S(1)}, u32[]{:S(2)}, u32[]{:S(2)}) collective-permute-start(bf16[128,1024]{1,0:T(8,128)(2,1)S(1)} %copy-done.171), channel_id=1, source_target_pairs={{0,4},{1,5},{2,6},{3,7},{4,0},{5,1},{6,2},{7,3},{8,12},{9,13},{10,... | collective-permute-start | bytes 786440 | tf_op jit(solution)/shard_map/c2/ppermute | solution.py:952
  227.7 35.0 %collective-permute-start.49 = (bf16[512,1024]{1,0:T(8,128)(2,1)S(1)}, bf16[512,1024]{1,0:T(8,128)(2,1)S(1)}, u32[]{:S(2)}, u32[]{:S(2)}) collective-permute-start(bf16[512,1024]{1,0:T(8,128)(2,1)S(1)} %pad_maximum_fusion.7.refs_0_), channel_id=1, source_target_pairs={{0,8},{8,0},{16,24},{24,16},{1,9},{9,1},{17,25},{25,17},{2,10},{10... | collective-permute-start | bytes 3145736 | tf_op jit(solution)/shard_map/pxI1/ppermute | solution.py:29
  268.9 38.5 %collective-permute-start.53 = (bf16[256,1024]{1,0:T(8,128)(2,1)}, bf16[256,1024]{1,0:T(8,128)(2,1)}, u32[]{:S(2)}, u32[]{:S(2)}) collective-permute-start(bf16[256,1024]{1,0:T(8,128)(2,1)} %slice.621), channel_id=1, source_target_pairs={{0,8},{8,0},{16,24},{24,16},{1,9},{9,1},{17,25},{25,17},{2,10},{10... | collective-permute-start | bytes 1572872 | tf_op jit(solution)/shard_map/fxI1/ppermute | solution.py:29
  272.4 35.0 %collective-permute-start.54 = (bf16[256,2048]{1,0:T(8,128)(2,1)}, bf16[256,2048]{1,0:T(8,128)(2,1)}, u32[]{:S(2)}, u32[]{:S(2)}) collective-permute-start(bf16[256,2048]{1,0:T(8,128)(2,1)} %constant_dynamic-update-slice_fusion.58.refs_0_), channel_id=1, source_target_pairs={{0,8},{8,0},{16,24},{24,16},{1,9},{9,1},{17,25},{25,17},{2,10},{10... | collective-permute-start | bytes 3145736 | tf_op jit(solution)/shard_map/pxD1/ppermute | solution.py:29
  273.7 33.8 %collective-permute-start.52 = (bf16[256,2048]{1,0:T(8,128)(2,1)}, bf16[256,2048]{1,0:T(8,128)(2,1)}, u32[]{:S(2)}, u32[]{:S(2)}) collective-permute-start(bf16[256,2048]{1,0:T(8,128)(2,1)} %constant_dynamic-update-slice_fusion.58.refs_0_), channel_id=1, source_target_pairs={{0,16},{8,24},{16,0},{24,8},{1,17},{9,25},{17,1},{25,9},{2,18},{10... | collective-permute-start | bytes 3145736 | tf_op jit(solution)/shard_map/pyD1/ppermute | solution.py:29
  310.3 27.3 %collective-permute-start.57 = (bf16[128,2048]{1,0:T(8,128)(2,1)S(1)}, bf16[128,2048]{1,0:T(8,128)(2,1)S(1)}, u32[]{:S(2)}, u32[]{:S(2)}) collective-permute-start(bf16[128,2048]{1,0:T(8,128)(2,1)S(1)} %slice.625), channel_id=1, source_target_pairs={{0,8},{8,0},{16,24},{24,16},{1,9},{9,1},{17,25},{25,17},{2,10},{10... | collective-permute-start | bytes 1572872 | tf_op jit(solution)/shard_map/fxD1/ppermute | solution.py:29
  384.5 24.7 %collective-permute-start.63 = (bf16[256,2048]{1,0:T(8,128)(2,1)}, bf16[256,2048]{1,0:T(8,128)(2,1)S(1)}, u32[]{:S(2)}, u32[]{:S(2)}) collective-permute-start(bf16[256,2048]{1,0:T(8,128)(2,1)} %share.27), channel_id=1, source_target_pairs={{0,8},{8,0},{16,24},{24,16},{1,9},{9,1},{17,25},{25,17},{2,10},{10... | collective-permute-start | bytes 3145736 | tf_op jit(solution)/shard_map/sxD1/ppermute | solution.py:29
  384.5 24.6 %collective-permute-start.64 = (bf16[256,2048]{1,0:T(8,128)(2,1)}, bf16[256,2048]{1,0:T(8,128)(2,1)}, u32[]{:S(2)}, u32[]{:S(2)}) collective-permute-start(bf16[256,2048]{1,0:T(8,128)(2,1)} %share.26), channel_id=1, source_target_pairs={{0,16},{8,24},{16,0},{24,8},{1,17},{9,25},{17,1},{25,9},{2,18},{10... | collective-permute-start | bytes 3145736 | tf_op jit(solution)/shard_map/syD1/ppermute | solution.py:29
  407.1 28.3 %collective-permute-start.66 = (bf16[512,1024]{1,0:T(8,128)(2,1)}, bf16[512,1024]{1,0:T(8,128)(2,1)S(1)}, u32[]{:S(2)}, u32[]{:S(2)}) collective-permute-start(bf16[512,1024]{1,0:T(8,128)(2,1)} %share.29), channel_id=1, source_target_pairs={{0,8},{8,0},{16,24},{24,16},{1,9},{9,1},{17,25},{25,17},{2,10},{10... | collective-permute-start | bytes 3145736 | tf_op jit(solution)/shard_map/sxI1/ppermute | solution.py:29
  407.8 27.6 %collective-permute-start.67 = (bf16[512,1024]{1,0:T(8,128)(2,1)}, bf16[512,1024]{1,0:T(8,128)(2,1)S(1)}, u32[]{:S(2)}, u32[]{:S(2)}) collective-permute-start(bf16[512,1024]{1,0:T(8,128)(2,1)} %share.28), channel_id=1, source_target_pairs={{0,16},{8,24},{16,0},{24,8},{1,17},{9,25},{17,1},{25,9},{2,18},{10... | collective-permute-start | bytes 3145736 | tf_op jit(solution)/shard_map/syI1/ppermute | solution.py:29
  461.9 29.7 %collective-permute-start.73 = (bf16[512,1024]{1,0:T(8,128)(2,1)S(1)}, bf16[512,1024]{1,0:T(8,128)(2,1)S(1)}, u32[]{:S(2)}, u32[]{:S(2)}) collective-permute-start(bf16[512,1024]{1,0:T(8,128)(2,1)S(1)} %share.34), channel_id=1, source_target_pairs={{0,8},{8,0},{16,24},{24,16},{1,9},{9,1},{17,25},{25,17},{2,10},{10... | collective-permute-start | bytes 3145736 | tf_op jit(solution)/shard_map/sxA1/ppermute | solution.py:29
  462.8 28.7 %collective-permute-start.74 = (bf16[512,1024]{1,0:T(8,128)(2,1)S(1)}, bf16[512,1024]{1,0:T(8,128)(2,1)S(1)}, u32[]{:S(2)}, u32[]{:S(2)}) collective-permute-start(bf16[512,1024]{1,0:T(8,128)(2,1)S(1)} %share.33), channel_id=1, source_target_pairs={{0,16},{8,24},{16,0},{24,8},{1,17},{9,25},{17,1},{25,9},{2,18},{10... | collective-permute-start | bytes 3145736 | tf_op jit(solution)/shard_map/syA1/ppermute | solution.py:29
  534.5 27.0 %collective-permute-start.86 = (bf16[512,1024]{1,0:T(8,128)(2,1)S(1)}, bf16[512,1024]{1,0:T(8,128)(2,1)S(1)}, u32[]{:S(2)}, u32[]{:S(2)}) collective-permute-start(bf16[512,1024]{1,0:T(8,128)(2,1)S(1)} %share.38), channel_id=1, source_target_pairs={{0,8},{8,0},{16,24},{24,16},{1,9},{9,1},{17,25},{25,17},{2,10},{10... | collective-permute-start | bytes 3145736 | tf_op jit(solution)/shard_map/sxI0/ppermute | solution.py:29
  578.6 29.6 %collective-permute-start.90 = (bf16[1024,1024]{1,0:T(8,128)(2,1)S(1)}, bf16[1024,1024]{1,0:T(8,128)(2,1)}, u32[]{:S(2)}, u32[]{:S(2)}) collective-permute-start(bf16[1024,1024]{1,0:T(8,128)(2,1)S(1)} %by_rows.11.own_ref), channel_id=1, source_target_pairs={{0,1},{1,0},{2,3},{3,2},{4,5},{5,4},{6,7},{7,6},{8,9},{9,8},{10,11... | collective-permute-start | bytes 6291464 | tf_op jit(solution)/shard_map/qswap0/ppermute | solution.py:29
  583.0 25.1 %collective-permute-start.91 = (bf16[256,2048]{1,0:T(8,128)(2,1)}, bf16[256,2048]{1,0:T(8,128)(2,1)}, u32[]{:S(2)}, u32[]{:S(2)}) collective-permute-start(bf16[256,2048]{1,0:T(8,128)(2,1)} %share.40), channel_id=1, source_target_pairs={{0,8},{8,0},{16,24},{24,16},{1,9},{9,1},{17,25},{25,17},{2,10},{10... | collective-permute-start | bytes 3145736 | tf_op jit(solution)/shard_map/sxD0/ppermute | solution.py:29
  583.0 27.3 %collective-permute-start.92 = (bf16[256,2048]{1,0:T(8,128)(2,1)}, bf16[256,2048]{1,0:T(8,128)(2,1)}, u32[]{:S(2)}, u32[]{:S(2)}) collective-permute-start(bf16[256,2048]{1,0:T(8,128)(2,1)} %share.41), channel_id=1, source_target_pairs={{0,16},{8,24},{16,0},{24,8},{1,17},{9,25},{17,1},{25,9},{2,18},{10... | collective-permute-start | bytes 3145736 | tf_op jit(solution)/shard_map/syD0/ppermute | solution.py:29
  584.5 25.8 %collective-permute-start.93 = (bf16[512,256]{1,0:T(8,128)(2,1)S(1)}, bf16[512,256]{1,0:T(8,128)(2,1)S(1)}, u32[]{:S(2)}, u32[]{:S(2)}) collective-permute-start(bf16[512,256]{1,0:T(8,128)(2,1)S(1)} %slice_bitcast_fusion.4), channel_id=1, source_target_pairs={{0,2},{1,3},{2,4},{3,5},{4,6},{5,7},{6,0},{7,1},{8,10},{9,11},{10,... | collective-permute-start | bytes 786440 | tf_op jit(solution)/shard_map/q1I0/ppermute | solution.py:29
  630.3 32.9 %collective-permute-start.105 = (bf16[512,1024]{1,0:T(8,128)(2,1)}, bf16[512,1024]{1,0:T(8,128)(2,1)S(1)}, u32[]{:S(2)}, u32[]{:S(2)}) collective-permute-start(bf16[512,1024]{1,0:T(8,128)(2,1)} %share.45), channel_id=1, source_target_pairs={{0,16},{8,24},{16,0},{24,8},{1,17},{9,25},{17,1},{25,9},{2,18},{10... | collective-permute-start | bytes 3145736 | tf_op jit(solution)/shard_map/syA0/ppermute | solution.py:29
  (276 other events, 3461.5 us)

commit v4 on v3

--- a/solution.py
+++ b/solution.py
@@ -1407,7 +1407,7 @@
     )
 
 
-ORDER = (75, 76, 80, 71, 72, 85, 81, 83, 73, 53, 54, -77, 74, 60, 70, 56, -73, 61, 55, 0, -75, 1, 57, 58, 77, -62, 59, 78, -2, 2, -58, -79, 3, 79, -60, 37, 62, 63, 64, -4, 4, -65, 65, 68, -38, 12, 67, -5, 5, 69, -13, 13, -6, 20, 6, 7, 8, 66, -14, 14, -21, 21, -15, 28, 15, 16, -22, 17, -8, 22, -9, 10, -29, 9, -23, 82, 23, -83, 29, -17, 24, -18, 19, -30, 30, -10, 18, -11, 25, 11, 90, -31, 86, 31, -20, -87, 33, 45, -25, 32, 91, -46, -19, -26, 26, 27, 38, 92, -39, 93, -33, 39, -34, 35, -94, 34, 94, -40, 46, -27, 84, 40, -28, 41, 95, -47, -35, -36, 42, 47, 96, -85, -48, 97, 87, 88, 48, -42, -98, -89, 49, 44, -43, 50, 43, 89, 36, 98, -45, 99, -50, -44, 52, -51, 51, 100, 101, -102, 102, -53, 103, -52, 130, 131, 132, 115, 116, 117, 133, -133, 134, 135, 148, 149, -117, 119, -118, 121, 118, 120, -135, 137, -136, 139, 136, 138, 150, -122, -121, 153, 154, 155, 122, 151, 152, 104, -140, -139, -153, 105, 140, -156, -155, 141, 142, 157, -106, 159, 156, 158, -143, 143, 144, 123, 124, 170, 106, -145, 145, 146, 110, 108, 107, 168, -125, 111, 186, -147, -160, -159, 109, 187, -112, 188, 189, 190, 191, -110, 160, -189, 204, 161, 162, 171, -191, -192, 172, 173, -163, 192, 194, 163, 164, 193, -173, -165, -174, 195, 174, 176, 175, 177, 125, 126, 165, 205, 206, -127, -195, -196, 166, 196, 207, -167, 208, 197, 198, 209, -177, 210, -209, 211, 226, 167, -178, -199, 199, 200, 127, 128, 147, 178, 179, 224, -201, -211, -212, -129, 180, 213, 215, 212, -181, 214, 129, 201, 202, 181, 182, 227, 233, 231, 228, 229, 225, 169, 236, 237, 112, -203, 234, 203, -238, 250, 251, 238, -183, 230, -252, 252, -216, 183, -235, 184, -215, 216, -231, 232, 217, -185, 218, 185, 247, 248, -249, 249, -233, 113, 235, -219, 239, 219, -114, 220, -240, 114, 240, 241, -221, 221, -242, 222, 242, 243, -244, 244, 245, -223, 223, 253, 254, -246, 246, -255, 255)
+ORDER = (75, 76, 80, 71, 72, 85, 81, 83, 73, 53, 54, -77, 74, 60, 70, 56, -73, 61, 55, 0, -75, 1, 57, 58, 77, -62, 59, 78, -2, 2, -58, -79, 3, 79, -60, 37, 62, 63, 64, -4, 4, -65, 65, 68, -38, 12, 67, -5, 5, 69, -13, 13, -6, 20, 6, 7, 8, 66, -14, 14, -21, 21, -15, 28, 15, 16, -22, 17, -8, 22, -9, 10, -29, 9, -23, 82, 23, -83, 29, -17, 24, -18, 19, -30, 30, -10, 18, -11, 25, 11, 90, -31, 86, 31, -20, -87, 33, 45, -25, 32, 91, -46, -19, -26, 26, 27, 38, 92, -39, 93, -33, 39, -34, 35, -94, 34, 94, -40, 46, -27, 84, 40, -28, 41, 95, -47, -35, -36, 42, 47, 96, -85, -48, 97, 87, 88, 48, -42, -98, -89, 49, 44, -43, 50, 43, 89, 36, 98, -45, 99, -50, -44, 52, -51, 51, 100, 101, -102, 102, -53, 103, -52, 130, 131, 132, 115, 116, 117, 133, -133, 134, 135, 148, 149, -117, 119, -118, 121, 118, 120, -135, 137, -136, 139, 136, 138, 150, -122, -121, 153, 154, 155, 122, 151, 152, 104, -140, -139, -153, 105, 140, -156, -155, 141, 142, 157, -106, 159, 156, 158, -143, 143, 144, 123, 124, 170, 106, -145, 145, 146, 110, 108, 107, 168, -125, 111, 186, -147, -160, -159, 109, 187, -112, 188, 189, 190, 191, -110, 160, -189, 204, 161, 162, 171, -191, -192, 172, 173, -163, 192, 194, 163, 164, 193, -173, -165, -174, 195, 174, 176, 175, 177, 125, 126, 165, 205, 206, -127, -195, -196, 166, 196, 207, -167, 208, 197, 198, 209, -177, 210, -209, 211, 226, 167, -178, -199, 199, 200, 127, 128, 147, 178, 179, 224, -201, -211, -212, -129, 180, 213, 215, 212, -181, 214, 201, 202, 129, 181, 182, 227, 233, 231, 228, 229, 225, 169, 236, -203, 234, 237, 203, 250, 112, -238, 251, 238, -183, 230, -252, 252, -216, 183, -235, 184, -215, 216, -231, 232, 217, -185, 218, 185, 247, 248, -249, 249, -233, 113, 235, -219, 239, 219, -114, 220, -240, 114, 240, 241, -221, 221, -242, 222, 242, 243, -244, 244, 245, -223, 223, 253, 254, -246, 246, -255, 255)
 
 
 def solution(mesh):

time: 754 us -> 755 us (level)
    unnamed x420 -> x422, local copies, waits for them, and re-layouts: 65.2 us -> 65.8 us
  transfers between devices with their start and end apart: 119 -> 119, of which waited for: 42 -> 44; matrix products, arithmetic and copies ran while one was open for 12% -> 12% of each run, Pallas kernels for 34% -> 34%
where the time goes in v4:
time: 755 us; the launch traced here: 745 us
  Pallas kernels  277 us (37%)
  waiting for transfers between devices  188 us (25%)
  starting transfers between devices  127 us (17%)
  local copies, waits for them, and re-layouts  110 us (15%)
  other arithmetic  36.7 us (5%)
    pallas_call x52, Pallas kernels, in_vmem(): pl.pallas_call(kernel, out_shape=outs, in_specs=([smem_block] if scalars...  225 us
    ppermute x104, waiting for transfers between devices, permuted(): return lax.ppermute(block, axis, [(i, route(i)) for i in range(count)])  147 us
    ppermute x104, starting transfers between devices, permuted(): return lax.ppermute(block, axis, [(i, route(i)) for i in range(count)])  106 us
    unnamed x422, local copies, waits for them, and re-layouts  65.8 us
    ppermute x15, waiting for transfers between devices, route_blocks(): lax.ppermute(v, SEG, route)  41.3 us
    pallas_call x2, Pallas kernels, attend(): pl.pallas_call(functools.partial(forward_kernel, halo, memory is not None...  27 us
    pallas_call x2, Pallas kernels, attend_back(): pl.pallas_call(functools.partial(backward_kernel, halo, memory is not Non...  25.1 us
    ppermute x15, starting transfers between devices, route_blocks(): lax.ppermute(v, SEG, route)  21.2 us
  transfers between devices with their start and end apart: 119, of which 44 were waited for; matrix products, arithmetic and copies ran while one was open for 12% of the time, Pallas kernels for 34%

profile of v4, /device:TPU:1, one launch (start us, length us, event | category | flops | bytes accessed | tf_op | source)
XLA Modules:
  0.0 744.7 jit_solution(8078615782501997427)
XLA Ops:
  54.9 6.7 collective-permute-done.10
  61.7 6.4 slot_mask.4
  68.3 6.4 slot_mask.5
  75.9 6.4 slot_mask.6
  90.1 6.4 slot_mask.7
  97.4 7.0 collective-permute-done.16
  107.9 8.7 %collective-permute-done.20 = bf16[512,256]{1,0:T(8,128)(2,1)S(1)} collective-permute-done((bf16[512,256]{1,0:T(8,128)(2,1)S(1)}, bf16[512,256]{1,0:T(8,128)(2,1)S(1)}, u32[]{:S(2)}, u32[]{:S(2)}) %collective-permute-start.20) | collective-permute-done | bytes 262176 | tf_op jit(solution)/shard_map/z2D0/ppermute | solution.py:29
  137.9 9.4 %collective-permute-done.23 = bf16[784,256]{1,0:T(8,128)(2,1)S(1)} collective-permute-done((bf16[784,256]{1,0:T(8,128)(2,1)S(1)}, bf16[784,256]{1,0:T(8,128)(2,1)S(1)}, u32[]{:S(2)}, u32[]{:S(2)}) %collective-permute-start.23) | collective-permute-done | bytes 401440 | tf_op jit(solution)/shard_map/z2A1/ppermute | solution.py:29
  150.4 6.1 head.2
  174.5 10.5 %attend.2 = (bf16[1024,512]{1,0:T(8,128)(2,1)S(1)}, bf16[4,1024,768]{2,1,0:T(8,128)(2,1)S(1)}) custom-call(f32[4,1,1024]{2,1,0:T(1,128)S(1)} %get-tuple-element.1171.refs_0_, s32[1024,1]{1,0:T(8,128)S(1)} %copy-done.34, s32[1,1024]{1,0:T(1,128)S(1)} %constant_dynamic-slice_fusion.2.refs_2_, ...), custom_call_target="tpu_custom_call" | custom-call | flops 1610612736 | bytes 16777216 | tf_op jit(solution)/shard_map/att0/attend/pallas_call | solution.py:775
  196.6 19.0 %collective-permute-start.38 = (bf16[1024,1024]{1,0:T(8,128)(2,1)S(1)}, bf16[1024,1024]{1,0:T(8,128)(2,1)S(1)}, u32[]{:S(2)}, u32[]{:S(2)}) collective-permute-start(bf16[1024,1024]{1,0:T(8,128)(2,1)S(1)} %out.2.own_ref), channel_id=1, source_target_pairs={{0,1},{1,0},{2,3},{3,2},{4,5},{5,4},{6,7},{7,6},{8,9},{9,8},{10,11... | collective-permute-start | bytes 6291464 | tf_op jit(solution)/shard_map/oswap0/ppermute | solution.py:29
  228.2 10.2 %expand.2 = (bf16[1024,2048]{1,0:T(8,128)(2,1)S(1)}, bf16[1024,2048]{1,0:T(8,128)(2,1)S(1)}) custom-call(s32[1]{0:T(128)} %bitcast.at_ref, bf16[1024,1024]{1,0:T(8,128)(2,1)S(1)} %get-tuple-element.1709.rows_ref.refs_1_, bf16[512,1024]{1,0:T(8,128)(2,1)S(1)} %copy-done.42, bf16[512,1024]{1,0:T(8,128)(2,1)S(1)} %copy-done.61, ...), custom_call_target="tpu_custom_call" | custom-call | flops 12884901888 | tf_op jit(solution)/shard_map/ex0/expand/pallas_call | solution.py:417
  244.7 8.3 %down.2.refs_1_ = bf16[1024,1024]{1,0:T(8,128)(2,1)S(1)} custom-call(s32[1]{0:T(128)} %bitcast.at_ref, bf16[1024,2048]{1,0:T(8,128)(2,1)S(1)} %get-tuple-element.1759.rows_ref.refs_1_, bf16[256,2048]{1,0:T(8,128)(2,1)} %constant_dynamic-update-slice_fusion.18.refs_0_, bf16[256,2048]{1,0:T(8,128)(2,1)} %collective-permute-done.29.refs_1_, ...), custom_call_target="tpu_custom_call" | custom-call | flops 12884901888 | tf_op jit(solution)/shard_map/dp0/down/pallas_call | solution.py:417
  274.1 6.5 head.3
  291.0 16.5 %attend.3 = (bf16[1024,512]{1,0:T(8,128)(2,1)S(1)}, bf16[4,1024,768]{2,1,0:T(8,128)(2,1)S(1)}, bf16[4,1024,256]{2,1,0:T(8,128)(2,1)S(1)}, bf16[1024,512]{1,0:T(8,128)(2,1)S(1)}) custom-call(f32[4,1,1024]{2,1,0:T(1,128)S(1)} %get-tuple-element.1315.refs_0_, s32[1024,1]{1,0:T(8,128)S(1)} %copy-done.33, s32[1,1024]{1,0:T(1,128)S(1)} %constant_dynamic-slice_fusion.2.refs_2_, ...), custom_call_target="tpu_custom_call" | custom-call | flops 2147483648 | bytes 16777216 | tf_op jit(solution)/shard_map/att1/attend/pallas_call | solution.py:775
  324.8 10.8 %expand.3 = (bf16[1024,2048]{1,0:T(8,128)(2,1)S(1)}, bf16[1024,2048]{1,0:T(8,128)(2,1)S(1)}) custom-call(s32[1]{0:T(128)} %bitcast.at_ref, bf16[1024,1024]{1,0:T(8,128)(2,1)S(1)} %get-tuple-element.1513.rows_ref.refs_1_, bf16[512,1024]{1,0:T(8,128)(2,1)S(1)} %copy-done.45, bf16[512,1024]{1,0:T(8,128)(2,1)S(1)} %copy-done.67, ...), custom_call_target="tpu_custom_call" | custom-call | flops 12884901888 | tf_op jit(solution)/shard_map/ex1/expand/pallas_call | solution.py:417
  337.6 8.7 %by_rows.6.rows_ref.refs_0_ = bf16[1024,2048]{1,0:T(8,128)(2,1)S(1)} custom-call(s32[1]{0:T(128)} %bitcast.at_ref, bf16[1024,1024]{1,0:T(8,128)(2,1)S(1)} %bitcast.334, bf16[256,2048]{1,0:T(8,128)(2,1)} %constant_dynamic-update-slice_fusion.58.refs_0_, bf16[256,2048]{1,0:T(8,128)(2,1)} %collective-permute-done.54.refs_1_, ...), custom_call_target="tpu_custom_call" | custom-call | flops 12884901888 | tf_op jit(solution)/shard_map/pg1/by_rows/pallas_call | solution.py:417
  346.3 6.3 by_rows.7.own_ref
  392.8 14.3 %attend_back.2 = (bf16[1024,1536]{1,0:T(8,128)(2,1)S(1)}, f32[4,1,1024]{2,1,0:T(1,128)S(1)}, f32[4,1,128]{2,1,0:T(1,128)S(1)}) custom-call(bf16[1024,1536]{1,0:T(8,128)(2,1)S(1)} %copy-done.3, bf16[1024,1536]{1,0:T(8,128)(2,1)S(1)} %copy-done.3, bf16[1024,1536]{1,0:T(8,128)(2,1)S(1)} %copy-done.3, bf16[1024,512]{1,0:T(8,128)(2,1)S(1)} %attended_back.2.refs_3_, ...), custom_call_target="tpu_custom_call" | custom-call | flops 3758096384 | bytes 20971520 | tf_op jit(solution)/shard_map/ab1/attend_back/pallas_call | solution.py:831
  423.3 8.6 %down.3 = bf16[1024,1024]{1,0:T(8,128)(2,1)S(1)} custom-call(s32[1]{0:T(128)} %bitcast.at_ref, bf16[1024,2048]{1,0:T(8,128)(2,1)S(1)} %copy-done.131, bf16[256,2048]{1,0:T(8,128)(2,1)} %constant_dynamic-update-slice_fusion.58.refs_0_, bf16[256,2048]{1,0:T(8,128)(2,1)} %collective-permute-done.54.refs_1_, bf16[256,2048]{1,0:T(8,128)(2,1)} %collective-permute-done.52.refs_2_, ...), custom_call_target="tpu_custom_call" | custom-call | flops 12884901888 | tf_op jit(solution)/shard_map/dp1/down/pallas_call | solution.py:417
  463.1 6.2 collective-permute-done.72
  475.0 8.6 %by_rows.9.rows_ref.refs_0_ = bf16[1024,2048]{1,0:T(8,128)(2,1)S(1)} custom-call(s32[1]{0:T(128)} %bitcast.at_ref, bf16[1024,1024]{1,0:T(8,128)(2,1)S(1)} %get-tuple-element.1758.rows_ref.refs_0_, bf16[256,2048]{1,0:T(8,128)(2,1)} %constant_dynamic-update-slice_fusion.18.refs_0_, bf16[256,2048]{1,0:T(8,128)(2,1)} %collective-permute-done.29.refs_1_, ...), custom_call_target="tpu_custom_call" | custom-call | flops 12884901888 | tf_op jit(solution)/shard_map/pg0/by_rows/pallas_call | solution.py:417
  485.2 6.5 collective-permute-done.75
  491.7 6.2 by_rows.10.own_ref
  550.7 10.8 %attend_back.3 = (bf16[1024,1536]{1,0:T(8,128)(2,1)S(1)}, f32[4,1,1024]{2,1,0:T(1,128)S(1)}) custom-call(bf16[1024,1536]{1,0:T(8,128)(2,1)S(1)} %get-tuple-element.1692.refs_3_.refs_4_.refs_5_.refs_0_.refs_1_.refs_2_, bf16[1024,1536]{1,0:T(8,128)(2,1)S(1)} %get-tuple-element.1692.refs_3_.refs_4_.refs_5_.refs_0_.refs_1_.refs_2_, ...), custom_call_target="tpu_custom_call" | custom-call | flops 3221225472 | bytes 20971520 | tf_op jit(solution)/shard_map/ab0/attend_back/pallas_call | solution.py:831
  561.5 6.9 collective-permute-done.88.refs_3_
  593.7 14.5 %collective-permute-done.93.refs_2_ = bf16[256,2048]{1,0:T(8,128)(2,1)} collective-permute-done((bf16[256,2048]{1,0:T(8,128)(2,1)}, bf16[256,2048]{1,0:T(8,128)(2,1)}, u32[]{:S(2)}, u32[]{:S(2)}) %collective-permute-start.93) | collective-permute-done | bytes 1048608 | tf_op jit(solution)/shard_map/sxD0/ppermute | solution.py:29
  618.0 7.8 %join_back.7 = (f32[1024,1024]{1,0:T(8,128)}, bf16[1024,1024]{1,0:T(8,128)(2,1)S(1)}, f32[1,1024]{1,0:T(1,128)S(1)}, f32[1,1024]{1,0:T(1,128)S(1)}) custom-call(f32[1024,1024]{1,0:T(8,128)S(1)} %copy-done.19, bf16[1024,1024]{1,0:T(8,128)(2,1)S(1)} %by_rows.11.own_ref, bf16[1024,1024]{1,0:T(8,128)(2,1)} %collective-permute-done.92.got_ref, ...), custom_call_target="tpu_custom_call" | custom-call | flops 62914560 | tf_op jit(solution)/shard_map/jk0/join_back/pallas_call | solution.py:417
  652.9 6.4 collective-permute-start.101
  688.1 16.8 %collective-permute-done.107 = bf16[128,1024]{1,0:T(8,128)(2,1)S(1)} collective-permute-done((bf16[128,1024]{1,0:T(8,128)(2,1)}, bf16[128,1024]{1,0:T(8,128)(2,1)S(1)}, u32[]{:S(2)}, u32[]{:S(2)}) %collective-permute-start.107) | collective-permute-done | bytes 262176 | tf_op jit(solution)/shard_map/i2/ppermute | solution.py:952
  707.3 6.9 collective-permute-done.110
  717.0 8.0 %collective-permute-done.113 = bf16[512,256]{1,0:T(8,128)(2,1)S(1)} collective-permute-done((bf16[512,256]{1,0:T(8,128)(2,1)S(1)}, bf16[512,256]{1,0:T(8,128)(2,1)S(1)}, u32[]{:S(2)}, u32[]{:S(2)}) %collective-permute-start.113) | collective-permute-done | bytes 262176 | tf_op jit(solution)/shard_map/q2A0/ppermute | solution.py:29
  (894 shorter events, 451.2 us)
Async XLA Ops:
  87.6 29.3 %collective-permute-start.19 = (bf16[528,1024]{1,0:T(8,128)(2,1)S(1)}, bf16[528,1024]{1,0:T(8,128)(2,1)S(1)}, u32[]{:S(2)}, u32[]{:S(2)}) collective-permute-start(bf16[528,1024]{1,0:T(8,128)(2,1)S(1)} %pad_maximum_fusion.3.own_ref.refs_3_.refs_0_), channel_id=1, source_target_pairs={{0,8},{8,0},{16,24},{24,16},{1,9},{9,1},{17,25},{25,17},{2,10},{10... | collective-permute-start | bytes 3244040 | tf_op jit(solution)/shard_map/pxA0/ppermute | solution.py:29
  88.9 28.0 %collective-permute-start.18 = (bf16[528,1024]{1,0:T(8,128)(2,1)S(1)}, bf16[528,1024]{1,0:T(8,128)(2,1)S(1)}, u32[]{:S(2)}, u32[]{:S(2)}) collective-permute-start(bf16[528,1024]{1,0:T(8,128)(2,1)S(1)} %pad_maximum_fusion.3.own_ref.refs_3_.refs_0_), channel_id=1, source_target_pairs={{0,16},{8,24},{16,0},{24,8},{1,17},{9,25},{17,1},{25,9},{2,18},{10... | collective-permute-start | bytes 3244040 | tf_op jit(solution)/shard_map/pyA0/ppermute | solution.py:29
  107.6 27.7 %collective-permute-start.25 = (bf16[512,1024]{1,0:T(8,128)(2,1)S(1)}, bf16[512,1024]{1,0:T(8,128)(2,1)S(1)}, u32[]{:S(2)}, u32[]{:S(2)}) collective-permute-start(bf16[512,1024]{1,0:T(8,128)(2,1)S(1)} %pad_maximum_fusion.6.refs_0_), channel_id=1, source_target_pairs={{0,8},{8,0},{16,24},{24,16},{1,9},{9,1},{17,25},{25,17},{2,10},{10... | collective-permute-start | bytes 3145736 | tf_op jit(solution)/shard_map/pxI0/ppermute | solution.py:29
  121.0 26.2 %collective-permute-start.27 = (bf16[256,1024]{1,0:T(8,128)(2,1)S(1)}, bf16[256,1024]{1,0:T(8,128)(2,1)S(1)}, u32[]{:S(2)}, u32[]{:S(2)}) collective-permute-start(bf16[256,1024]{1,0:T(8,128)(2,1)S(1)} %slice.558), channel_id=1, source_target_pairs={{0,8},{8,0},{16,24},{24,16},{1,9},{9,1},{17,25},{25,17},{2,10},{10... | collective-permute-start | bytes 1572872 | tf_op jit(solution)/shard_map/fxA0/ppermute | solution.py:29
  121.4 25.9 %collective-permute-start.28 = (bf16[272,1024]{1,0:T(8,128)(2,1)S(1)}, bf16[272,1024]{1,0:T(8,128)(2,1)S(1)}, u32[]{:S(2)}, u32[]{:S(2)}) collective-permute-start(bf16[272,1024]{1,0:T(8,128)(2,1)S(1)} %slice.559), channel_id=1, source_target_pairs={{0,16},{8,24},{16,0},{24,8},{1,17},{9,25},{17,1},{25,9},{2,18},{10... | collective-permute-start | bytes 1671176 | tf_op jit(solution)/shard_map/fyA0/ppermute | solution.py:29
  136.1 33.6 %collective-permute-start.31 = (bf16[256,1024]{1,0:T(8,128)(2,1)S(1)}, bf16[256,1024]{1,0:T(8,128)(2,1)S(1)}, u32[]{:S(2)}, u32[]{:S(2)}) collective-permute-start(bf16[256,1024]{1,0:T(8,128)(2,1)S(1)} %slice.566), channel_id=1, source_target_pairs={{0,16},{8,24},{16,0},{24,8},{1,17},{9,25},{17,1},{25,9},{2,18},{10... | collective-permute-start | bytes 1572872 | tf_op jit(solution)/shard_map/fyI0/ppermute | solution.py:29
  137.6 33.6 %collective-permute-start.29 = (bf16[256,2048]{1,0:T(8,128)(2,1)}, bf16[256,2048]{1,0:T(8,128)(2,1)}, u32[]{:S(2)}, u32[]{:S(2)}) collective-permute-start(bf16[256,2048]{1,0:T(8,128)(2,1)} %constant_dynamic-update-slice_fusion.18.refs_0_), channel_id=1, source_target_pairs={{0,8},{8,0},{16,24},{24,16},{1,9},{9,1},{17,25},{25,17},{2,10},{10... | collective-permute-start | bytes 3145736 | tf_op jit(solution)/shard_map/pxD0/ppermute | solution.py:29
  148.5 39.2 %collective-permute-start.34 = (bf16[256,1024]{1,0:T(8,128)(2,1)}, bf16[256,1024]{1,0:T(8,128)(2,1)}, u32[]{:S(2)}, u32[]{:S(2)}) collective-permute-start(bf16[256,1024]{1,0:T(8,128)(2,1)} %slice.599), channel_id=1, source_target_pairs={{0,8},{8,0},{16,24},{24,16},{1,9},{9,1},{17,25},{25,17},{2,10},{10... | collective-permute-start | bytes 1572872 | tf_op jit(solution)/shard_map/fxI0/ppermute | solution.py:29
  148.7 39.0 %collective-permute-start.33 = (bf16[256,2048]{1,0:T(8,128)(2,1)}, bf16[256,2048]{1,0:T(8,128)(2,1)}, u32[]{:S(2)}, u32[]{:S(2)}) collective-permute-start(bf16[256,2048]{1,0:T(8,128)(2,1)} %constant_dynamic-update-slice_fusion.18.refs_0_), channel_id=1, source_target_pairs={{0,16},{8,24},{16,0},{24,8},{1,17},{9,25},{17,1},{25,9},{2,18},{10... | collective-permute-start | bytes 3145736 | tf_op jit(solution)/shard_map/pyD0/ppermute | solution.py:29
  172.2 43.4 %collective-permute-start.37 = (bf16[528,1024]{1,0:T(8,128)(2,1)}, bf16[528,1024]{1,0:T(8,128)(2,1)S(1)}, u32[]{:S(2)}, u32[]{:S(2)}) collective-permute-start(bf16[528,1024]{1,0:T(8,128)(2,1)} %pad_maximum_fusion.4.own_ref.refs_5_.refs_0_), channel_id=1, source_target_pairs={{0,16},{8,24},{16,0},{24,8},{1,17},{9,25},{17,1},{25,9},{2,18},{10... | collective-permute-start | bytes 3244040 | tf_op jit(solution)/shard_map/pyA1/ppermute | solution.py:29
  172.3 43.4 %collective-permute-start.32 = (bf16[528,1024]{1,0:T(8,128)(2,1)}, bf16[528,1024]{1,0:T(8,128)(2,1)S(1)}, u32[]{:S(2)}, u32[]{:S(2)}) collective-permute-start(bf16[528,1024]{1,0:T(8,128)(2,1)} %pad_maximum_fusion.4.own_ref.refs_5_.refs_0_), channel_id=1, source_target_pairs={{0,8},{8,0},{16,24},{24,16},{1,9},{9,1},{17,25},{25,17},{2,10},{10... | collective-permute-start | bytes 3244040 | tf_op jit(solution)/shard_map/pxA1/ppermute | solution.py:29
  190.4 34.0 %collective-permute-start.43 = (bf16[128,2048]{1,0:T(8,128)(2,1)S(1)}, bf16[128,2048]{1,0:T(8,128)(2,1)S(1)}, u32[]{:S(2)}, u32[]{:S(2)}) collective-permute-start(bf16[128,2048]{1,0:T(8,128)(2,1)S(1)} %slice.604), channel_id=1, source_target_pairs={{0,8},{8,0},{16,24},{24,16},{1,9},{9,1},{17,25},{25,17},{2,10},{10... | collective-permute-start | bytes 1572872 | tf_op jit(solution)/shard_map/fxD0/ppermute | solution.py:29
  190.7 34.0 %collective-permute-start.42 = (bf16[128,2048]{1,0:T(8,128)(2,1)S(1)}, bf16[128,2048]{1,0:T(8,128)(2,1)S(1)}, u32[]{:S(2)}, u32[]{:S(2)}) collective-permute-start(bf16[128,2048]{1,0:T(8,128)(2,1)S(1)} %slice.603), channel_id=1, source_target_pairs={{0,16},{8,24},{16,0},{24,8},{1,17},{9,25},{17,1},{25,9},{2,18},{10... | collective-permute-start | bytes 1572872 | tf_op jit(solution)/shard_map/fyD0/ppermute | solution.py:29
  215.8 26.0 %collective-permute-start.44 = (bf16[272,1024]{1,0:T(8,128)(2,1)S(1)}, bf16[272,1024]{1,0:T(8,128)(2,1)S(1)}, u32[]{:S(2)}, u32[]{:S(2)}) collective-permute-start(bf16[272,1024]{1,0:T(8,128)(2,1)S(1)} %slice.605), channel_id=1, source_target_pairs={{0,16},{8,24},{16,0},{24,8},{1,17},{9,25},{17,1},{25,9},{2,18},{10... | collective-permute-start | bytes 1671176 | tf_op jit(solution)/shard_map/fyA1/ppermute | solution.py:29
  225.6 27.3 %collective-permute-start.45 = (bf16[128,1024]{1,0:T(8,128)(2,1)S(1)}, bf16[128,1024]{1,0:T(8,128)(2,1)S(1)}, u32[]{:S(2)}, u32[]{:S(2)}) collective-permute-start(bf16[128,1024]{1,0:T(8,128)(2,1)S(1)} %copy-done.171), channel_id=1, source_target_pairs={{0,4},{1,5},{2,6},{3,7},{4,0},{5,1},{6,2},{7,3},{8,12},{9,13},{10,... | collective-permute-start | bytes 786440 | tf_op jit(solution)/shard_map/c2/ppermute | solution.py:952
  227.7 35.0 %collective-permute-start.49 = (bf16[512,1024]{1,0:T(8,128)(2,1)S(1)}, bf16[512,1024]{1,0:T(8,128)(2,1)S(1)}, u32[]{:S(2)}, u32[]{:S(2)}) collective-permute-start(bf16[512,1024]{1,0:T(8,128)(2,1)S(1)} %pad_maximum_fusion.7.refs_0_), channel_id=1, source_target_pairs={{0,8},{8,0},{16,24},{24,16},{1,9},{9,1},{17,25},{25,17},{2,10},{10... | collective-permute-start | bytes 3145736 | tf_op jit(solution)/shard_map/pxI1/ppermute | solution.py:29
  269.0 38.5 %collective-permute-start.53 = (bf16[256,1024]{1,0:T(8,128)(2,1)}, bf16[256,1024]{1,0:T(8,128)(2,1)}, u32[]{:S(2)}, u32[]{:S(2)}) collective-permute-start(bf16[256,1024]{1,0:T(8,128)(2,1)} %slice.621), channel_id=1, source_target_pairs={{0,8},{8,0},{16,24},{24,16},{1,9},{9,1},{17,25},{25,17},{2,10},{10... | collective-permute-start | bytes 1572872 | tf_op jit(solution)/shard_map/fxI1/ppermute | solution.py:29
  272.5 35.0 %collective-permute-start.54 = (bf16[256,2048]{1,0:T(8,128)(2,1)}, bf16[256,2048]{1,0:T(8,128)(2,1)}, u32[]{:S(2)}, u32[]{:S(2)}) collective-permute-start(bf16[256,2048]{1,0:T(8,128)(2,1)} %constant_dynamic-update-slice_fusion.58.refs_0_), channel_id=1, source_target_pairs={{0,8},{8,0},{16,24},{24,16},{1,9},{9,1},{17,25},{25,17},{2,10},{10... | collective-permute-start | bytes 3145736 | tf_op jit(solution)/shard_map/pxD1/ppermute | solution.py:29
  273.8 33.8 %collective-permute-start.52 = (bf16[256,2048]{1,0:T(8,128)(2,1)}, bf16[256,2048]{1,0:T(8,128)(2,1)}, u32[]{:S(2)}, u32[]{:S(2)}) collective-permute-start(bf16[256,2048]{1,0:T(8,128)(2,1)} %constant_dynamic-update-slice_fusion.58.refs_0_), channel_id=1, source_target_pairs={{0,16},{8,24},{16,0},{24,8},{1,17},{9,25},{17,1},{25,9},{2,18},{10... | collective-permute-start | bytes 3145736 | tf_op jit(solution)/shard_map/pyD1/ppermute | solution.py:29
  310.3 27.3 %collective-permute-start.57 = (bf16[128,2048]{1,0:T(8,128)(2,1)S(1)}, bf16[128,2048]{1,0:T(8,128)(2,1)S(1)}, u32[]{:S(2)}, u32[]{:S(2)}) collective-permute-start(bf16[128,2048]{1,0:T(8,128)(2,1)S(1)} %slice.625), channel_id=1, source_target_pairs={{0,8},{8,0},{16,24},{24,16},{1,9},{9,1},{17,25},{25,17},{2,10},{10... | collective-permute-start | bytes 1572872 | tf_op jit(solution)/shard_map/fxD1/ppermute | solution.py:29
  384.5 24.7 %collective-permute-start.63 = (bf16[256,2048]{1,0:T(8,128)(2,1)}, bf16[256,2048]{1,0:T(8,128)(2,1)S(1)}, u32[]{:S(2)}, u32[]{:S(2)}) collective-permute-start(bf16[256,2048]{1,0:T(8,128)(2,1)} %share.27), channel_id=1, source_target_pairs={{0,8},{8,0},{16,24},{24,16},{1,9},{9,1},{17,25},{25,17},{2,10},{10... | collective-permute-start | bytes 3145736 | tf_op jit(solution)/shard_map/sxD1/ppermute | solution.py:29
  407.1 28.3 %collective-permute-start.66 = (bf16[512,1024]{1,0:T(8,128)(2,1)}, bf16[512,1024]{1,0:T(8,128)(2,1)S(1)}, u32[]{:S(2)}, u32[]{:S(2)}) collective-permute-start(bf16[512,1024]{1,0:T(8,128)(2,1)} %share.29), channel_id=1, source_target_pairs={{0,8},{8,0},{16,24},{24,16},{1,9},{9,1},{17,25},{25,17},{2,10},{10... | collective-permute-start | bytes 3145736 | tf_op jit(solution)/shard_map/sxI1/ppermute | solution.py:29
  407.8 27.6 %collective-permute-start.67 = (bf16[512,1024]{1,0:T(8,128)(2,1)}, bf16[512,1024]{1,0:T(8,128)(2,1)S(1)}, u32[]{:S(2)}, u32[]{:S(2)}) collective-permute-start(bf16[512,1024]{1,0:T(8,128)(2,1)} %share.28), channel_id=1, source_target_pairs={{0,16},{8,24},{16,0},{24,8},{1,17},{9,25},{17,1},{25,9},{2,18},{10... | collective-permute-start | bytes 3145736 | tf_op jit(solution)/shard_map/syI1/ppermute | solution.py:29
  461.9 29.7 %collective-permute-start.73 = (bf16[512,1024]{1,0:T(8,128)(2,1)S(1)}, bf16[512,1024]{1,0:T(8,128)(2,1)S(1)}, u32[]{:S(2)}, u32[]{:S(2)}) collective-permute-start(bf16[512,1024]{1,0:T(8,128)(2,1)S(1)} %share.34), channel_id=1, source_target_pairs={{0,8},{8,0},{16,24},{24,16},{1,9},{9,1},{17,25},{25,17},{2,10},{10... | collective-permute-start | bytes 3145736 | tf_op jit(solution)/shard_map/sxA1/ppermute | solution.py:29
  462.9 28.7 %collective-permute-start.74 = (bf16[512,1024]{1,0:T(8,128)(2,1)S(1)}, bf16[512,1024]{1,0:T(8,128)(2,1)S(1)}, u32[]{:S(2)}, u32[]{:S(2)}) collective-permute-start(bf16[512,1024]{1,0:T(8,128)(2,1)S(1)} %share.33), channel_id=1, source_target_pairs={{0,16},{8,24},{16,0},{24,8},{1,17},{9,25},{17,1},{25,9},{2,18},{10... | collective-permute-start | bytes 3145736 | tf_op jit(solution)/shard_map/syA1/ppermute | solution.py:29
  534.5 27.0 %collective-permute-start.83 = (bf16[512,1024]{1,0:T(8,128)(2,1)S(1)}, bf16[512,1024]{1,0:T(8,128)(2,1)S(1)}, u32[]{:S(2)}, u32[]{:S(2)}) collective-permute-start(bf16[512,1024]{1,0:T(8,128)(2,1)S(1)} %share.38), channel_id=1, source_target_pairs={{0,8},{8,0},{16,24},{24,16},{1,9},{9,1},{17,25},{25,17},{2,10},{10... | collective-permute-start | bytes 3145736 | tf_op jit(solution)/shard_map/sxI0/ppermute | solution.py:29
  578.8 29.6 %collective-permute-start.92 = (bf16[1024,1024]{1,0:T(8,128)(2,1)S(1)}, bf16[1024,1024]{1,0:T(8,128)(2,1)}, u32[]{:S(2)}, u32[]{:S(2)}) collective-permute-start(bf16[1024,1024]{1,0:T(8,128)(2,1)S(1)} %by_rows.11.own_ref), channel_id=1, source_target_pairs={{0,1},{1,0},{2,3},{3,2},{4,5},{5,4},{6,7},{7,6},{8,9},{9,8},{10,11... | collective-permute-start | bytes 6291464 | tf_op jit(solution)/shard_map/qswap0/ppermute | solution.py:29
  583.1 25.1 %collective-permute-start.93 = (bf16[256,2048]{1,0:T(8,128)(2,1)}, bf16[256,2048]{1,0:T(8,128)(2,1)}, u32[]{:S(2)}, u32[]{:S(2)}) collective-permute-start(bf16[256,2048]{1,0:T(8,128)(2,1)} %share.40), channel_id=1, source_target_pairs={{0,8},{8,0},{16,24},{24,16},{1,9},{9,1},{17,25},{25,17},{2,10},{10... | collective-permute-start | bytes 3145736 | tf_op jit(solution)/shard_map/sxD0/ppermute | solution.py:29
  583.1 27.3 %collective-permute-start.91 = (bf16[256,2048]{1,0:T(8,128)(2,1)}, bf16[256,2048]{1,0:T(8,128)(2,1)}, u32[]{:S(2)}, u32[]{:S(2)}) collective-permute-start(bf16[256,2048]{1,0:T(8,128)(2,1)} %share.41), channel_id=1, source_target_pairs={{0,16},{8,24},{16,0},{24,8},{1,17},{9,25},{17,1},{25,9},{2,18},{10... | collective-permute-start | bytes 3145736 | tf_op jit(solution)/shard_map/syD0/ppermute | solution.py:29
  584.6 25.8 %collective-permute-start.90 = (bf16[512,256]{1,0:T(8,128)(2,1)S(1)}, bf16[512,256]{1,0:T(8,128)(2,1)S(1)}, u32[]{:S(2)}, u32[]{:S(2)}) collective-permute-start(bf16[512,256]{1,0:T(8,128)(2,1)S(1)} %slice_bitcast_fusion.4), channel_id=1, source_target_pairs={{0,2},{1,3},{2,4},{3,5},{4,6},{5,7},{6,0},{7,1},{8,10},{9,11},{10,... | collective-permute-start | bytes 786440 | tf_op jit(solution)/shard_map/q1I0/ppermute | solution.py:29
  630.5 37.1 %collective-permute-start.105 = (bf16[512,1024]{1,0:T(8,128)(2,1)}, bf16[512,1024]{1,0:T(8,128)(2,1)S(1)}, u32[]{:S(2)}, u32[]{:S(2)}) collective-permute-start(bf16[512,1024]{1,0:T(8,128)(2,1)} %share.45), channel_id=1, source_target_pairs={{0,16},{8,24},{16,0},{24,8},{1,17},{9,25},{17,1},{25,9},{2,18},{10... | collective-permute-start | bytes 3145736 | tf_op jit(solution)/shard_map/syA0/ppermute | solution.py:29
  645.7 26.8 %collective-permute-start.103 = (bf16[512,1024]{1,0:T(8,128)(2,1)}, bf16[512,1024]{1,0:T(8,128)(2,1)}, u32[]{:S(2)}, u32[]{:S(2)}) collective-permute-start(bf16[512,1024]{1,0:T(8,128)(2,1)} %share.46), channel_id=1, source_target_pairs={{0,8},{8,0},{16,24},{24,16},{1,9},{9,1},{17,25},{25,17},{2,10},{10... | collective-permute-start | bytes 3145736 | tf_op jit(solution)/shard_map/sxA0/ppermute | solution.py:29
  (277 other events, 3472.6 us)
